TPU v7x, 32 devices: a whole 2x2x4 slice. The times are simulated.
32 devices in a mesh: region: 2 (over x), dom: 16 (over z, y, core).
Axes of the slice: x: 2, y: 2, z: 4, core: 2. Of those that a mesh axis runs over, the one named last changes fastest.
Arguments:
- descriptors: bfloat16 [49152, 768], P(('region', 'dom')), parts along dimension 0, may hold values from -8 to 8
- queries: bfloat16 [256, 768], P('region'), parts along dimension 0, may hold values from -0.21875 to 0.21875
- affinity: bfloat16 [384, 4, 128, 128], P(('region', 'dom')), parts along dimension 0, may hold values from 0 to 1, as said below
- tile_col: int32 [384, 4], P(('region', 'dom')), parts along dimension 0, may hold values from 0 to 191, as said below
Outputs:
- ranking: float32 [49152, 128], P(('region', 'dom')), parts along dimension 0
There are 2 independent parts, one for each index of `region`. A program takes and returns all parts, laid end to end along the dimension named above; each array names one. Nothing has to cross between parts.
Inputs may be any that keep to these rules, and one draw needn't show every extreme that they name: `tile_col`: tile slot 0 of row block g names g, slot 1 names g - 1 and slot 2 names g + 1 around the cycle of 192 blocks. Every named block lies within 6 blocks of the named device's own blocks around the cycle, and of the 6 blocks of each neighbour nearest to a device, the device's tiles name exactly 3. `affinity`: the matrix S with these tiles is symmetric with nonnegative entries: D^-1/2 W D^-1/2 for a symmetric W positive on its tiles, D the row sums of W.
All inputs are finite; a program needn't handle non-finite values.
Results may differ from a plain program's by a relative error of at most 0.0029.
Values may be sent and summed in bfloat16 or wider, within the bound.
No kernel may reach another device: no remote copies, remote signals or barrier semaphores. Data moves between devices by JAX's collectives and lax.ppermute only.
A program may use at most 64 MiB of HBM per device.

v0:
```python
import jax
import jax.numpy as jnp
from jax import lax
from jax.sharding import PartitionSpec as P

HALO_W = 6
ITERATIONS = 5


def padded(block, sides, width):
    for axis, dim in sides:
        count = lax.axis_size(axis)
        forward = [(i, i + 1) for i in range(count - 1)]
        forward.append((count - 1, 0))
        backward = [(target, source) for source, target in forward]
        low = lax.ppermute(
            lax.slice_in_dim(block, block.shape[dim] - width, None, axis=dim), axis, forward
        )
        high = lax.ppermute(lax.slice_in_dim(block, 0, width, axis=dim), axis, backward)
        block = jnp.concatenate([low, block, high], axis=dim)
    return block


def shards(descriptors, queries, affinity, tile_col):
    block_count = affinity.shape[0]
    tile_rows = affinity.shape[2]
    query_count = queries.shape[0]
    block_total = block_count * lax.axis_size("dom")
    first_block = lax.axis_index("dom") * block_count
    relative = (tile_col - first_block) % block_total
    position = jnp.where(
        relative >= block_total - HALO_W, relative - (block_total - HALO_W), HALO_W + relative
    )
    far_position = position[:, 3]
    scores = lax.dot_general(
        descriptors, queries, (((1,), (1,)), ((), ())), preferred_element_type=jnp.float32
    )
    targets = jnp.maximum(scores, 0.0) ** 3
    ranking = jnp.zeros_like(targets)
    residual = targets
    direction = targets
    norm_now = lax.psum(jnp.sum(residual * residual, axis=0), "dom")
    for step_index in range(ITERATIONS):
        operate_rounded = direction.astype(jnp.bfloat16).reshape(
            block_count, tile_rows, query_count
        )
        extended = padded(operate_rounded, (("dom", 0),), HALO_W)
        below = extended[HALO_W - 1 : HALO_W - 1 + block_count]
        above = extended[HALO_W + 1 : HALO_W + 1 + block_count]
        distant = jnp.take(extended, far_position, axis=0)
        spread = jnp.einsum(
            "bij,bjq->biq", affinity[:, 0], operate_rounded, preferred_element_type=jnp.float32
        )
        spread = spread + jnp.einsum(
            "bij,bjq->biq", affinity[:, 1], below, preferred_element_type=jnp.float32
        )
        spread = spread + jnp.einsum(
            "bij,bjq->biq", affinity[:, 2], above, preferred_element_type=jnp.float32
        )
        spread = spread + jnp.einsum(
            "bij,bjq->biq", affinity[:, 3], distant, preferred_element_type=jnp.float32
        )
        applied = direction - 0.99 * spread.reshape(block_count * tile_rows, query_count)
        curve_sum, mixed_term, image_norm = lax.psum(
            (
                jnp.sum(direction * applied, axis=0),
                jnp.sum(residual * applied, axis=0),
                jnp.sum(applied * applied, axis=0),
            ),
            "dom",
        )
        step_size = norm_now / curve_sum
        ranking = ranking + step_size * direction
        if step_index + 1 < ITERATIONS:
            residual = residual - step_size * applied
            norm_next = norm_now - 2.0 * step_size * mixed_term + step_size * step_size * image_norm
            direction = residual + norm_next / norm_now * direction
            norm_now = norm_next
    return ranking


def solution(mesh):
    return jax.shard_map(
        shards,
        mesh=mesh,
        in_specs=(
            P(("region", "dom"), None),
            P("region", None),
            P(("region", "dom"), None, None, None),
            P(("region", "dom"), None),
        ),
        out_specs=P(("region", "dom"), None),
        check_vma=False,
    )
```

profile of v0, /device:TPU:0, one launch (start us, length us, event | category | flops | bytes accessed | tf_op | source)
XLA Modules:
  0.0 260.3 jit_solution(6780519526210502453)
XLA Ops:
  4.1 5.5 %collective-permute-start.1 = (bf16[6,128,128]{2,1,0:T(8,128)(2,1)}, bf16[6,128,128]{2,1,0:T(8,128)(2,1)}, u32[]{:S(2)}, u32[]{:S(2)}) collective-permute-start(bf16[6,128,128]{2,1,0:T(8,128)(2,1)} %bitcast.4), channel_id=1, source_target_pairs={{1,0},{2,1},{3,2},{4,3},{5,4},{6,5},{7,6},{8,7},{9,8},{10,9},{11,1... | collective-permute-start | bytes 589832 | tf_op jit(solution)/shard_map/ppermute | solution.py:19
  9.7 2.2 fusion.41
  13.1 4.6 %collective-permute-done = bf16[6,128,128]{2,1,0:T(8,128)(2,1)} collective-permute-done((bf16[6,128,128]{2,1,0:T(8,128)(2,1)}, bf16[6,128,128]{2,1,0:T(8,128)(2,1)}, u32[]{:S(2)}, u32[]{:S(2)}) %collective-permute-start) | collective-permute-done | bytes 196640 | tf_op jit(solution)/shard_map/ppermute | solution.py:16
  19.7 2.5 gather_fusion
  27.4 29.5 %all-reduce.3 = (f32[128]{0:T(128)S(1)}, f32[128]{0:T(128)S(1)}, f32[128]{0:T(128)S(1)}) all-reduce(f32[128]{0:T(128)S(1)} %get-tuple-element.16, f32[128]{0:T(128)S(1)} %get-tuple-element.17, f32[128]{0:T(128)S(1)} %get-tuple-element.15), channel_id=1, replica_groups=mesh['region'=2,'dom'=16] {'dom'}, use_global_device_ids=true, to_apply=%region_5.7 | all-reduce | flops 384 | bytes 3072 | tf_op jit(solution)/shard_map/psum | solution.py:64
  59.3 2.2 fusion.43
  62.0 4.7 %collective-permute-done.2 = bf16[6,128,128]{2,1,0:T(8,128)(2,1)S(1)} collective-permute-done((bf16[6,128,128]{2,1,0:T(8,128)(2,1)S(1)}, bf16[6,128,128]{2,1,0:T(8,128)(2,1)S(1)}, u32[]{:S(2)}, u32[]{:S(2)}) %collective-permute-start.2) | collective-permute-done | bytes 196640 | tf_op jit(solution)/shard_map/ppermute | solution.py:16
  68.3 2.5 gather_fusion.1
  75.9 30.1 %all-reduce.2 = (f32[128]{0:T(128)S(1)}, f32[128]{0:T(128)S(1)}, f32[128]{0:T(128)S(1)}) all-reduce(f32[128]{0:T(128)S(1)} %get-tuple-element.8, f32[128]{0:T(128)S(1)} %get-tuple-element.7, f32[128]{0:T(128)S(1)} %get-tuple-element.6), channel_id=1, replica_groups=mesh['region'=2,'dom'=16] {'dom'}, use_global_device_ids=true, to_apply=%region_7.9 | all-reduce | flops 384 | bytes 3072 | tf_op jit(solution)/shard_map/psum | solution.py:64
  106.6 2.8 %fusion.106 = (bf16[1536,128]{1,0:T(8,128)(2,1)S(1)}, f32[1536,128]{1,0:T(8,128)}, f32[1536,128]{1,0:T(8,128)}) fusion(f32[1536,128]{1,0:T(8,128)S(1)} %get-tuple-element.63, f32[128]{0:T(128)S(1)} %get-tuple-element.47, f32[12,128,128]{1,2,0:T(8,128)} %copy-done.6, f32[128]{0:T(128)S(1)} %get-tuple-element.49, f32[128]{0:T(128)S(1)} %get-tuple-element.44, ...), kind=kLoop, calls=%fused_computation.173 | loop fusion | flops 2162688 | bytes 4327424 | tf_op jit(solution)/shard_map/convert_element_type | solution.py:44
  110.0 2.1 fusion.45
  112.7 4.7 %collective-permute-done.4 = bf16[6,128,128]{2,1,0:T(8,128)(2,1)S(1)} collective-permute-done((bf16[6,128,128]{2,1,0:T(8,128)(2,1)S(1)}, bf16[6,128,128]{2,1,0:T(8,128)(2,1)S(1)}, u32[]{:S(2)}, u32[]{:S(2)}) %collective-permute-start.4) | collective-permute-done | bytes 196640 | tf_op jit(solution)/shard_map/ppermute | solution.py:16
  119.0 2.5 gather_fusion.2
  126.5 30.1 %all-reduce.1 = (f32[128]{0:T(128)S(1)}, f32[128]{0:T(128)S(1)}, f32[128]{0:T(128)S(1)}) all-reduce(f32[128]{0:T(128)S(1)} %get-tuple-element.14, f32[128]{0:T(128)S(1)} %get-tuple-element.13, f32[128]{0:T(128)S(1)} %get-tuple-element.12), channel_id=1, replica_groups=mesh['region'=2,'dom'=16] {'dom'}, use_global_device_ids=true, to_apply=%region_13.15 | all-reduce | flops 384 | bytes 3072 | tf_op jit(solution)/shard_map/psum | solution.py:64
  157.2 3.0 %fusion.104 = (bf16[1536,128]{1,0:T(8,128)(2,1)S(1)}, f32[1536,128]{1,0:T(8,128)}, f32[1536,128]{1,0:T(8,128)}) fusion(f32[1536,128]{1,0:T(8,128)} %get-tuple-element.42, f32[128]{0:T(128)S(1)} %get-tuple-element.38, f32[1536,128]{1,0:T(8,128)} %get-tuple-element.43, f32[12,128,128]{1,2,0:T(8,128)} %copy-done.10, f32[128]{0:T(128)S(1)} %get-tuple-element.40), kind=kLoop, calls=%fused_computation.171 | loop fusion | flops 1179648 | bytes 4326400 | tf_op jit(solution)/shard_map/convert_element_type | solution.py:44
  163.5 4.7 %collective-permute-done.6 = bf16[6,128,128]{2,1,0:T(8,128)(2,1)S(1)} collective-permute-done((bf16[6,128,128]{2,1,0:T(8,128)(2,1)S(1)}, bf16[6,128,128]{2,1,0:T(8,128)(2,1)S(1)}, u32[]{:S(2)}, u32[]{:S(2)}) %collective-permute-start.6) | collective-permute-done | bytes 196640 | tf_op jit(solution)/shard_map/ppermute | solution.py:16
  169.8 2.5 gather_fusion.3
  177.3 30.1 %all-reduce = (f32[128]{0:T(128)S(1)}, f32[128]{0:T(128)S(1)}, f32[128]{0:T(128)S(1)}) all-reduce(f32[128]{0:T(128)S(1)} %get-tuple-element.10, f32[128]{0:T(128)S(1)} %get-tuple-element.11, f32[128]{0:T(128)S(1)} %get-tuple-element.9), channel_id=1, replica_groups=mesh['region'=2,'dom'=16] {'dom'}, use_global_device_ids=true, to_apply=%region_23.25 | all-reduce | flops 384 | bytes 3072 | tf_op jit(solution)/shard_map/psum | solution.py:64
  207.9 2.7 %fusion.102 = (bf16[1536,128]{1,0:T(8,128)(2,1)S(1)}, f32[1536,128]{1,0:T(8,128)}) fusion(f32[1536,128]{1,0:T(8,128)} %get-tuple-element.36, f32[128]{0:T(128)S(1)} %get-tuple-element.32, f32[1536,128]{1,0:T(8,128)} %get-tuple-element.37, f32[12,128,128]{1,2,0:T(8,128)} %copy-done.14, f32[128]{0:T(128)S(1)} %get-tuple-element.34), kind=kLoop, calls=%fused_computation.169 | loop fusion | flops 1179648 | bytes 3539968 | tf_op jit(solution)/shard_map/convert_element_type | solution.py:44
  211.1 2.2 fusion.49
  213.8 4.7 %collective-permute-done.8 = bf16[6,128,128]{2,1,0:T(8,128)(2,1)S(1)} collective-permute-done((bf16[6,128,128]{2,1,0:T(8,128)(2,1)S(1)}, bf16[6,128,128]{2,1,0:T(8,128)(2,1)S(1)}, u32[]{:S(2)}, u32[]{:S(2)}) %collective-permute-start.8) | collective-permute-done | bytes 196640 | tf_op jit(solution)/shard_map/ppermute | solution.py:16
  220.1 2.5 gather_fusion.4
  227.1 30.1 %psum.106 = f32[128]{0:T(128)S(1)} all-reduce(f32[128]{0:T(128)S(1)} %fusion.10), channel_id=1, replica_groups=mesh['region'=2,'dom'=16] {'dom'}, use_global_device_ids=true, to_apply=%region_25.27 | all-reduce | flops 128 | bytes 1024 | tf_op jit(solution)/shard_map/psum | solution.py:64
  257.2 3.1 %multiply_add_fusion = f32[1536,128]{1,0:T(8,128)} fusion(f32[1536,128]{1,0:T(8,128)} %get-tuple-element.31, f32[1536,128]{1,0:T(8,128)} %get-tuple-element.36, f32[1536,128]{1,0:T(8,128)} %get-tuple-element.42, f32[1536,128]{1,0:T(8,128)S(1)} %get-tuple-element.63, f32[128]{0:T(128)S(1)} %div.35, f32[128]{0:T(128)S(1)} %copy-done.31, f32[128]{0:T(128)S(1)} %copy-done.29, ...), kind=kLoop, calls=%fused_computation.38 | loop fusion | flops 2752512 | bytes 4721664 | tf_op jit(solution)/shard_map/add | solution.py:73
  (133 shorter events, 48.7 us)
Async XLA Ops:
  0.0 9.6 %copy-start.36 = (s32[12,4]{0,1:T(4,128)S(1)}, s32[12,4]{0,1:T(4,128)}, u32[]{:S(2)}) copy-start(s32[12,4]{0,1:T(4,128)} %param.9) | copy-start | bytes 580
  4.1 9.0 %collective-permute-start.1 = (bf16[6,128,128]{2,1,0:T(8,128)(2,1)}, bf16[6,128,128]{2,1,0:T(8,128)(2,1)}, u32[]{:S(2)}, u32[]{:S(2)}) collective-permute-start(bf16[6,128,128]{2,1,0:T(8,128)(2,1)} %bitcast.4), channel_id=1, source_target_pairs={{1,0},{2,1},{3,2},{4,3},{5,4},{6,5},{7,6},{8,7},{9,8},{10,9},{11,1... | collective-permute-start | bytes 589832 | tf_op jit(solution)/shard_map/ppermute | solution.py:19
  9.6 8.1 %collective-permute-start = (bf16[6,128,128]{2,1,0:T(8,128)(2,1)}, bf16[6,128,128]{2,1,0:T(8,128)(2,1)}, u32[]{:S(2)}, u32[]{:S(2)}) collective-permute-start(bf16[6,128,128]{2,1,0:T(8,128)(2,1)} %bitcast.2), channel_id=1, source_target_pairs={{0,1},{1,2},{2,3},{3,4},{4,5},{5,6},{6,7},{7,8},{8,9},{9,10},{10,1... | collective-permute-start | bytes 589832 | tf_op jit(solution)/shard_map/ppermute | solution.py:16
  58.8 3.2 %collective-permute-start.3 = (bf16[6,128,128]{2,1,0:T(8,128)(2,1)S(1)}, bf16[6,128,128]{2,1,0:T(8,128)(2,1)S(1)}, u32[]{:S(2)}, u32[]{:S(2)}) collective-permute-start(bf16[6,128,128]{2,1,0:T(8,128)(2,1)S(1)} %bitcast.176), channel_id=1, source_target_pairs={{1,0},{2,1},{3,2},{4,3},{5,4},{6,5},{7,6},{8,7},{9,8},{10,9},{11,1... | collective-permute-start | bytes 589832 | tf_op jit(solution)/shard_map/ppermute | solution.py:19
  58.8 7.8 %collective-permute-start.2 = (bf16[6,128,128]{2,1,0:T(8,128)(2,1)S(1)}, bf16[6,128,128]{2,1,0:T(8,128)(2,1)S(1)}, u32[]{:S(2)}, u32[]{:S(2)}) collective-permute-start(bf16[6,128,128]{2,1,0:T(8,128)(2,1)S(1)} %bitcast.172), channel_id=1, source_target_pairs={{0,1},{1,2},{2,3},{3,4},{4,5},{5,6},{6,7},{7,8},{8,9},{9,10},{10,1... | collective-permute-start | bytes 589832 | tf_op jit(solution)/shard_map/ppermute | solution.py:16
  62.0 4.7 %copy-start.18 = (bf16[6,128,128]{2,1,0:T(8,128)(2,1)}, bf16[6,128,128]{2,1,0:T(8,128)(2,1)S(1)}, u32[]{:S(2)}) copy-start(bf16[6,128,128]{2,1,0:T(8,128)(2,1)S(1)} %collective-permute-done.3) | copy-start | bytes 589828
  75.1 30.9 %copy-start.37 = (f32[128]{0:T(128)S(1)}, f32[128]{0:T(128)}, u32[]{:S(2)}) copy-start(f32[128]{0:T(128)} %get-tuple-element.48) | copy-start | bytes 1540
  106.6 2.8 %copy-start.32 = (f32[128]{0:T(128)}, f32[128]{0:T(128)S(1)}, u32[]{:S(2)}) copy-start(f32[128]{0:T(128)S(1)} %get-tuple-element.46) | copy-start | bytes 1540
  109.5 3.2 %collective-permute-start.5 = (bf16[6,128,128]{2,1,0:T(8,128)(2,1)S(1)}, bf16[6,128,128]{2,1,0:T(8,128)(2,1)S(1)}, u32[]{:S(2)}, u32[]{:S(2)}) collective-permute-start(bf16[6,128,128]{2,1,0:T(8,128)(2,1)S(1)} %bitcast.177), channel_id=1, source_target_pairs={{1,0},{2,1},{3,2},{4,3},{5,4},{6,5},{7,6},{8,7},{9,8},{10,9},{11,1... | collective-permute-start | bytes 589832 | tf_op jit(solution)/shard_map/ppermute | solution.py:19
  109.5 7.8 %collective-permute-start.4 = (bf16[6,128,128]{2,1,0:T(8,128)(2,1)S(1)}, bf16[6,128,128]{2,1,0:T(8,128)(2,1)S(1)}, u32[]{:S(2)}, u32[]{:S(2)}) collective-permute-start(bf16[6,128,128]{2,1,0:T(8,128)(2,1)S(1)} %bitcast.173), channel_id=1, source_target_pairs={{0,1},{1,2},{2,3},{3,4},{4,5},{5,6},{6,7},{7,8},{8,9},{9,10},{10,1... | collective-permute-start | bytes 589832 | tf_op jit(solution)/shard_map/ppermute | solution.py:16
  112.7 4.7 %copy-start.20 = (bf16[6,128,128]{2,1,0:T(8,128)(2,1)}, bf16[6,128,128]{2,1,0:T(8,128)(2,1)S(1)}, u32[]{:S(2)}) copy-start(bf16[6,128,128]{2,1,0:T(8,128)(2,1)S(1)} %collective-permute-done.5) | copy-start | bytes 589828
  124.9 31.7 %copy-start.35 = (f32[128]{0:T(128)S(1)}, f32[128]{0:T(128)}, u32[]{:S(2)}) copy-start(f32[128]{0:T(128)} %get-tuple-element.45) | copy-start | bytes 1540
  157.2 3.0 %copy-start.28 = (f32[128]{0:T(128)}, f32[128]{0:T(128)S(1)}, u32[]{:S(2)}) copy-start(f32[128]{0:T(128)S(1)} %get-tuple-element.40) | copy-start | bytes 1540
  160.2 3.2 %collective-permute-start.7 = (bf16[6,128,128]{2,1,0:T(8,128)(2,1)S(1)}, bf16[6,128,128]{2,1,0:T(8,128)(2,1)S(1)}, u32[]{:S(2)}, u32[]{:S(2)}) collective-permute-start(bf16[6,128,128]{2,1,0:T(8,128)(2,1)S(1)} %bitcast.178), channel_id=1, source_target_pairs={{1,0},{2,1},{3,2},{4,3},{5,4},{6,5},{7,6},{8,7},{9,8},{10,9},{11,1... | collective-permute-start | bytes 589832 | tf_op jit(solution)/shard_map/ppermute | solution.py:19
  160.3 7.8 %collective-permute-start.6 = (bf16[6,128,128]{2,1,0:T(8,128)(2,1)S(1)}, bf16[6,128,128]{2,1,0:T(8,128)(2,1)S(1)}, u32[]{:S(2)}, u32[]{:S(2)}) collective-permute-start(bf16[6,128,128]{2,1,0:T(8,128)(2,1)S(1)} %bitcast.174), channel_id=1, source_target_pairs={{0,1},{1,2},{2,3},{3,4},{4,5},{5,6},{6,7},{7,8},{8,9},{9,10},{10,1... | collective-permute-start | bytes 589832 | tf_op jit(solution)/shard_map/ppermute | solution.py:16
  163.5 4.7 %copy-start.22 = (bf16[6,128,128]{2,1,0:T(8,128)(2,1)}, bf16[6,128,128]{2,1,0:T(8,128)(2,1)S(1)}, u32[]{:S(2)}) copy-start(bf16[6,128,128]{2,1,0:T(8,128)(2,1)S(1)} %collective-permute-done.7) | copy-start | bytes 589828
  175.7 31.7 %copy-start.34 = (f32[128]{0:T(128)S(1)}, f32[128]{0:T(128)}, u32[]{:S(2)}) copy-start(f32[128]{0:T(128)} %get-tuple-element.39) | copy-start | bytes 1540
  210.6 3.2 %collective-permute-start.9 = (bf16[6,128,128]{2,1,0:T(8,128)(2,1)S(1)}, bf16[6,128,128]{2,1,0:T(8,128)(2,1)S(1)}, u32[]{:S(2)}, u32[]{:S(2)}) collective-permute-start(bf16[6,128,128]{2,1,0:T(8,128)(2,1)S(1)} %bitcast.179), channel_id=1, source_target_pairs={{1,0},{2,1},{3,2},{4,3},{5,4},{6,5},{7,6},{8,7},{9,8},{10,9},{11,1... | collective-permute-start | bytes 589832 | tf_op jit(solution)/shard_map/ppermute | solution.py:19
  210.6 7.8 %collective-permute-start.8 = (bf16[6,128,128]{2,1,0:T(8,128)(2,1)S(1)}, bf16[6,128,128]{2,1,0:T(8,128)(2,1)S(1)}, u32[]{:S(2)}, u32[]{:S(2)}) collective-permute-start(bf16[6,128,128]{2,1,0:T(8,128)(2,1)S(1)} %bitcast.175), channel_id=1, source_target_pairs={{0,1},{1,2},{2,3},{3,4},{4,5},{5,6},{6,7},{7,8},{8,9},{9,10},{10,1... | collective-permute-start | bytes 589832 | tf_op jit(solution)/shard_map/ppermute | solution.py:16
  213.8 4.7 %copy-start.16 = (bf16[6,128,128]{2,1,0:T(8,128)(2,1)}, bf16[6,128,128]{2,1,0:T(8,128)(2,1)S(1)}, u32[]{:S(2)}) copy-start(bf16[6,128,128]{2,1,0:T(8,128)(2,1)S(1)} %collective-permute-done.9) | copy-start | bytes 589828
  226.0 31.2 %copy-start.38 = (f32[128]{0:T(128)S(1)}, f32[128]{0:T(128)}, u32[]{:S(2)}) copy-start(f32[128]{0:T(128)} %get-tuple-element.33) | copy-start | bytes 1540
  226.0 31.2 %copy-start.29 = (f32[128]{0:T(128)S(1)}, f32[128]{0:T(128)}, u32[]{:S(2)}) copy-start(f32[128]{0:T(128)} %copy-done.28) | copy-start | bytes 1540
  226.0 31.2 %copy-start.31 = (f32[128]{0:T(128)S(1)}, f32[128]{0:T(128)}, u32[]{:S(2)}) copy-start(f32[128]{0:T(128)} %copy-done.30) | copy-start | bytes 1540
  226.0 31.2 %copy-start.33 = (f32[128]{0:T(128)S(1)}, f32[128]{0:T(128)}, u32[]{:S(2)}) copy-start(f32[128]{0:T(128)} %copy-done.32) | copy-start | bytes 1540
  (25 other events, 33.9 us)
where the time goes:
time: 262 us; the launch traced here: 260 us
  blocking collectives  150 us (57%)
  matrix products  29.5 us (11%)
  waiting for transfers between devices  26.7 us (10%)
  local copies, waits for them, and re-layouts  24 us (9%)
  other arithmetic  22.2 us (8%)
  starting transfers between devices  7.7 us (3%)
    psum x5, blocking collectives, shards(): lax.psum((jnp.sum(direction * applied, axis=0), jnp.sum(residual * applie...  150 us
    ppermute x5, waiting for transfers between devices, padded(): lax.ppermute(lax.slice_in_dim(block, block.shape[dim] - width, None, axis...  23.2 us
    gather x5, local copies, waits for them, and re-layouts, shards(): distant = jnp.take(extended, far_position, axis=0)  12.4 us
    dot_general x5, matrix products, shards(): jnp.einsum('bij,bjq->biq', affinity[:, 0], operate_rounded, preferred_ele...  10.8 us
    unnamed x78, local copies, waits for them, and re-layouts  10.6 us
    convert_element_type x4, other arithmetic, shards(): direction.astype(jnp.bfloat16).reshape(block_count, tile_rows, query_count)  9.76 us
    dot_general x5, matrix products, shards(): jnp.einsum('bij,bjq->biq', affinity[:, 3], distant, preferred_element_typ...  7.83 us
    dot_general x5, matrix products, shards(): jnp.einsum('bij,bjq->biq', affinity[:, 1], below, preferred_element_type=...  7.2 us
  transfers between devices with their start and end apart: 10, of which 10 were waited for; matrix products, arithmetic and copies ran while one was open for 4% of the time, Pallas kernels for 0%

commit v1 on v0

v1 whole, which is shorter than its diff:
```python
import functools

import jax
import jax.numpy as jnp
from jax import lax
from jax.experimental import pallas as pl
from jax.experimental.pallas import tpu as pltpu
from jax.sharding import PartitionSpec as P

HALO_W = 6
NAMED = 3
ITERATIONS = 5
DAMP = 0.99
SHIFTS = (0.0, 1.0, -0.25, 0.5)
PIVOT_MIN = 1e-6
BF = jnp.bfloat16
F32 = jnp.float32
PAIRS = [(i, j) for i in range(ITERATIONS) for j in range(i, ITERATIONS)]
ROWS = len(PAIRS) + 1
ENTRIES = 2 + 2 * NAMED

VMEM = pl.BlockSpec(memory_space=pltpu.VMEM)
SMEM = pl.BlockSpec(memory_space=pltpu.SMEM)
ANY = pl.BlockSpec(memory_space=pl.ANY)


def params(mib):
    return pltpu.CompilerParams(vmem_limit_bytes=mib << 20)


def dot(a, b):
    return jnp.dot(a, b, preferred_element_type=F32)


def dot_t(a, b):
    return lax.dot_general(a, b, (((0,), (0,)), ((), ())), preferred_element_type=F32)


def put_split(ref, index, value):
    high = value.astype(BF)
    width = value.shape[-1]
    ref[index, :, :width] = high
    ref[index, :, width:] = (value - high.astype(F32)).astype(BF)


def row_product(aff, pos, base, g, hl):
    count = aff.shape[0]
    width = hl.shape[2] // 2
    lower = hl[g - 1] if g > 0 else hl[pos[2 * count + base // count]]
    upper = hl[g + 1] if g + 1 < count else hl[pos[2 * count + 2 + base // count]]
    left = jnp.concatenate([aff[g, 0], aff[g, 1]], axis=1)
    right = jnp.concatenate([hl[g], lower], axis=0)
    out = dot(left, right)
    left = jnp.concatenate([aff[g, 2], aff[g, 3]], axis=1)
    right = jnp.concatenate([upper, hl[pos[base + g]]], axis=0)
    out = out + dot(left, right)
    return out[:, :width] + out[:, width:]


def pack(meta, shift, t, y, send, base):
    for j in range(NAMED):
        g = meta[base + j]
        value = t[g]
        send[j] = value.astype(BF)
        send[NAMED + j] = (y[g] - shift * value).astype(BF)


def first_kernel(pos, lists, desc, queries, aff, t0, y0, send_a, send_b, hl, buf, sems, *, chunks):
    count, rows = t0.shape[0], t0.shape[1]
    per = count // chunks
    copies = []
    for c in range(chunks):
        copy = pltpu.make_async_copy(
            desc.at[pl.ds(c * per * rows, per * rows)], buf.at[c], sems.at[c]
        )
        copy.start()
        copies.append(copy)
    hl[count + 2 * NAMED] = jnp.zeros(hl.shape[1:], BF)
    for c in range(chunks):
        copies[c].wait()
        scores = lax.dot_general(
            buf[c], queries[...], (((1,), (1,)), ((), ())), preferred_element_type=F32
        )
        value = jnp.maximum(scores, 0.0)
        value = value * value * value
        for i in range(per):
            block = value[i * rows : (i + 1) * rows]
            t0[c * per + i] = block
            put_split(hl, c * per + i, block)
    for g in range(count):
        y0[g] = row_product(aff, pos, 0, g, hl)
    pack(lists, SHIFTS[0], t0, y0, send_b, NAMED)
    pack(lists, SHIFTS[0], t0, y0, send_a, 0)


def two_steps(pos, cross, aff, t, y, recv_a, recv_b, t1, t2, hl, hl2, acc, hacc, step):
    count, width = t.shape[0], t.shape[2]
    zero = count + 2 * NAMED
    hl[zero] = jnp.zeros(hl.shape[1:], BF)
    hl2[zero] = jnp.zeros(hl.shape[1:], BF)
    for h in range(NAMED):
        hl[count + h, :, :width] = recv_a[h]
        hl[count + NAMED + h, :, :width] = recv_b[h]
        hacc[h] = recv_a[NAMED + h].astype(F32)
        hacc[NAMED + h] = recv_b[NAMED + h].astype(F32)
    for g in range(count):
        acc[g] = y[g] - SHIFTS[step] * t[g]
    for e in range(ENTRIES):
        g, slot, h = cross[3 * e], cross[3 * e + 1], cross[3 * e + 2]
        row = jnp.minimum(g, count - 1)
        tile = aff[row, slot]
        acc[g] += dot(tile, hl[count + h, :, :width])
        hacc[h] += dot_t(tile, t[row].astype(BF))
    for g in range(count):
        value = acc[g]
        t1[g] = value
        put_split(hl, g, value)
    for h in range(2 * NAMED):
        put_split(hl, count + h, hacc[h])
    for g in range(count):
        value = row_product(aff, pos, count, g, hl) - SHIFTS[step + 1] * t1[g]
        t2[g] = value
        put_split(hl2, g, value)


def middle_kernel(
    pos, lists, cross, aff, t, y, recv_a, recv_b, t1, t2, y2, send_a, send_b, hl, hl2, acc, hacc
):
    two_steps(pos, cross, aff, t, y, recv_a, recv_b, t1, t2, hl, hl2, acc, hacc, 0)
    for g in range(t.shape[0]):
        y2[g] = row_product(aff, pos, 0, g, hl2)
    pack(lists, SHIFTS[2], t2, y2, send_b, NAMED)
    pack(lists, SHIFTS[2], t2, y2, send_a, 0)


def last_kernel(
    pos, lists, cross, aff, t, y, recv_a, recv_b, t3, t4, send, hl, hl2, acc, hacc
):
    two_steps(pos, cross, aff, t, y, recv_a, recv_b, t3, t4, hl, hl2, acc, hacc, 2)
    for j in range(NAMED):
        send[j] = t4[lists[2 * NAMED + j]].astype(BF)


def gram_kernel(pos, aff, t0, t1, t2, t3, t4, out, hl):
    count, rows, width = t0.shape
    hl[count + 2 * NAMED] = jnp.zeros(hl.shape[1:], BF)
    for g in range(count):
        put_split(hl, g, t4[g])
    fields = (t0, t1, t2, t3, t4)
    sums = [jnp.zeros((8, width), F32) for _ in range(ROWS)]
    for g in range(count):
        local = row_product(aff, pos, 0, g, hl)
        sums[-1] = sums[-1] + (t4[g] * local).reshape(rows // 8, 8, width).sum(0)

    def body(i, sums):
        sums = list(sums)
        g = i // (rows // 32)
        start = pl.multiple_of((i % (rows // 32)) * 32, 32)
        for part in range(4):
            v = [f[g, pl.ds(pl.multiple_of(start + 8 * part, 8), 8), :] for f in fields]
            for n, (a, b) in enumerate(PAIRS):
                sums[n] = sums[n] + v[a] * v[b]
        return tuple(sums)

    sums = lax.fori_loop(0, count * rows // 32, body, tuple(sums))
    for n in range(ROWS):
        out[pl.ds(n, 1), :] = jnp.sum(sums[n], axis=0, keepdims=True)


def cross_kernel(lists, cross, aff, t4, recv, gram, out):
    count = t4.shape[0]
    total = jnp.zeros((8, gram.shape[1]), F32)
    for e in range(1 + NAMED):
        g, slot, h = (cross[3 * ENTRIES + 3 * e + i] for i in range(3))
        row = jnp.minimum(g, count - 1)
        part = t4[row] * dot(aff[row, slot], recv[jnp.minimum(h, NAMED - 1)])
        part = part.reshape(-1, 8, part.shape[-1]).sum(0)
        total = total + jnp.where(g < count, part, 0.0)
    value = gram[...]
    extra = 2.0 * jnp.sum(total, axis=0, keepdims=True)
    index = lax.broadcasted_iota(jnp.int32, value.shape, 0)
    value = value + jnp.where(index == ROWS - 1, extra, 0.0)
    for d in range(out.shape[0]):
        out[d] = value


def final_kernel(parts, t0, t1, t2, t3, t4, out):
    n = ITERATIONS
    value = parts[0]
    for d in range(1, parts.shape[0]):
        value = value + parts[d]
    gram = {}
    for k, (i, j) in enumerate(PAIRS):
        gram[i, j] = gram[j, i] = value[k : k + 1]
    matrix = {}
    for i in range(n):
        for j in range(i, n):
            terms = []
            if j + 1 < n:
                terms.append(gram[i, j + 1] + SHIFTS[j] * gram[i, j])
            if i + 1 < n and i != j:
                terms.append(gram[i + 1, j] + SHIFTS[i] * gram[i, j])
            if not terms:
                terms = [value[ROWS - 1 : ROWS]]
            product = terms[0] if len(terms) == 1 else 0.5 * (terms[0] + terms[1])
            matrix[i, j] = gram[i, j] - DAMP * product
    scale = [
        jnp.where(matrix[i, i] > 0.0, lax.rsqrt(jnp.maximum(matrix[i, i], 1e-37)), 0.0)
        for i in range(n)
    ]
    for i in range(n):
        for j in range(i, n):
            matrix[i, j] = matrix[i, j] * (scale[i] * scale[j])
    right = [gram[i, 0] * scale[i] for i in range(n)]
    inverse = []
    for k in range(n):
        pivot = matrix[k, k]
        inverse.append(jnp.where(pivot > PIVOT_MIN, 1.0 / jnp.maximum(pivot, PIVOT_MIN), 0.0))
        for i in range(k + 1, n):
            factor = matrix[k, i] * inverse[k]
            for j in range(i, n):
                matrix[i, j] = matrix[i, j] - factor * matrix[k, j]
            right[i] = right[i] - factor * right[k]
    coef = [None] * n
    for k in range(n - 1, -1, -1):
        rest = right[k]
        for j in range(k + 1, n):
            rest = rest - matrix[k, j] * coef[j]
        coef[k] = rest * inverse[k]
    coef = [coef[k] * scale[k] for k in range(n)]
    fields = (t0, t1, t2, t3, t4)
    count, rows, width = t0.shape
    wide = [jnp.broadcast_to(c, (8, width)) for c in coef]
    for g in range(count):
        total = None
        for f, c in zip(fields, coef):
            term = f[g] * c
            total = term if total is None else total + term
        out[pl.ds(g * rows, rows), :] = total


def tables(tile_col, count, axis):
    devices = lax.axis_size(axis)
    total = count * devices
    me = lax.axis_index(axis)
    even = me % 2 == 0
    relative = (tile_col[:, 3] - me * count) % total
    local = relative < count
    up = (relative >= count) & (relative < count + HALO_W)
    low = relative >= total - HALO_W
    up_place = relative - count
    low_place = relative - (total - HALO_W)
    places = jnp.arange(HALO_W)
    blocks = jnp.arange(count)
    up_named = jnp.any(up[:, None] & (up_place[:, None] == places), 0) | (places == 0)
    low_named = jnp.any(low[:, None] & (low_place[:, None] == places), 0) | (places == HALO_W - 1)
    up_rank = jnp.sum(up_named[None] & (places[None] < up_place[:, None]), 1)
    low_rank = jnp.sum(low_named[None] & (places[None] < low_place[:, None]), 1)
    up_base = jnp.where(even, 0, NAMED)
    low_base = NAMED - up_base
    halo = jnp.where(up, up_base + up_rank, low_base + low_rank)
    halo = jnp.clip(halo, 0, 2 * NAMED - 1)
    zero = count + 2 * NAMED
    pos_local = jnp.where(local, relative, zero)
    pos_full = jnp.where(local, relative, count + halo)
    low_chain = low_base + NAMED - 1
    up_chain = up_base
    pos = jnp.concatenate(
        [pos_local, pos_full, jnp.stack([zero + 0 * me, count + low_chain, zero + 0 * me, count + up_chain])]
    )

    def members(flag, fill):
        rank = jnp.sum(flag[None] & (blocks[None] < blocks[:, None]), 1)
        hit = flag[None] & (rank[None] == jnp.arange(NAMED)[:, None])
        return jnp.sum(jnp.where(hit, blocks[None] + 1, 0), 1) - 1, hit

    up_list, _ = members(up | (blocks == count - 1), 0)
    low_list, _ = members(low | (blocks == 0), 0)
    up_list = jnp.clip(up_list, 0, count - 1)
    low_list = jnp.clip(low_list, 0, count - 1)
    lists = jnp.concatenate(
        [jnp.where(even, up_list, low_list), jnp.where(even, low_list, up_list), low_list]
    )

    def entries(flag, rank, base, chain_row, chain_slot, chain_rank):
        rows, hit = members(flag, count)
        used = rows >= 0
        ranks = jnp.sum(jnp.where(hit, rank[None], 0), 1)
        rows = jnp.where(used, rows, count)
        ranks = jnp.where(used, jnp.clip(base + ranks, 0, 2 * NAMED - 1), 2 * NAMED)
        first = jnp.stack([chain_row + 0 * base, chain_slot + 0 * base, base + chain_rank])
        rest = jnp.stack([rows, 3 + 0 * rows, ranks], 1).reshape(-1)
        return jnp.concatenate([first, rest])

    cross = jnp.concatenate(
        [
            entries(low, low_rank, low_base, 0, 1, NAMED - 1),
            entries(up, up_rank, up_base, count - 1, 2, 0),
            entries(up, up_rank, 0 * up_base, count - 1, 2, 0),
        ]
    )
    return pos.astype(jnp.int32), lists.astype(jnp.int32), cross.astype(jnp.int32)


def swap(block_a, block_b, axis):
    n = lax.axis_size(axis)
    pairs_a = [(i, i ^ 1) for i in range(n)]
    pairs_b = [(i, (i + 1) % n if i % 2 else (i - 1) % n) for i in range(n)]
    got_b = lax.ppermute(block_b, axis, pairs_b)
    got_a = lax.ppermute(block_a, axis, pairs_a)
    return got_a, got_b


def shards(descriptors, queries, affinity, tile_col):
    count, _, rows, _ = affinity.shape
    width = queries.shape[0]
    depth = descriptors.shape[1]
    axis = "dom"
    devices = lax.axis_size(axis)
    pos, lists, cross = tables(tile_col, count, axis)
    blocks = count + 2 * NAMED + 1
    field = jax.ShapeDtypeStruct((count, rows, width), F32)
    edge = jax.ShapeDtypeStruct((2 * NAMED, rows, width), BF)
    half = jax.ShapeDtypeStruct((NAMED, rows, width), BF)
    split = pltpu.VMEM((blocks, rows, 2 * width), BF)
    work = [
        split,
        split,
        pltpu.VMEM((count + 1, rows, width), F32),
        pltpu.VMEM((2 * NAMED + 1, rows, width), F32),
    ]
    chunks = 4
    flops = 2 * count * rows * 4 * rows * 2 * width

    def cost(products, extra=0, bytes_accessed=4 << 20):
        return pl.CostEstimate(
            flops=products * flops + extra, bytes_accessed=bytes_accessed, transcendentals=0
        )

    t0, y0, send_a, send_b = pl.pallas_call(
        functools.partial(first_kernel, chunks=chunks),
        out_shape=(field, field, edge, edge),
        in_specs=[SMEM, SMEM, ANY, VMEM, VMEM],
        out_specs=(VMEM,) * 4,
        scratch_shapes=[
            split,
            pltpu.VMEM((chunks, count * rows // chunks, depth), BF),
            pltpu.SemaphoreType.DMA((chunks,)),
        ],
        compiler_params=params(24),
        cost_estimate=cost(1, 2 * count * rows * depth * width),
        name="first",
    )(pos, lists, descriptors, queries, affinity)
    recv_a, recv_b = swap(send_a, send_b, axis)
    t1, t2, y2, send_a, send_b = pl.pallas_call(
        middle_kernel,
        out_shape=(field, field, field, edge, edge),
        in_specs=[SMEM] * 3 + [VMEM] * 5,
        out_specs=(VMEM,) * 5,
        scratch_shapes=work,
        compiler_params=params(24),
        cost_estimate=cost(2),
        name="middle",
    )(pos, lists, cross, affinity, t0, y0, recv_a, recv_b)
    recv_a, recv_b = swap(send_a, send_b, axis)
    t3, t4, send = pl.pallas_call(
        last_kernel,
        out_shape=(field, field, half),
        in_specs=[SMEM] * 3 + [VMEM] * 5,
        out_specs=(VMEM,) * 3,
        scratch_shapes=work,
        compiler_params=params(24),
        cost_estimate=cost(2),
        name="last",
    )(pos, lists, cross, affinity, t2, y2, recv_a, recv_b)
    recv = lax.ppermute(send, axis, [(i, (i - 1) % devices) for i in range(devices)])
    gram = pl.pallas_call(
        gram_kernel,
        out_shape=jax.ShapeDtypeStruct((ROWS, width), F32),
        in_specs=[SMEM] + [VMEM] * 6,
        out_specs=VMEM,
        scratch_shapes=[split],
        compiler_params=params(24),
        cost_estimate=cost(1),
        name="gram",
    )(pos, affinity, t0, t1, t2, t3, t4)
    parts = pl.pallas_call(
        cross_kernel,
        out_shape=jax.ShapeDtypeStruct((devices, ROWS, width), F32),
        in_specs=[SMEM] * 2 + [VMEM] * 4,
        out_specs=VMEM,
        compiler_params=params(8),
        name="cross",
    )(lists, cross, affinity, t4, recv, gram)
    parts = lax.all_to_all(parts, axis, 0, 0)
    return pl.pallas_call(
        final_kernel,
        out_shape=jax.ShapeDtypeStruct((count * rows, width), F32),
        in_specs=[VMEM] * 6,
        out_specs=VMEM,
        compiler_params=params(24),
        name="final",
    )(parts, t0, t1, t2, t3, t4)


def solution(mesh):
    return jax.shard_map(
        shards,
        mesh=mesh,
        in_specs=(
            P(("region", "dom"), None),
            P("region", None),
            P(("region", "dom"), None, None, None),
            P(("region", "dom"), None),
        ),
        out_specs=P(("region", "dom"), None),
        check_vma=False,
    )
```

time: 262 us -> 56 us (0.21)
  blocking collectives: 150 us -> 13.2 us
  matrix products: 29.5 us -> 0 us
  waiting for transfers between devices: 26.7 us -> 5.53 us
  other arithmetic: 22.2 us -> 4.36 us
  local copies, waits for them, and re-layouts: 24 us -> 8.42 us
  Pallas kernels: 0 us -> 13.1 us
  starting transfers between devices: 7.7 us -> 11 us
    psum x5 -> x0, blocking collectives: 150 us -> none  [shards(): lax.psum((jnp.sum(direction * applied, axis=0), jnp.sum(residual * applie...]
    dot_general x21 -> x0, matrix products: 29.5 us -> none  [the longest x5 10.8 us: shards(): jnp.einsum('bij,bjq->biq', affinity[:, 0], operate_rounded, preferred_ele...]
    ppermute x10 -> x5, waiting for transfers between devices: 26.7 us -> 5.53 us  [the longest x2 5.52 us: swap(): got_b = lax.ppermute(block_b, axis, pairs_b)]
    all_to_all x0 -> x1, blocking collectives: none -> 13.2 us  [shards(): parts = lax.all_to_all(parts, axis, 0, 0)]
    pallas_call x0 -> x6, Pallas kernels: none -> 13.1 us  [the longest x1 4.23 us: shards(): pl.pallas_call(functools.partial(first_kernel, chunks=chunks), out_shape=...]
    gather x5 -> x0, local copies, waits for them, and re-layouts: 12.4 us -> none  [shards(): distant = jnp.take(extended, far_position, axis=0)]
    convert_element_type x4 -> x0, other arithmetic: 9.76 us -> none  [shards(): direction.astype(jnp.bfloat16).reshape(block_count, tile_rows, query_count)]
    unnamed x78 -> x8, local copies, waits for them, and re-layouts: 10.6 us -> 4.01 us
  transfers between devices with their start and end apart: 10 -> 5, of which waited for: 10 -> 1; matrix products, arithmetic and copies ran while one was open for 4% -> 10% of each run, Pallas kernels for 0% -> 5%
where the time goes in v1:
time: 56 us; the launch traced here: 55.6 us
  blocking collectives  13.2 us (24%)
  Pallas kernels  13.1 us (23%)
  starting transfers between devices  11 us (20%)
  local copies, waits for them, and re-layouts  8.42 us (15%)
  waiting for transfers between devices  5.53 us (10%)
  other arithmetic  4.36 us (8%)
    all_to_all x1, blocking collectives, shards(): parts = lax.all_to_all(parts, axis, 0, 0)  13.2 us
    ppermute x2, starting transfers between devices, swap(): got_b = lax.ppermute(block_b, axis, pairs_b)  8.01 us
    ppermute x2, waiting for transfers between devices, swap(): got_b = lax.ppermute(block_b, axis, pairs_b)  5.52 us
    pallas_call x1, Pallas kernels, shards(): pl.pallas_call(functools.partial(first_kernel, chunks=chunks), out_shape=...  4.23 us
    unnamed x8, local copies, waits for them, and re-layouts  4.01 us
    pallas_call x1, Pallas kernels, shards(): pl.pallas_call(gram_kernel, out_shape=jax.ShapeDtypeStruct((ROWS, width),...  2.63 us
    pallas_call x1, Pallas kernels, shards(): pl.pallas_call(middle_kernel, out_shape=(field, field, field, edge, edge)...  2.43 us
    ppermute x1, starting transfers between devices, shards(): lax.ppermute(send, axis, [(i, (i - 1) % devices) for i in range(devices)])  2.33 us
  transfers between devices with their start and end apart: 5, of which 1 were waited for; matrix products, arithmetic and copies ran while one was open for 10% of the time, Pallas kernels for 5%

profile of v1, /device:TPU:0, one launch (start us, length us, event | category | flops | bytes accessed | tf_op | source)
XLA Modules:
  0.0 55.6 jit_solution(15419920872799541075)
XLA Ops:
  0.0 0.7 %compare_bitcast_fusion = (pred[12]{0:T(512)(128)(4,1)S(1)}, s32[12,1]{0,1:T(1,128)S(1)}) fusion(s32[]{:T(128)S(6)} %mul.3, s32[12,4]{0,1:T(4,128)} %param.7), kind=kLoop, calls=%fused_computation.46 | loop fusion | flops 96 | bytes 112 | tf_op jit(solution)/shard_map/and | solution.py:256
  1.1 0.7 %compare_select_fusion = (s32[12]{0:T(128)S(1)}, s32[12]{0:T(128)S(1)}) fusion(s32[12]{0:T(128)S(1)} %get-tuple-element.59, s32[12]{0:T(128)S(1)} %get-tuple-element.58, s32[]{:T(128)S(6)} %sub.57, s32[]{:T(128)} %select_n.139, s32[]{:T(128)S(6)} %mul.3, s32[12,4]{0,1:T(4,128)} %param.7), kind=kLoop, calls=%fused_computation.21 | loop fusion | flops 204 | bytes 252 | tf_op jit(solution)/shard_map/jit(_where)/select_n | solution.py:265
  2.3 0.7 %select_reduce_fusion.1 = (s32[3]{0:T(128)}, s32[3]{0:T(128)}, s32[3]{0:T(128)S(1)}, s32[3]{0:T(128)S(1)}, s32[3]{0:T(128)S(1)}, /*index=5*/s32[3]{0:T(128)S(1)}) fusion(s32[12]{0:T(128)S(1)} %convert_reduce_fusion, s32[12]{0:T(128)S(1)} %iota_add_fusion, pred[12]{0:T(512)(128)(4,1)S(1)} %get-tuple-element.55, s32[12]{0:T(128)S(1)} %get-tuple-element.58, ...), kind=kLoop, calls=%fused_computation.30 | loop fusion | flops 702 | bytes 456 | tf_op jit(solution)/shard_map/reduce_sum | solution.py:275
  3.1 1.4 %copy-done = bf16[12,4,128,128]{3,2,1,0:T(8,128)(2,1)S(1)} copy-done((bf16[12,4,128,128]{3,2,1,0:T(8,128)(2,1)S(1)}, bf16[12,4,128,128]{3,2,1,0:T(8,128)(2,1)}, u32[]{:S(2)}) %copy-start) | copy-done | bytes 1572888
  4.6 1.7 %copy-done.2 = bf16[1536,768]{1,0:T(8,128)(2,1)S(1)} copy-done((bf16[1536,768]{1,0:T(8,128)(2,1)S(1)}, bf16[1536,768]{1,0:T(8,128)(2,1)}, u32[]{:S(2)}) %copy-start.2) | copy-done | bytes 2359320
  6.2 0.9 %copy-done.3 = bf16[128,768]{1,0:T(8,128)(2,1)S(1)} copy-done((bf16[128,768]{1,0:T(8,128)(2,1)S(1)}, bf16[128,768]{1,0:T(8,128)(2,1)}, u32[]{:S(2)}) %copy-start.3) | copy-done | bytes 196632
  7.2 4.2 %first.1 = (f32[12,128,128]{2,1,0:T(8,128)S(1)}, f32[12,128,128]{2,1,0:T(8,128)S(1)}, bf16[6,128,128]{2,1,0:T(8,128)(2,1)}, bf16[6,128,128]{2,1,0:T(8,128)(2,1)}) custom-call(s32[28]{0:T(128)S(1)} %concatenate.11.pos, s32[9]{0:T(128)S(1)} %pad_add_fusion.3.lists, bf16[1536,768]{1,0:T(8,128)(2,1)S(1)} %copy-done.2, bf16[128,768]{1,0:T(8,128)(2,1)S(1)} %copy-done.3, ...), custom_call_target="tpu_custom_call" | custom-call | flops 704643072 | bytes 4194304 | tf_op jit(solution)/shard_map/first/pallas_call | solution.py:340
  12.0 5.7 %collective-permute-start.1 = (bf16[6,128,128]{2,1,0:T(8,128)(2,1)}, bf16[6,128,128]{2,1,0:T(8,128)(2,1)S(1)}, u32[]{:S(2)}, u32[]{:S(2)}) collective-permute-start(bf16[6,128,128]{2,1,0:T(8,128)(2,1)} %get-tuple-element.20), channel_id=1, source_target_pairs={{0,15},{1,2},{2,1},{3,4},{4,3},{5,6},{6,5},{7,8},{8,7},{9,10},{10,... | collective-permute-start | bytes 589832 | tf_op jit(solution)/shard_map/ppermute | solution.py:309
  17.7 0.7 %compare_select_fusion.4 = (s32[3,1]{0,1:T(1,128)S(1)}, s32[3,1]{0,1:T(1,128)S(1)}, s32[3,1]{0,1:T(1,128)S(1)}) fusion(s32[3]{0:T(128)} %get-tuple-element.30, s32[3]{0:T(128)} %get-tuple-element.29, s32[]{:T(128)} %select_n.139), kind=kLoop, calls=%fused_computation.52 | loop fusion | flops 24 | bytes 64 | tf_op jit(solution)/shard_map/jit(_where)/select_n | solution.py:290
  18.4 0.7 %fusion.10 = (s32[3,3]{0,1:T(4,128)}, s32[3,3]{0,1:T(4,128)}, s32[3,3]{0,1:T(4,128)S(1)}) fusion(s32[3,1]{0,1:T(1,128)S(1)} %get-tuple-element.48, s32[3,1]{0,1:T(1,128)S(1)} %get-tuple-element.43, s32[3]{0:T(128)S(1)} %pad.7.clone, s32[3,1]{0,1:T(1,128)S(1)} %get-tuple-element.44, s32[3,1]{0,1:T(1,128)S(1)} %get-tuple-element.50, ...), kind=kLoop, calls=%fused_computation.28 | loop fusion | flops 45 | bytes 180 | tf_op jit(solution)/shard_map/stack | solution.py:292
  19.0 0.7 %copy.10 = s32[3,3]{1,0:T(4,128)S(1)} copy(s32[3,3]{0,1:T(4,128)} %get-tuple-element.41) | data formatting | bytes 72 | tf_op jit(solution)/shard_map/stack | solution.py:292
  20.4 0.8 %copy.9 = s32[3,3]{1,0:T(4,128)S(1)} copy(s32[3,3]{0,1:T(4,128)} %get-tuple-element.42) | data formatting | bytes 72 | tf_op jit(solution)/shard_map/stack | solution.py:292
  21.1 0.7 %reshape.164 = s32[9]{0:T(128)} reshape(s32[3,3]{1,0:T(4,128)S(1)} %copy.9) | data formatting | bytes 72 | tf_op jit(solution)/shard_map/reshape | solution.py:292
  21.9 0.7 %reshape.163 = s32[9]{0:T(128)} reshape(s32[3,3]{1,0:T(4,128)S(1)} %copy.8) | data formatting | bytes 72 | tf_op jit(solution)/shard_map/reshape | solution.py:292
  22.5 0.7 %concatenate.10.cross = s32[36]{0:T(128)S(1)} concatenate(s32[1]{0:T(128)} %constant.69.clone.1, s32[1]{0:T(128)} %constant.70.clone.1, s32[1]{0:T(128)} %bitcast.1, s32[9]{0:T(128)} %reshape.163, s32[1]{0:T(128)} %constant.76.clone.1, s32[1]{0:T(128)} %constant.77.clone.1, s32[1]{0:T(128)} %bitcast.6, s32[9]{0:T(128)} %reshape.164, s32[1]{0:T(128)} %constant.76.clone.1, ...), dimensions={0} | concatenate | bytes 288 | tf_op jit(solution)/shard_map/concatenate | solution.py:295
  23.3 2.4 %middle.1 = (f32[12,128,128]{2,1,0:T(8,128)S(1)}, f32[12,128,128]{2,1,0:T(8,128)S(1)}, f32[12,128,128]{2,1,0:T(8,128)S(1)}, bf16[6,128,128]{2,1,0:T(8,128)(2,1)S(1)}, bf16[6,128,128]{2,1,0:T(8,128)(2,1)S(1)}) custom-call(s32[28]{0:T(128)S(1)} %concatenate.11.pos, s32[9]{0:T(128)S(1)} %pad_add_fusion.3.lists, s32[36]{0:T(128)S(1)} %concatenate.10.cross, ...), custom_call_target="tpu_custom_call" | custom-call | flops 805306368 | bytes 4194304 | tf_op jit(solution)/shard_map/middle/pallas_call | solution.py:355
  25.8 2.4 %collective-permute-start.3 = (bf16[6,128,128]{2,1,0:T(8,128)(2,1)S(1)}, bf16[6,128,128]{2,1,0:T(8,128)(2,1)S(1)}, u32[]{:S(2)}, u32[]{:S(2)}) collective-permute-start(bf16[6,128,128]{2,1,0:T(8,128)(2,1)S(1)} %get-tuple-element.24), channel_id=1, source_target_pairs={{0,15},{1,2},{2,1},{3,4},{4,3},{5,6},{6,5},{7,8},{8,7},{9,10},{10,... | collective-permute-start | bytes 589832 | tf_op jit(solution)/shard_map/ppermute | solution.py:309
  28.2 5.5 %collective-permute-done.3.recv_b = bf16[6,128,128]{2,1,0:T(8,128)(2,1)S(1)} collective-permute-done((bf16[6,128,128]{2,1,0:T(8,128)(2,1)S(1)}, bf16[6,128,128]{2,1,0:T(8,128)(2,1)S(1)}, u32[]{:S(2)}, u32[]{:S(2)}) %collective-permute-start.3) | collective-permute-done | bytes 196640 | tf_op jit(solution)/shard_map/ppermute | solution.py:309
  33.7 1.7 %last.1 = (f32[12,128,128]{2,1,0:T(8,128)S(1)}, f32[12,128,128]{2,1,0:T(8,128)S(1)}, bf16[3,128,128]{2,1,0:T(8,128)(2,1)S(1)}) custom-call(s32[28]{0:T(128)S(1)} %concatenate.11.pos, s32[9]{0:T(128)S(1)} %pad_add_fusion.3.lists, s32[36]{0:T(128)S(1)} %concatenate.10.cross, bf16[12,4,128,128]{3,2,1,0:T(8,128)(2,1)S(1)} %copy-done.1, ...), custom_call_target="tpu_custom_call" | custom-call | flops 805306368 | bytes 4194304 | tf_op jit(solution)/shard_map/last/pallas_call | solution.py:366
  35.5 2.3 %collective-permute-start.4 = (bf16[3,128,128]{2,1,0:T(8,128)(2,1)S(1)}, bf16[3,128,128]{2,1,0:T(8,128)(2,1)S(1)}, u32[]{:S(2)}, u32[]{:S(2)}) collective-permute-start(bf16[3,128,128]{2,1,0:T(8,128)(2,1)S(1)} %get-tuple-element.26), channel_id=1, source_target_pairs={{0,15},{1,0},{2,1},{3,2},{4,3},{5,4},{6,5},{7,6},{8,7},{9,8},{10,9... | collective-permute-start | bytes 294920 | tf_op jit(solution)/shard_map/ppermute | solution.py:376
  37.8 2.6 %gram.1 = f32[16,128]{1,0:T(8,128)S(1)} custom-call(s32[28]{0:T(128)S(1)} %concatenate.11.pos, bf16[12,4,128,128]{3,2,1,0:T(8,128)(2,1)S(1)} %copy-done.1, f32[12,128,128]{2,1,0:T(8,128)S(1)} %get-tuple-element.17.t.t0, f32[12,128,128]{2,1,0:T(8,128)S(1)} %get-tuple-element.27.t1, f32[12,128,128]{2,1,0:T(8,128)S(1)} %get-tuple-element.21.t.t2, ...), custom_call_target="tpu_custom_call" | custom-call | flops 402653184 | bytes 4194304 | tf_op jit(solution)/shard_map/gram/pallas_call | solution.py:377
  40.4 0.7 %cross.1 = f32[16,16,128]{2,1,0:T(8,128)S(1)} custom-call(s32[9]{0:T(128)S(1)} %pad_add_fusion.3.lists, s32[36]{0:T(128)S(1)} %concatenate.10.cross, bf16[12,4,128,128]{3,2,1,0:T(8,128)(2,1)S(1)} %copy-done.1, f32[12,128,128]{2,1,0:T(8,128)S(1)} %get-tuple-element.25.t4, bf16[3,128,128]{2,1,0:T(8,128)(2,1)S(1)} %collective-permute-done.4.recv, ...), custom_call_target="tpu_custom_call" | custom-call | tf_op jit(solution)/shard_map/cross/pallas_call | solution.py:387
  41.2 13.2 %all_to_all.5.parts = f32[16,16,128]{2,1,0:T(8,128)S(1)} all-to-all(f32[16,16,128]{2,1,0:T(8,128)S(1)} %cross.1), channel_id=1, replica_groups=mesh['region'=2,'dom'=16] {'dom'}, dimensions={0} | all-to-all | bytes 262144 | tf_op jit(solution)/shard_map/all_to_all | solution.py:395
  54.4 1.3 %final.1 = f32[1536,128]{1,0:T(8,128)} custom-call(f32[16,16,128]{2,1,0:T(8,128)S(1)} %all_to_all.5.parts, f32[12,128,128]{2,1,0:T(8,128)S(1)} %get-tuple-element.17.t.t0, f32[12,128,128]{2,1,0:T(8,128)S(1)} %get-tuple-element.27.t1, f32[12,128,128]{2,1,0:T(8,128)S(1)} %get-tuple-element.21.t.t2, f32[12,128,128]{2,1,0:T(8,128)S(1)} %get-tuple-element.28.t3, ...), custom_call_target="tpu_custom_call" | custom-call | tf_op jit(solution)/shard_map/final/pallas_call | solution.py:396
  (32 shorter events, 2.4 us)
Async XLA Ops:
  3.1 1.4 %copy-start = (bf16[12,4,128,128]{3,2,1,0:T(8,128)(2,1)S(1)}, bf16[12,4,128,128]{3,2,1,0:T(8,128)(2,1)}, u32[]{:S(2)}) copy-start(bf16[12,4,128,128]{3,2,1,0:T(8,128)(2,1)} %aff.9) | copy-start | bytes 4718596
  4.6 1.7 %copy-start.2 = (bf16[1536,768]{1,0:T(8,128)(2,1)S(1)}, bf16[1536,768]{1,0:T(8,128)(2,1)}, u32[]{:S(2)}) copy-start(bf16[1536,768]{1,0:T(8,128)(2,1)} %desc.1) | copy-start | bytes 7077892
  6.2 0.9 %copy-start.3 = (bf16[128,768]{1,0:T(8,128)(2,1)S(1)}, bf16[128,768]{1,0:T(8,128)(2,1)}, u32[]{:S(2)}) copy-start(bf16[128,768]{1,0:T(8,128)(2,1)} %queries.1) | copy-start | bytes 589828
  7.2 16.2 %copy-start.1 = (bf16[12,4,128,128]{3,2,1,0:T(8,128)(2,1)S(1)}, bf16[12,4,128,128]{3,2,1,0:T(8,128)(2,1)}, u32[]{:S(2)}) copy-start(bf16[12,4,128,128]{3,2,1,0:T(8,128)(2,1)} %aff.9) | copy-start | bytes 4718596
  11.4 11.9 %collective-permute-start = (bf16[6,128,128]{2,1,0:T(8,128)(2,1)}, bf16[6,128,128]{2,1,0:T(8,128)(2,1)S(1)}, u32[]{:S(2)}, u32[]{:S(2)}) collective-permute-start(bf16[6,128,128]{2,1,0:T(8,128)(2,1)} %get-tuple-element.19), channel_id=1, source_target_pairs={{0,1},{1,0},{2,3},{3,2},{4,5},{5,4},{6,7},{7,6},{8,9},{9,8},{10,11... | collective-permute-start | bytes 589832 | tf_op jit(solution)/shard_map/ppermute | solution.py:310
  12.0 11.3 %collective-permute-start.1 = (bf16[6,128,128]{2,1,0:T(8,128)(2,1)}, bf16[6,128,128]{2,1,0:T(8,128)(2,1)S(1)}, u32[]{:S(2)}, u32[]{:S(2)}) collective-permute-start(bf16[6,128,128]{2,1,0:T(8,128)(2,1)} %get-tuple-element.20), channel_id=1, source_target_pairs={{0,15},{1,2},{2,1},{3,4},{4,3},{5,6},{6,5},{7,8},{8,7},{9,10},{10,... | collective-permute-start | bytes 589832 | tf_op jit(solution)/shard_map/ppermute | solution.py:309
  25.8 2.4 %collective-permute-start.2 = (bf16[6,128,128]{2,1,0:T(8,128)(2,1)S(1)}, bf16[6,128,128]{2,1,0:T(8,128)(2,1)S(1)}, u32[]{:S(2)}, u32[]{:S(2)}) collective-permute-start(bf16[6,128,128]{2,1,0:T(8,128)(2,1)S(1)} %get-tuple-element.23), channel_id=1, source_target_pairs={{0,1},{1,0},{2,3},{3,2},{4,5},{5,4},{6,7},{7,6},{8,9},{9,8},{10,11... | collective-permute-start | bytes 589832 | tf_op jit(solution)/shard_map/ppermute | solution.py:310
  25.8 7.9 %collective-permute-start.3 = (bf16[6,128,128]{2,1,0:T(8,128)(2,1)S(1)}, bf16[6,128,128]{2,1,0:T(8,128)(2,1)S(1)}, u32[]{:S(2)}, u32[]{:S(2)}) collective-permute-start(bf16[6,128,128]{2,1,0:T(8,128)(2,1)S(1)} %get-tuple-element.24), channel_id=1, source_target_pairs={{0,15},{1,2},{2,1},{3,4},{4,3},{5,6},{6,5},{7,8},{8,7},{9,10},{10,... | collective-permute-start | bytes 589832 | tf_op jit(solution)/shard_map/ppermute | solution.py:309
  35.5 5.0 %collective-permute-start.4 = (bf16[3,128,128]{2,1,0:T(8,128)(2,1)S(1)}, bf16[3,128,128]{2,1,0:T(8,128)(2,1)S(1)}, u32[]{:S(2)}, u32[]{:S(2)}) collective-permute-start(bf16[3,128,128]{2,1,0:T(8,128)(2,1)S(1)} %get-tuple-element.26), channel_id=1, source_target_pairs={{0,15},{1,0},{2,1},{3,2},{4,3},{5,4},{6,5},{7,6},{8,7},{9,8},{10,9... | collective-permute-start | bytes 294920 | tf_op jit(solution)/shard_map/ppermute | solution.py:376

commit v2 on v1

v2 whole, which is shorter than its diff:
```python
import functools

import jax
import jax.numpy as jnp
from jax import lax
from jax.experimental import pallas as pl
from jax.experimental.pallas import tpu as pltpu
from jax.sharding import PartitionSpec as P

HALO_W = 6
NAMED = 3
ITERATIONS = 5
DAMP = 0.99
SHIFTS = (0.0, 1.0, -0.25, 0.5)
PIVOT_MIN = 1e-6
BF = jnp.bfloat16
F32 = jnp.float32
PAIRS = [(i, j) for i in range(ITERATIONS) for j in range(i, ITERATIONS)]
ROWS = len(PAIRS) + 1
ENTRIES = 2 + 2 * NAMED

VMEM = pl.BlockSpec(memory_space=pltpu.VMEM)
SMEM = pl.BlockSpec(memory_space=pltpu.SMEM)
HBM = pl.BlockSpec(memory_space=pltpu.HBM)


def params(mib):
    return pltpu.CompilerParams(vmem_limit_bytes=mib << 20)


def dot(a, b):
    return jnp.dot(a, b, preferred_element_type=F32)


def dot_t(a, b):
    return lax.dot_general(a, b, (((0,), (0,)), ((), ())), preferred_element_type=F32)


def put_split(ref, index, value):
    high = value.astype(BF)
    width = value.shape[-1]
    ref[index, :, :width] = high
    ref[index, :, width:] = (value - high.astype(F32)).astype(BF)


def row_product(aff, tab, base, g, hl):
    count = aff.shape[0]
    width = hl.shape[2] // 2
    lower = hl[g - 1] if g > 0 else hl[tab[base + count]]
    upper = hl[g + 1] if g + 1 < count else hl[tab[base + count + 1]]
    left = jnp.concatenate([aff[g, 0], aff[g, 1]], axis=1)
    right = jnp.concatenate([hl[g], lower], axis=0)
    out = dot(left, right)
    left = jnp.concatenate([aff[g, 2], aff[g, 3]], axis=1)
    right = jnp.concatenate([upper, hl[tab[base + g]]], axis=0)
    out = out + dot(left, right)
    return out[:, :width] + out[:, width:]


def offsets(count):
    full = count + 2
    lists = 2 * full
    cross = lists + 3 * NAMED
    high = cross + 3 * ENTRIES
    return full, lists, cross, high, high + 3 * (1 + NAMED)


def fill_table(tile_col, tab, up_rows, low_rows, axis):
    count = tile_col.shape[1]
    total = count * lax.axis_size(axis)
    me = lax.axis_index(axis)
    even = lax.rem(me, 2) == 0
    full, lists, cross, high, _ = offsets(count)
    zero = count + 2 * NAMED
    up_base = jnp.where(even, 0, NAMED)
    low_base = NAMED - up_base
    relative, ups, lows = [], [], []
    up_mask = jnp.int32(1)
    low_mask = jnp.int32(1 << (HALO_W - 1))
    for g in range(count):
        rel = tile_col[3, g] - me * count
        rel = jnp.where(rel < 0, rel + total, rel)
        up = (rel >= count) & (rel < count + HALO_W)
        low = rel >= total - HALO_W
        place = jnp.where(up, rel - count, rel - (total - HALO_W))
        place = jnp.clip(place, 0, HALO_W - 1)
        bit = lax.shift_left(jnp.int32(1), place)
        up_mask = up_mask | jnp.where(up, bit, 0)
        low_mask = low_mask | jnp.where(low, bit, 0)
        relative.append((rel, place, bit))
        ups.append(up)
        lows.append(low)
    up_count = low_count = up_cross = low_cross = jnp.int32(0)
    for g in range(count):
        rel, place, bit = relative[g]
        below = jnp.where(ups[g], up_mask, low_mask) & (bit - 1)
        rank = below & 1
        for p in range(1, HALO_W - 1):
            rank = rank + (lax.shift_right_logical(below, jnp.int32(p)) & 1)
        halo = jnp.where(ups[g], up_base, low_base) + jnp.minimum(rank, NAMED - 1)
        local = rel < count
        tab[g] = jnp.where(local, rel, zero)
        tab[full + g] = jnp.where(local, rel, count + halo)
        up_rows[0, up_count] = g
        low_rows[0, low_count] = g
        up_rows[1, up_cross] = g
        low_rows[1, low_cross] = g
        up_rows[2, up_cross] = halo
        low_rows[2, low_cross] = halo
        up_cross = up_cross + jnp.where(ups[g], 1, 0)
        low_cross = low_cross + jnp.where(lows[g], 1, 0)
        up_count = up_count + (1 if g == count - 1 else jnp.where(ups[g], 1, 0))
        low_count = low_count + (1 if g == 0 else jnp.where(lows[g], 1, 0))
    tab[count] = zero
    tab[count + 1] = zero
    tab[full + count] = count + low_base + NAMED - 1
    tab[full + count + 1] = count + up_base
    for j in range(NAMED):
        up, low = up_rows[0, j], low_rows[0, j]
        tab[lists + j] = jnp.where(even, up, low)
        tab[lists + NAMED + j] = jnp.where(even, low, up)
        tab[lists + 2 * NAMED + j] = low
    chains = ((0, 1, low_base + NAMED - 1), (count - 1, 2, up_base))
    for side, (rows, used) in enumerate(((low_rows, low_cross), (up_rows, up_cross))):
        for i in range(3):
            tab[cross + 3 * side * (1 + NAMED) + i] = jnp.int32(chains[side][i])
        for j in range(NAMED):
            at = cross + 3 * (side * (1 + NAMED) + 1 + j)
            tab[at] = jnp.where(j < used, rows[1, j], count)
            tab[at + 1] = jnp.int32(3)
            tab[at + 2] = jnp.where(j < used, rows[2, j], 2 * NAMED)
    for j in range(1 + NAMED):
        at = cross + 3 * (1 + NAMED + j)
        tab[high + 3 * j] = tab[at]
        tab[high + 3 * j + 1] = tab[at + 1]
        tab[high + 3 * j + 2] = tab[at + 2] - up_base


def pack(tab, shift, t, y, send, base):
    for j in range(NAMED):
        g = tab[base + j]
        value = t[g]
        send[j] = value.astype(BF)
        send[NAMED + j] = (y[g] - shift * value).astype(BF)


def first_kernel(
    desc, queries, affinity, tile_col, t0, y0, send_a, send_b, aff, tab,
    hl, buf, wide, tall, cols, up_rows, low_rows, sems, *, chunks, axis,
):
    count, rows = t0.shape[0], t0.shape[1]
    per = count // chunks
    _, lists, _, _, _ = offsets(count)
    load_q = pltpu.make_async_copy(queries, wide, sems.at[chunks])
    load_c = pltpu.make_async_copy(tile_col, cols, sems.at[chunks + 1])
    load_q.start()
    load_c.start()
    copies = []
    for c in range(chunks):
        copy = pltpu.make_async_copy(
            desc.at[pl.ds(c * per * rows, per * rows)], buf.at[c], sems.at[c]
        )
        copy.start()
        copies.append(copy)
    load_a = pltpu.make_async_copy(affinity, aff, sems.at[chunks + 2])
    load_a.start()
    hl[count + 2 * NAMED] = jnp.zeros(hl.shape[1:], BF)
    load_q.wait()
    tall[...] = wide[...].T
    load_c.wait()
    fill_table(cols, tab, up_rows, low_rows, axis)
    for c in range(chunks):
        copies[c].wait()
        value = jnp.maximum(dot(buf[c], tall[...]), 0.0)
        value = value * value * value
        for i in range(per):
            block = value[i * rows : (i + 1) * rows]
            t0[c * per + i] = block
            put_split(hl, c * per + i, block)
    load_a.wait()
    for g in range(count):
        y0[g] = row_product(aff, tab, 0, g, hl)
    pack(tab, SHIFTS[0], t0, y0, send_b, lists + NAMED)
    pack(tab, SHIFTS[0], t0, y0, send_a, lists)


def two_steps(tab, aff, t, y, recv_a, recv_b, t1, t2, hl, hl2, acc, hacc, step):
    count, width = t.shape[0], t.shape[2]
    full, _, cross, _, _ = offsets(count)
    zero = count + 2 * NAMED
    hl[zero] = jnp.zeros(hl.shape[1:], BF)
    hl2[zero] = jnp.zeros(hl.shape[1:], BF)
    for h in range(NAMED):
        hl[count + h, :, :width] = recv_a[h]
        hl[count + NAMED + h, :, :width] = recv_b[h]
        hacc[h] = recv_a[NAMED + h].astype(F32)
        hacc[NAMED + h] = recv_b[NAMED + h].astype(F32)
    for g in range(count):
        acc[g] = y[g] - SHIFTS[step] * t[g]
    for e in range(ENTRIES):
        g, slot, h = (tab[cross + 3 * e + i] for i in range(3))
        row = jnp.minimum(g, count - 1)
        tile = aff[row, slot]
        acc[g] += dot(tile, hl[count + h, :, :width])
        hacc[h] += dot_t(tile, t[row].astype(BF))
    for g in range(count):
        value = acc[g]
        t1[g] = value
        put_split(hl, g, value)
    for h in range(2 * NAMED):
        put_split(hl, count + h, hacc[h])
    for g in range(count):
        value = row_product(aff, tab, full, g, hl) - SHIFTS[step + 1] * t1[g]
        t2[g] = value
        put_split(hl2, g, value)


def middle_kernel(
    tab, aff, t, y, recv_a, recv_b, t1, t2, y2, send_a, send_b, hl, hl2, acc, hacc
):
    _, lists, _, _, _ = offsets(t.shape[0])
    two_steps(tab, aff, t, y, recv_a, recv_b, t1, t2, hl, hl2, acc, hacc, 0)
    for g in range(t.shape[0]):
        y2[g] = row_product(aff, tab, 0, g, hl2)
    pack(tab, SHIFTS[2], t2, y2, send_b, lists + NAMED)
    pack(tab, SHIFTS[2], t2, y2, send_a, lists)


def last_kernel(tab, aff, t, y, recv_a, recv_b, t3, t4, send, hl, hl2, acc, hacc):
    _, lists, _, _, _ = offsets(t.shape[0])
    two_steps(tab, aff, t, y, recv_a, recv_b, t3, t4, hl, hl2, acc, hacc, 2)
    for j in range(NAMED):
        send[j] = t4[tab[lists + 2 * NAMED + j]].astype(BF)


def gram_kernel(tab, aff, t0, t1, t2, t3, t4, out, hl):
    count, rows, width = t0.shape
    hl[count + 2 * NAMED] = jnp.zeros(hl.shape[1:], BF)
    for g in range(count):
        put_split(hl, g, t4[g])
    fields = (t0, t1, t2, t3, t4)
    sums = [jnp.zeros((8, width), F32) for _ in range(ROWS)]
    for g in range(count):
        local = row_product(aff, tab, 0, g, hl)
        sums[-1] = sums[-1] + (t4[g] * local).reshape(rows // 8, 8, width).sum(0)

    def body(i, sums):
        sums = list(sums)
        g = i // (rows // 32)
        start = pl.multiple_of((i % (rows // 32)) * 32, 32)
        for part in range(4):
            v = [f[g, pl.ds(pl.multiple_of(start + 8 * part, 8), 8), :] for f in fields]
            for n, (a, b) in enumerate(PAIRS):
                sums[n] = sums[n] + v[a] * v[b]
        return tuple(sums)

    sums = lax.fori_loop(0, count * rows // 32, body, tuple(sums))
    for n in range(ROWS):
        out[pl.ds(n, 1), :] = jnp.sum(sums[n], axis=0, keepdims=True)


def cross_kernel(tab, aff, t4, recv, gram, out):
    count = t4.shape[0]
    _, _, _, high, _ = offsets(count)
    total = jnp.zeros((8, gram.shape[1]), F32)
    for e in range(1 + NAMED):
        g, slot, h = (tab[high + 3 * e + i] for i in range(3))
        row = jnp.minimum(g, count - 1)
        part = t4[row] * dot(aff[row, slot], recv[jnp.minimum(h, NAMED - 1)])
        part = part.reshape(-1, 8, part.shape[-1]).sum(0)
        total = total + jnp.where(g < count, part, 0.0)
    value = gram[...]
    extra = 2.0 * jnp.sum(total, axis=0, keepdims=True)
    index = lax.broadcasted_iota(jnp.int32, value.shape, 0)
    value = value + jnp.where(index == ROWS - 1, extra, 0.0)
    for d in range(out.shape[0]):
        out[d] = value


def final_kernel(parts, t0, t1, t2, t3, t4, out):
    n = ITERATIONS
    value = parts[0]
    for d in range(1, parts.shape[0]):
        value = value + parts[d]
    gram = {}
    for k, (i, j) in enumerate(PAIRS):
        gram[i, j] = gram[j, i] = value[k : k + 1]
    matrix = {}
    for i in range(n):
        for j in range(i, n):
            terms = []
            if j + 1 < n:
                terms.append(gram[i, j + 1] + SHIFTS[j] * gram[i, j])
            if i + 1 < n and i != j:
                terms.append(gram[i + 1, j] + SHIFTS[i] * gram[i, j])
            if not terms:
                terms = [value[ROWS - 1 : ROWS]]
            product = terms[0] if len(terms) == 1 else 0.5 * (terms[0] + terms[1])
            matrix[i, j] = gram[i, j] - DAMP * product
    scale = [
        jnp.where(matrix[i, i] > 0.0, lax.rsqrt(jnp.maximum(matrix[i, i], 1e-37)), 0.0)
        for i in range(n)
    ]
    for i in range(n):
        for j in range(i, n):
            matrix[i, j] = matrix[i, j] * (scale[i] * scale[j])
    right = [gram[i, 0] * scale[i] for i in range(n)]
    inverse = []
    for k in range(n):
        pivot = matrix[k, k]
        inverse.append(jnp.where(pivot > PIVOT_MIN, 1.0 / jnp.maximum(pivot, PIVOT_MIN), 0.0))
        for i in range(k + 1, n):
            factor = matrix[k, i] * inverse[k]
            for j in range(i, n):
                matrix[i, j] = matrix[i, j] - factor * matrix[k, j]
            right[i] = right[i] - factor * right[k]
    coef = [None] * n
    for k in range(n - 1, -1, -1):
        rest = right[k]
        for j in range(k + 1, n):
            rest = rest - matrix[k, j] * coef[j]
        coef[k] = rest * inverse[k]
    coef = [coef[k] * scale[k] for k in range(n)]
    fields = (t0, t1, t2, t3, t4)
    count, rows, width = t0.shape
    wide = [jnp.broadcast_to(c, (8, width)) for c in coef]
    for g in range(count):
        total = None
        for f, c in zip(fields, coef):
            term = f[g] * c
            total = term if total is None else total + term
        out[pl.ds(g * rows, rows), :] = total


def swap(block_a, block_b, axis):
    n = lax.axis_size(axis)
    pairs_a = [(i, i ^ 1) for i in range(n)]
    pairs_b = [(i, (i + 1) % n if i % 2 else (i - 1) % n) for i in range(n)]
    got_b = lax.ppermute(block_b, axis, pairs_b)
    got_a = lax.ppermute(block_a, axis, pairs_a)
    return got_a, got_b


def shards(descriptors, queries, affinity, tile_col):
    count, _, rows, _ = affinity.shape
    width = queries.shape[0]
    depth = descriptors.shape[1]
    axis = "dom"
    devices = lax.axis_size(axis)
    size = 128 * pl.cdiv(offsets(count)[-1], 128)
    blocks = count + 2 * NAMED + 1
    field = jax.ShapeDtypeStruct((count, rows, width), F32)
    edge = jax.ShapeDtypeStruct((2 * NAMED, rows, width), BF)
    half = jax.ShapeDtypeStruct((NAMED, rows, width), BF)
    split = pltpu.VMEM((blocks, rows, 2 * width), BF)
    work = [
        split,
        split,
        pltpu.VMEM((count + 1, rows, width), F32),
        pltpu.VMEM((2 * NAMED + 1, rows, width), F32),
    ]
    chunks = 4
    flops = 2 * count * rows * 4 * rows * 2 * width

    def cost(products, extra=0, bytes_accessed=4 << 20):
        return pl.CostEstimate(
            flops=products * flops + extra, bytes_accessed=bytes_accessed, transcendentals=0
        )

    t0, y0, send_a, send_b, aff, tab = pl.pallas_call(
        functools.partial(first_kernel, chunks=chunks, axis=axis),
        out_shape=(
            field,
            field,
            edge,
            edge,
            jax.ShapeDtypeStruct(affinity.shape, BF),
            jax.ShapeDtypeStruct((size,), jnp.int32),
        ),
        in_specs=[HBM] * 4,
        out_specs=(VMEM,) * 5 + (SMEM,),
        scratch_shapes=[
            split,
            pltpu.VMEM((chunks, count * rows // chunks, depth), BF),
            pltpu.VMEM((width, depth), BF),
            pltpu.VMEM((depth, width), BF),
            pltpu.SMEM((4, count), jnp.int32),
            pltpu.SMEM((3, count + 1), jnp.int32),
            pltpu.SMEM((3, count + 1), jnp.int32),
            pltpu.SemaphoreType.DMA((chunks + 3,)),
        ],
        compiler_params=params(24),
        cost_estimate=cost(1, 2 * count * rows * depth * width),
        name="first",
    )(descriptors, queries, affinity, tile_col.T)
    recv_a, recv_b = swap(send_a, send_b, axis)
    t1, t2, y2, send_a, send_b = pl.pallas_call(
        middle_kernel,
        out_shape=(field, field, field, edge, edge),
        in_specs=[SMEM] + [VMEM] * 5,
        out_specs=(VMEM,) * 5,
        scratch_shapes=work,
        compiler_params=params(24),
        cost_estimate=cost(2),
        name="middle",
    )(tab, aff, t0, y0, recv_a, recv_b)
    recv_a, recv_b = swap(send_a, send_b, axis)
    t3, t4, send = pl.pallas_call(
        last_kernel,
        out_shape=(field, field, half),
        in_specs=[SMEM] + [VMEM] * 5,
        out_specs=(VMEM,) * 3,
        scratch_shapes=work,
        compiler_params=params(24),
        cost_estimate=cost(2),
        name="last",
    )(tab, aff, t2, y2, recv_a, recv_b)
    recv = lax.ppermute(send, axis, [(i, (i - 1) % devices) for i in range(devices)])
    gram = pl.pallas_call(
        gram_kernel,
        out_shape=jax.ShapeDtypeStruct((ROWS, width), F32),
        in_specs=[SMEM] + [VMEM] * 6,
        out_specs=VMEM,
        scratch_shapes=[split],
        compiler_params=params(24),
        cost_estimate=cost(1),
        name="gram",
    )(tab, aff, t0, t1, t2, t3, t4)
    parts = pl.pallas_call(
        cross_kernel,
        out_shape=jax.ShapeDtypeStruct((devices, ROWS, width), F32),
        in_specs=[SMEM] + [VMEM] * 4,
        out_specs=VMEM,
        compiler_params=params(8),
        name="cross",
    )(tab, aff, t4, recv, gram)
    parts = lax.all_to_all(parts, axis, 0, 0)
    return pl.pallas_call(
        final_kernel,
        out_shape=jax.ShapeDtypeStruct((count * rows, width), F32),
        in_specs=[VMEM] * 6,
        out_specs=VMEM,
        compiler_params=params(24),
        name="final",
    )(parts, t0, t1, t2, t3, t4)


def solution(mesh):
    return jax.shard_map(
        shards,
        mesh=mesh,
        in_specs=(
            P(("region", "dom"), None),
            P("region", None),
            P(("region", "dom"), None, None, None),
            P(("region", "dom"), None),
        ),
        out_specs=P(("region", "dom"), None),
        check_vma=False,
    )
```

time: 56 us -> 53.5 us (0.955)
  other arithmetic: 4.36 us -> 0 us
  starting transfers between devices: 11 us -> 15.3 us
  local copies, waits for them, and re-layouts: 8.42 us -> 4.68 us
  waiting for transfers between devices: 5.53 us -> 6.73 us
    ppermute x2, starting transfers between devices: 8.01 us -> 10.2 us  [swap(): got_b = lax.ppermute(block_b, axis, pairs_b)]
    ppermute x1, starting transfers between devices: 2.33 us -> 4.48 us  [shards(): lax.ppermute(send, axis, [(i, (i - 1) % devices) for i in range(devices)])]
    reshape x3 -> x0, local copies, waits for them, and re-layouts: 1.93 us -> none  [entries(): rest = jnp.stack([rows, 3 + 0 * rows, ranks], 1).reshape(-1)]
    another operation x4 -> x0, local copies, waits for them, and re-layouts: 1.66 us -> none  [entries(): rest = jnp.stack([rows, 3 + 0 * rows, ranks], 1).reshape(-1)]
    select_n x5 -> x0, other arithmetic: 1.4 us -> none  [the longest x1 0.71 us: tables(): pos_full = jnp.where(local, relative, count + halo)]
    reduce_sum x6 -> x0, other arithmetic: 1.26 us -> none  [the longest x1 0.7 us: members(): return (jnp.sum(jnp.where(hit, blocks[None] + 1, 0), 1) - 1, hit)]
    ppermute x2, waiting for transfers between devices: 5.52 us -> 6.72 us  [swap(): got_b = lax.ppermute(block_b, axis, pairs_b)]
    concatenate x2 -> x0, local copies, waits for them, and re-layouts: 0.83 us -> none  [the longest x1 0.75 us: tables(): jnp.concatenate([entries(low, low_rank, low_base, 0, 1, NAMED - 1), entri...]
  transfers between devices with their start and end apart: 5 -> 5, of which waited for: 1 -> 2; matrix products, arithmetic and copies ran while one was open for 10% -> 0% of each run, Pallas kernels for 5% -> 5%
where the time goes in v2:
time: 53.5 us; the launch traced here: 53.2 us
  starting transfers between devices  15.3 us (29%)
  Pallas kernels  13.4 us (25%)
  blocking collectives  13.2 us (25%)
  waiting for transfers between devices  6.73 us (13%)
  local copies, waits for them, and re-layouts  4.68 us (9%)
    all_to_all x1, blocking collectives, shards(): parts = lax.all_to_all(parts, axis, 0, 0)  13.2 us
    ppermute x2, starting transfers between devices, swap(): got_b = lax.ppermute(block_b, axis, pairs_b)  10.2 us
    ppermute x2, waiting for transfers between devices, swap(): got_b = lax.ppermute(block_b, axis, pairs_b)  6.72 us
    unnamed x8, local copies, waits for them, and re-layouts  4.68 us
    ppermute x1, starting transfers between devices, shards(): lax.ppermute(send, axis, [(i, (i - 1) % devices) for i in range(devices)])  4.48 us
    pallas_call x1, Pallas kernels, shards(): pl.pallas_call(functools.partial(first_kernel, chunks=chunks, axis=axis),...  4.32 us
    pallas_call x1, Pallas kernels, shards(): pl.pallas_call(gram_kernel, out_shape=jax.ShapeDtypeStruct((ROWS, width),...  2.65 us
    pallas_call x1, Pallas kernels, shards(): pl.pallas_call(middle_kernel, out_shape=(field, field, field, edge, edge)...  2.52 us
  transfers between devices with their start and end apart: 5, of which 2 were waited for; matrix products, arithmetic and copies ran while one was open for 0% of the time, Pallas kernels for 5%

profile of v2, /device:TPU:0, one launch (start us, length us, event | category | flops | bytes accessed | tf_op | source)
XLA Modules:
  0.0 53.2 jit_solution(17810742964918860750)
XLA Ops:
  0.0 0.0 copy-start
  0.0 1.7 %copy-done = bf16[1536,768]{1,0:T(8,128)(2,1)S(1)} copy-done((bf16[1536,768]{1,0:T(8,128)(2,1)S(1)}, bf16[1536,768]{1,0:T(8,128)(2,1)}, u32[]{:S(2)}) %copy-start) | copy-done | bytes 2359320
  1.7 1.4 %copy-done.1 = bf16[12,4,128,128]{3,2,1,0:T(8,128)(2,1)S(1)} copy-done((bf16[12,4,128,128]{3,2,1,0:T(8,128)(2,1)S(1)}, bf16[12,4,128,128]{3,2,1,0:T(8,128)(2,1)}, u32[]{:S(2)}) %copy-start.1) | copy-done | bytes 1572888
  3.1 0.0 copy-start.2
  3.1 0.9 %copy-done.2 = bf16[128,768]{1,0:T(8,128)(2,1)S(1)} copy-done((bf16[128,768]{1,0:T(8,128)(2,1)S(1)}, bf16[128,768]{1,0:T(8,128)(2,1)}, u32[]{:S(2)}) %copy-start.2) | copy-done | bytes 196632
  4.0 0.0 copy-start.3
  4.0 0.7 %copy-done.3 = s32[12,4]{0,1:T(4,128)S(1)} copy-done((s32[12,4]{0,1:T(4,128)S(1)}, s32[12,4]{0,1:T(4,128)}, u32[]{:S(2)}) %copy-start.3) | copy-done | bytes 216
  4.7 4.3 %first.1 = (f32[12,128,128]{2,1,0:T(8,128)S(1)}, f32[12,128,128]{2,1,0:T(8,128)S(1)}, bf16[6,128,128]{2,1,0:T(8,128)(2,1)S(1)}, bf16[6,128,128]{2,1,0:T(8,128)(2...) custom-call(bf16[1536,768]{1,0:T(8,128)(2,1)S(1)} %copy-done, bf16[128,768]{1,0:T(8,128)(2,1)S(1)} %copy-done.2, ...), custom_call_target="tpu_custom_call" | custom-call | flops 704643072 | bytes 4194304 | tf_op jit(solution)/shard_map/first/pallas_call | solution.py:370
  9.0 0.6 %collective-permute-start = (bf16[6,128,128]{2,1,0:T(8,128)(2,1)S(1)}, bf16[6,128,128]{2,1,0:T(8,128)(2,1)S(1)}, u32[]{:S(2)}, u32[]{:S(2)}) collective-permute-start(bf16[6,128,128]{2,1,0:T(8,128)(2,1)S(1)} %get-tuple-element.23), channel_id=1, source_target_pairs={{0,1},{1,0},{2,3},{3,2},{4,5},{5,4},{6,7},{7,6},{8,9},{9,8},{10,11... | collective-permute-start | bytes 589832 | tf_op jit(solution)/shard_map/ppermute | solution.py:340
  9.6 5.7 %collective-permute-start.1 = (bf16[6,128,128]{2,1,0:T(8,128)(2,1)S(1)}, bf16[6,128,128]{2,1,0:T(8,128)(2,1)S(1)}, u32[]{:S(2)}, u32[]{:S(2)}) collective-permute-start(bf16[6,128,128]{2,1,0:T(8,128)(2,1)S(1)} %get-tuple-element.24), channel_id=1, source_target_pairs={{0,15},{1,2},{2,1},{3,4},{4,3},{5,6},{6,5},{7,8},{8,7},{9,10},{10,... | collective-permute-start | bytes 589832 | tf_op jit(solution)/shard_map/ppermute | solution.py:339
  15.2 0.0 collective-permute-done.recv_a
  15.2 3.3 %collective-permute-done.1.recv_b = bf16[6,128,128]{2,1,0:T(8,128)(2,1)S(1)} collective-permute-done((bf16[6,128,128]{2,1,0:T(8,128)(2,1)S(1)}, bf16[6,128,128]{2,1,0:T(8,128)(2,1)S(1)}, u32[]{:S(2)}, u32[]{:S(2)}) %collective-permute-start.1) | collective-permute-done | bytes 196640 | tf_op jit(solution)/shard_map/ppermute | solution.py:339
  18.6 2.5 %middle.1 = (f32[12,128,128]{2,1,0:T(8,128)S(1)}, f32[12,128,128]{2,1,0:T(8,128)S(1)}, f32[12,128,128]{2,1,0:T(8,128)S(1)}, bf16[6,128,128]{2,1,0:T(8,128)(2,1)S(1)}, bf16[6,128,128]{2,1,0:T(8,128)(2,1)S(1)}) custom-call(s32[128]{0:T(128)S(1)} %get-tuple-element.19.tab, bf16[12,4,128,128]{3,2,1,0:T(8,128)(2,1)S(1)} %get-tuple-element.20.aff, ...), custom_call_target="tpu_custom_call" | custom-call | flops 805306368 | bytes 4194304 | tf_op jit(solution)/shard_map/middle/pallas_call | solution.py:397
  21.1 0.1 collective-permute-start.2
  21.2 4.5 %collective-permute-start.3 = (bf16[6,128,128]{2,1,0:T(8,128)(2,1)S(1)}, bf16[6,128,128]{2,1,0:T(8,128)(2,1)S(1)}, u32[]{:S(2)}, u32[]{:S(2)}) collective-permute-start(bf16[6,128,128]{2,1,0:T(8,128)(2,1)S(1)} %get-tuple-element.28), channel_id=1, source_target_pairs={{0,15},{1,2},{2,1},{3,4},{4,3},{5,6},{6,5},{7,8},{8,7},{9,10},{10,... | collective-permute-start | bytes 589832 | tf_op jit(solution)/shard_map/ppermute | solution.py:339
  25.7 0.0 collective-permute-done.2.recv_a
  25.7 3.4 %collective-permute-done.3.recv_b = bf16[6,128,128]{2,1,0:T(8,128)(2,1)S(1)} collective-permute-done((bf16[6,128,128]{2,1,0:T(8,128)(2,1)S(1)}, bf16[6,128,128]{2,1,0:T(8,128)(2,1)S(1)}, u32[]{:S(2)}, u32[]{:S(2)}) %collective-permute-start.3) | collective-permute-done | bytes 196640 | tf_op jit(solution)/shard_map/ppermute | solution.py:339
  29.1 1.8 %last.1 = (f32[12,128,128]{2,1,0:T(8,128)S(1)}, f32[12,128,128]{2,1,0:T(8,128)S(1)}, bf16[3,128,128]{2,1,0:T(8,128)(2,1)S(1)}) custom-call(s32[128]{0:T(128)S(1)} %get-tuple-element.19.tab, bf16[12,4,128,128]{3,2,1,0:T(8,128)(2,1)S(1)} %get-tuple-element.20.aff, f32[12,128,128]{2,1,0:T(8,128)S(1)} %get-tuple-element.25.t.t2, ...), custom_call_target="tpu_custom_call" | custom-call | flops 805306368 | bytes 4194304 | tf_op jit(solution)/shard_map/last/pallas_call | solution.py:408
  30.9 4.5 %collective-permute-start.4 = (bf16[3,128,128]{2,1,0:T(8,128)(2,1)S(1)}, bf16[3,128,128]{2,1,0:T(8,128)(2,1)S(1)}, u32[]{:S(2)}, u32[]{:S(2)}) collective-permute-start(bf16[3,128,128]{2,1,0:T(8,128)(2,1)S(1)} %get-tuple-element.30), channel_id=1, source_target_pairs={{0,15},{1,0},{2,1},{3,2},{4,3},{5,4},{6,5},{7,6},{8,7},{9,8},{10,9... | collective-permute-start | bytes 294920 | tf_op jit(solution)/shard_map/ppermute | solution.py:418
  35.3 2.7 %gram.1 = f32[16,128]{1,0:T(8,128)S(1)} custom-call(s32[128]{0:T(128)S(1)} %get-tuple-element.19.tab, bf16[12,4,128,128]{3,2,1,0:T(8,128)(2,1)S(1)} %get-tuple-element.20.aff, f32[12,128,128]{2,1,0:T(8,128)S(1)} %get-tuple-element.21.t.t0, f32[12,128,128]{2,1,0:T(8,128)S(1)} %get-tuple-element.31.t1, f32[12,128,128]{2,1,0:T(8,128)S(1)} %get-tuple-element.25.t.t2, ...), custom_call_target="tpu_custom_call" | custom-call | flops 402653184 | bytes 4194304 | tf_op jit(solution)/shard_map/gram/pallas_call | solution.py:419
  38.0 0.0 collective-permute-done.4.recv
  38.0 0.7 %cross.1 = f32[16,16,128]{2,1,0:T(8,128)S(1)} custom-call(s32[128]{0:T(128)S(1)} %get-tuple-element.19.tab, bf16[12,4,128,128]{3,2,1,0:T(8,128)(2,1)S(1)} %get-tuple-element.20.aff, f32[12,128,128]{2,1,0:T(8,128)S(1)} %get-tuple-element.29.t4, bf16[3,128,128]{2,1,0:T(8,128)(2,1)S(1)} %collective-permute-done.4.recv, f32[16,128]{1,0:T(8,128)S(1)} %gram.1), custom_call_target="tpu_custom_call" | custom-call | tf_op jit(solution)/shard_map/cross/pallas_call | solution.py:429
  38.7 13.2 %all_to_all.5.parts = f32[16,16,128]{2,1,0:T(8,128)S(1)} all-to-all(f32[16,16,128]{2,1,0:T(8,128)S(1)} %cross.1), channel_id=1, replica_groups=mesh['region'=2,'dom'=16] {'dom'}, dimensions={0} | all-to-all | bytes 262144 | tf_op jit(solution)/shard_map/all_to_all | solution.py:437
  51.9 1.3 %final.1 = f32[1536,128]{1,0:T(8,128)} custom-call(f32[16,16,128]{2,1,0:T(8,128)S(1)} %all_to_all.5.parts, f32[12,128,128]{2,1,0:T(8,128)S(1)} %get-tuple-element.21.t.t0, f32[12,128,128]{2,1,0:T(8,128)S(1)} %get-tuple-element.31.t1, f32[12,128,128]{2,1,0:T(8,128)S(1)} %get-tuple-element.25.t.t2, f32[12,128,128]{2,1,0:T(8,128)S(1)} %get-tuple-element.32.t3, ...), custom_call_target="tpu_custom_call" | custom-call | tf_op jit(solution)/shard_map/final/pallas_call | solution.py:438
  (1 shorter events, 0.0 us)
Async XLA Ops:
  0.0 1.7 %copy-start = (bf16[1536,768]{1,0:T(8,128)(2,1)S(1)}, bf16[1536,768]{1,0:T(8,128)(2,1)}, u32[]{:S(2)}) copy-start(bf16[1536,768]{1,0:T(8,128)(2,1)} %desc.1) | copy-start | bytes 7077892
  1.7 1.4 %copy-start.1 = (bf16[12,4,128,128]{3,2,1,0:T(8,128)(2,1)S(1)}, bf16[12,4,128,128]{3,2,1,0:T(8,128)(2,1)}, u32[]{:S(2)}) copy-start(bf16[12,4,128,128]{3,2,1,0:T(8,128)(2,1)} %affinity.1) | copy-start | bytes 4718596
  3.1 0.9 %copy-start.2 = (bf16[128,768]{1,0:T(8,128)(2,1)S(1)}, bf16[128,768]{1,0:T(8,128)(2,1)}, u32[]{:S(2)}) copy-start(bf16[128,768]{1,0:T(8,128)(2,1)} %queries.1) | copy-start | bytes 589828
  4.0 0.7 %copy-start.3 = (s32[12,4]{0,1:T(4,128)S(1)}, s32[12,4]{0,1:T(4,128)}, u32[]{:S(2)}) copy-start(s32[12,4]{0,1:T(4,128)} %param.7) | copy-start | bytes 580
  9.0 6.2 %collective-permute-start = (bf16[6,128,128]{2,1,0:T(8,128)(2,1)S(1)}, bf16[6,128,128]{2,1,0:T(8,128)(2,1)S(1)}, u32[]{:S(2)}, u32[]{:S(2)}) collective-permute-start(bf16[6,128,128]{2,1,0:T(8,128)(2,1)S(1)} %get-tuple-element.23), channel_id=1, source_target_pairs={{0,1},{1,0},{2,3},{3,2},{4,5},{5,4},{6,7},{7,6},{8,9},{9,8},{10,11... | collective-permute-start | bytes 589832 | tf_op jit(solution)/shard_map/ppermute | solution.py:340
  9.6 9.0 %collective-permute-start.1 = (bf16[6,128,128]{2,1,0:T(8,128)(2,1)S(1)}, bf16[6,128,128]{2,1,0:T(8,128)(2,1)S(1)}, u32[]{:S(2)}, u32[]{:S(2)}) collective-permute-start(bf16[6,128,128]{2,1,0:T(8,128)(2,1)S(1)} %get-tuple-element.24), channel_id=1, source_target_pairs={{0,15},{1,2},{2,1},{3,4},{4,3},{5,6},{6,5},{7,8},{8,7},{9,10},{10,... | collective-permute-start | bytes 589832 | tf_op jit(solution)/shard_map/ppermute | solution.py:339
  21.1 4.6 %collective-permute-start.2 = (bf16[6,128,128]{2,1,0:T(8,128)(2,1)S(1)}, bf16[6,128,128]{2,1,0:T(8,128)(2,1)S(1)}, u32[]{:S(2)}, u32[]{:S(2)}) collective-permute-start(bf16[6,128,128]{2,1,0:T(8,128)(2,1)S(1)} %get-tuple-element.27), channel_id=1, source_target_pairs={{0,1},{1,0},{2,3},{3,2},{4,5},{5,4},{6,7},{7,6},{8,9},{9,8},{10,11... | collective-permute-start | bytes 589832 | tf_op jit(solution)/shard_map/ppermute | solution.py:340
  21.2 7.9 %collective-permute-start.3 = (bf16[6,128,128]{2,1,0:T(8,128)(2,1)S(1)}, bf16[6,128,128]{2,1,0:T(8,128)(2,1)S(1)}, u32[]{:S(2)}, u32[]{:S(2)}) collective-permute-start(bf16[6,128,128]{2,1,0:T(8,128)(2,1)S(1)} %get-tuple-element.28), channel_id=1, source_target_pairs={{0,15},{1,2},{2,1},{3,4},{4,3},{5,6},{6,5},{7,8},{8,7},{9,10},{10,... | collective-permute-start | bytes 589832 | tf_op jit(solution)/shard_map/ppermute | solution.py:339
  30.9 7.1 %collective-permute-start.4 = (bf16[3,128,128]{2,1,0:T(8,128)(2,1)S(1)}, bf16[3,128,128]{2,1,0:T(8,128)(2,1)S(1)}, u32[]{:S(2)}, u32[]{:S(2)}) collective-permute-start(bf16[3,128,128]{2,1,0:T(8,128)(2,1)S(1)} %get-tuple-element.30), channel_id=1, source_target_pairs={{0,15},{1,0},{2,1},{3,2},{4,3},{5,4},{6,5},{7,6},{8,7},{9,8},{10,9... | collective-permute-start | bytes 294920 | tf_op jit(solution)/shard_map/ppermute | solution.py:418

commit v3 on v2

--- a/solution.py
+++ b/solution.py
@@ -392,7 +392,7 @@
         compiler_params=params(24),
         cost_estimate=cost(1, 2 * count * rows * depth * width),
         name="first",
-    )(descriptors, queries, affinity, tile_col.T)
+    )(*(pltpu.with_memory_space_constraint(x, pltpu.HBM) for x in (descriptors, queries, affinity, tile_col.T)))
     recv_a, recv_b = swap(send_a, send_b, axis)
     t1, t2, y2, send_a, send_b = pl.pallas_call(
         middle_kernel,

time: 53.5 us -> 48.6 us (0.908)
  local copies, waits for them, and re-layouts: 4.68 us -> 0 us
    unnamed x8 -> x0, local copies, waits for them, and re-layouts: 4.68 us -> none
where the time goes in v3:
time: 48.6 us; the launch traced here: 48.4 us
  starting transfers between devices  15.2 us (31%)
  Pallas kernels  13.2 us (27%)
  blocking collectives  13.2 us (27%)
  waiting for transfers between devices  6.74 us (14%)
    all_to_all x1, blocking collectives, shards(): parts = lax.all_to_all(parts, axis, 0, 0)  13.2 us
    ppermute x2, starting transfers between devices, swap(): got_b = lax.ppermute(block_b, axis, pairs_b)  10.2 us
    ppermute x2, waiting for transfers between devices, swap(): got_b = lax.ppermute(block_b, axis, pairs_b)  6.73 us
    ppermute x1, starting transfers between devices, shards(): lax.ppermute(send, axis, [(i, (i - 1) % devices) for i in range(devices)])  4.45 us
    pallas_call x1, Pallas kernels, shards(): pl.pallas_call(functools.partial(first_kernel, chunks=chunks, axis=axis),...  4.4 us
    pallas_call x1, Pallas kernels, shards(): pl.pallas_call(gram_kernel, out_shape=jax.ShapeDtypeStruct((ROWS, width),...  2.62 us
    pallas_call x1, Pallas kernels, shards(): pl.pallas_call(middle_kernel, out_shape=(field, field, field, edge, edge)...  2.43 us
    pallas_call x1, Pallas kernels, shards(): pl.pallas_call(last_kernel, out_shape=(field, field, half), in_specs=[SME...  1.75 us
  transfers between devices with their start and end apart: 5, of which 2 were waited for; matrix products, arithmetic and copies ran while one was open for 0% of the time, Pallas kernels for 5%

profile of v3, /device:TPU:0, one launch (start us, length us, event | category | flops | bytes accessed | tf_op | source)
XLA Modules:
  0.0 48.4 jit_solution(1186893433031633047)
XLA Ops:
  0.0 4.4 %first.1 = (f32[12,128,128]{2,1,0:T(8,128)S(1)}, f32[12,128,128]{2,1,0:T(8,128)S(1)}, bf16[6,128,128]{2,1,0:T(8,128)(2,1)S(1)}, bf16[6,128,128]{2,1,0:T(8,128)(2...) custom-call(bf16[1536,768]{1,0:T(8,128)(2,1)} %desc.1, bf16[128,768]{1,0:T(8,128)(2,1)} %queries.1, ...), custom_call_target="tpu_custom_call" | custom-call | flops 704643072 | bytes 4194304 | tf_op jit(solution)/shard_map/first/pallas_call | solution.py:370
  4.4 0.6 %collective-permute-start = (bf16[6,128,128]{2,1,0:T(8,128)(2,1)S(1)}, bf16[6,128,128]{2,1,0:T(8,128)(2,1)S(1)}, u32[]{:S(2)}, u32[]{:S(2)}) collective-permute-start(bf16[6,128,128]{2,1,0:T(8,128)(2,1)S(1)} %get-tuple-element.23), channel_id=1, source_target_pairs={{0,1},{1,0},{2,3},{3,2},{4,5},{5,4},{6,7},{7,6},{8,9},{9,8},{10,11... | collective-permute-start | bytes 589832 | tf_op jit(solution)/shard_map/ppermute | solution.py:340
  5.0 5.7 %collective-permute-start.1 = (bf16[6,128,128]{2,1,0:T(8,128)(2,1)S(1)}, bf16[6,128,128]{2,1,0:T(8,128)(2,1)S(1)}, u32[]{:S(2)}, u32[]{:S(2)}) collective-permute-start(bf16[6,128,128]{2,1,0:T(8,128)(2,1)S(1)} %get-tuple-element.24), channel_id=1, source_target_pairs={{0,15},{1,2},{2,1},{3,4},{4,3},{5,6},{6,5},{7,8},{8,7},{9,10},{10,... | collective-permute-start | bytes 589832 | tf_op jit(solution)/shard_map/ppermute | solution.py:339
  10.6 0.0 collective-permute-done.recv_a
  10.6 3.3 %collective-permute-done.1.recv_b = bf16[6,128,128]{2,1,0:T(8,128)(2,1)S(1)} collective-permute-done((bf16[6,128,128]{2,1,0:T(8,128)(2,1)S(1)}, bf16[6,128,128]{2,1,0:T(8,128)(2,1)S(1)}, u32[]{:S(2)}, u32[]{:S(2)}) %collective-permute-start.1) | collective-permute-done | bytes 196640 | tf_op jit(solution)/shard_map/ppermute | solution.py:339
  14.0 2.4 %middle.1 = (f32[12,128,128]{2,1,0:T(8,128)S(1)}, f32[12,128,128]{2,1,0:T(8,128)S(1)}, f32[12,128,128]{2,1,0:T(8,128)S(1)}, bf16[6,128,128]{2,1,0:T(8,128)(2,1)S(1)}, bf16[6,128,128]{2,1,0:T(8,128)(2,1)S(1)}) custom-call(s32[128]{0:T(128)S(1)} %get-tuple-element.19.tab, bf16[12,4,128,128]{3,2,1,0:T(8,128)(2,1)S(1)} %get-tuple-element.20.aff, ...), custom_call_target="tpu_custom_call" | custom-call | flops 805306368 | bytes 4194304 | tf_op jit(solution)/shard_map/middle/pallas_call | solution.py:397
  16.4 0.1 collective-permute-start.2
  16.5 4.5 %collective-permute-start.3 = (bf16[6,128,128]{2,1,0:T(8,128)(2,1)S(1)}, bf16[6,128,128]{2,1,0:T(8,128)(2,1)S(1)}, u32[]{:S(2)}, u32[]{:S(2)}) collective-permute-start(bf16[6,128,128]{2,1,0:T(8,128)(2,1)S(1)} %get-tuple-element.28), channel_id=1, source_target_pairs={{0,15},{1,2},{2,1},{3,4},{4,3},{5,6},{6,5},{7,8},{8,7},{9,10},{10,... | collective-permute-start | bytes 589832 | tf_op jit(solution)/shard_map/ppermute | solution.py:339
  21.0 0.0 collective-permute-done.2.recv_a
  21.0 3.4 %collective-permute-done.3.recv_b = bf16[6,128,128]{2,1,0:T(8,128)(2,1)S(1)} collective-permute-done((bf16[6,128,128]{2,1,0:T(8,128)(2,1)S(1)}, bf16[6,128,128]{2,1,0:T(8,128)(2,1)S(1)}, u32[]{:S(2)}, u32[]{:S(2)}) %collective-permute-start.3) | collective-permute-done | bytes 196640 | tf_op jit(solution)/shard_map/ppermute | solution.py:339
  24.4 1.8 %last.1 = (f32[12,128,128]{2,1,0:T(8,128)S(1)}, f32[12,128,128]{2,1,0:T(8,128)S(1)}, bf16[3,128,128]{2,1,0:T(8,128)(2,1)S(1)}) custom-call(s32[128]{0:T(128)S(1)} %get-tuple-element.19.tab, bf16[12,4,128,128]{3,2,1,0:T(8,128)(2,1)S(1)} %get-tuple-element.20.aff, f32[12,128,128]{2,1,0:T(8,128)S(1)} %get-tuple-element.25.t.t2, ...), custom_call_target="tpu_custom_call" | custom-call | flops 805306368 | bytes 4194304 | tf_op jit(solution)/shard_map/last/pallas_call | solution.py:408
  26.1 4.5 %collective-permute-start.4 = (bf16[3,128,128]{2,1,0:T(8,128)(2,1)S(1)}, bf16[3,128,128]{2,1,0:T(8,128)(2,1)S(1)}, u32[]{:S(2)}, u32[]{:S(2)}) collective-permute-start(bf16[3,128,128]{2,1,0:T(8,128)(2,1)S(1)} %get-tuple-element.30), channel_id=1, source_target_pairs={{0,15},{1,0},{2,1},{3,2},{4,3},{5,4},{6,5},{7,6},{8,7},{9,8},{10,9... | collective-permute-start | bytes 294920 | tf_op jit(solution)/shard_map/ppermute | solution.py:418
  30.6 2.6 %gram.1 = f32[16,128]{1,0:T(8,128)S(1)} custom-call(s32[128]{0:T(128)S(1)} %get-tuple-element.19.tab, bf16[12,4,128,128]{3,2,1,0:T(8,128)(2,1)S(1)} %get-tuple-element.20.aff, f32[12,128,128]{2,1,0:T(8,128)S(1)} %get-tuple-element.21.t.t0, f32[12,128,128]{2,1,0:T(8,128)S(1)} %get-tuple-element.31.t1, f32[12,128,128]{2,1,0:T(8,128)S(1)} %get-tuple-element.25.t.t2, ...), custom_call_target="tpu_custom_call" | custom-call | flops 402653184 | bytes 4194304 | tf_op jit(solution)/shard_map/gram/pallas_call | solution.py:419
  33.2 0.0 collective-permute-done.4.recv
  33.2 0.7 %cross.1 = f32[16,16,128]{2,1,0:T(8,128)S(1)} custom-call(s32[128]{0:T(128)S(1)} %get-tuple-element.19.tab, bf16[12,4,128,128]{3,2,1,0:T(8,128)(2,1)S(1)} %get-tuple-element.20.aff, f32[12,128,128]{2,1,0:T(8,128)S(1)} %get-tuple-element.29.t4, bf16[3,128,128]{2,1,0:T(8,128)(2,1)S(1)} %collective-permute-done.4.recv, f32[16,128]{1,0:T(8,128)S(1)} %gram.1), custom_call_target="tpu_custom_call" | custom-call | tf_op jit(solution)/shard_map/cross/pallas_call | solution.py:429
  34.0 13.2 %all_to_all.5.parts = f32[16,16,128]{2,1,0:T(8,128)S(1)} all-to-all(f32[16,16,128]{2,1,0:T(8,128)S(1)} %cross.1), channel_id=1, replica_groups=mesh['region'=2,'dom'=16] {'dom'}, dimensions={0} | all-to-all | bytes 262144 | tf_op jit(solution)/shard_map/all_to_all | solution.py:437
  47.2 1.3 %final.1 = f32[1536,128]{1,0:T(8,128)} custom-call(f32[16,16,128]{2,1,0:T(8,128)S(1)} %all_to_all.5.parts, f32[12,128,128]{2,1,0:T(8,128)S(1)} %get-tuple-element.21.t.t0, f32[12,128,128]{2,1,0:T(8,128)S(1)} %get-tuple-element.31.t1, f32[12,128,128]{2,1,0:T(8,128)S(1)} %get-tuple-element.25.t.t2, f32[12,128,128]{2,1,0:T(8,128)S(1)} %get-tuple-element.32.t3, ...), custom_call_target="tpu_custom_call" | custom-call | tf_op jit(solution)/shard_map/final/pallas_call | solution.py:438
Async XLA Ops:
  4.4 6.2 %collective-permute-start = (bf16[6,128,128]{2,1,0:T(8,128)(2,1)S(1)}, bf16[6,128,128]{2,1,0:T(8,128)(2,1)S(1)}, u32[]{:S(2)}, u32[]{:S(2)}) collective-permute-start(bf16[6,128,128]{2,1,0:T(8,128)(2,1)S(1)} %get-tuple-element.23), channel_id=1, source_target_pairs={{0,1},{1,0},{2,3},{3,2},{4,5},{5,4},{6,7},{7,6},{8,9},{9,8},{10,11... | collective-permute-start | bytes 589832 | tf_op jit(solution)/shard_map/ppermute | solution.py:340
  5.0 9.0 %collective-permute-start.1 = (bf16[6,128,128]{2,1,0:T(8,128)(2,1)S(1)}, bf16[6,128,128]{2,1,0:T(8,128)(2,1)S(1)}, u32[]{:S(2)}, u32[]{:S(2)}) collective-permute-start(bf16[6,128,128]{2,1,0:T(8,128)(2,1)S(1)} %get-tuple-element.24), channel_id=1, source_target_pairs={{0,15},{1,2},{2,1},{3,4},{4,3},{5,6},{6,5},{7,8},{8,7},{9,10},{10,... | collective-permute-start | bytes 589832 | tf_op jit(solution)/shard_map/ppermute | solution.py:339
  16.4 4.6 %collective-permute-start.2 = (bf16[6,128,128]{2,1,0:T(8,128)(2,1)S(1)}, bf16[6,128,128]{2,1,0:T(8,128)(2,1)S(1)}, u32[]{:S(2)}, u32[]{:S(2)}) collective-permute-start(bf16[6,128,128]{2,1,0:T(8,128)(2,1)S(1)} %get-tuple-element.27), channel_id=1, source_target_pairs={{0,1},{1,0},{2,3},{3,2},{4,5},{5,4},{6,7},{7,6},{8,9},{9,8},{10,11... | collective-permute-start | bytes 589832 | tf_op jit(solution)/shard_map/ppermute | solution.py:340
  16.5 7.9 %collective-permute-start.3 = (bf16[6,128,128]{2,1,0:T(8,128)(2,1)S(1)}, bf16[6,128,128]{2,1,0:T(8,128)(2,1)S(1)}, u32[]{:S(2)}, u32[]{:S(2)}) collective-permute-start(bf16[6,128,128]{2,1,0:T(8,128)(2,1)S(1)} %get-tuple-element.28), channel_id=1, source_target_pairs={{0,15},{1,2},{2,1},{3,4},{4,3},{5,6},{6,5},{7,8},{8,7},{9,10},{10,... | collective-permute-start | bytes 589832 | tf_op jit(solution)/shard_map/ppermute | solution.py:339
  26.1 7.1 %collective-permute-start.4 = (bf16[3,128,128]{2,1,0:T(8,128)(2,1)S(1)}, bf16[3,128,128]{2,1,0:T(8,128)(2,1)S(1)}, u32[]{:S(2)}, u32[]{:S(2)}) collective-permute-start(bf16[3,128,128]{2,1,0:T(8,128)(2,1)S(1)} %get-tuple-element.30), channel_id=1, source_target_pairs={{0,15},{1,0},{2,1},{3,2},{4,3},{5,4},{6,5},{7,6},{8,7},{9,8},{10,9... | collective-permute-start | bytes 294920 | tf_op jit(solution)/shard_map/ppermute | solution.py:418

commit v4 on v3

--- a/solution.py
+++ b/solution.py
@@ -15,7 +15,9 @@
 PIVOT_MIN = 1e-6
 BF = jnp.bfloat16
 F32 = jnp.float32
-PAIRS = [(i, j) for i in range(ITERATIONS) for j in range(i, ITERATIONS)]
+EARLY = [(i, j) for i in range(3) for j in range(i, 3)]
+LATE = [(i, j) for j in range(3, ITERATIONS) for i in range(j + 1)]
+PAIRS = EARLY + LATE
 ROWS = len(PAIRS) + 1
 ENTRIES = 2 + 2 * NAMED
 
@@ -46,15 +48,23 @@
 def row_product(aff, tab, base, g, hl):
     count = aff.shape[0]
     width = hl.shape[2] // 2
-    lower = hl[g - 1] if g > 0 else hl[tab[base + count]]
-    upper = hl[g + 1] if g + 1 < count else hl[tab[base + count + 1]]
+    if isinstance(g, int):
+        low = g - 1 if g > 0 else tab[base + count]
+        high = g + 1 if g + 1 < count else tab[base + count + 1]
+    else:
+        low = jnp.where(g > 0, g - 1, tab[base + count])
+        high = jnp.where(g + 1 < count, g + 1, tab[base + count + 1])
     left = jnp.concatenate([aff[g, 0], aff[g, 1]], axis=1)
-    right = jnp.concatenate([hl[g], lower], axis=0)
+    right = jnp.concatenate([hl[g], hl[low]], axis=0)
     out = dot(left, right)
     left = jnp.concatenate([aff[g, 2], aff[g, 3]], axis=1)
-    right = jnp.concatenate([upper, hl[tab[base + g]]], axis=0)
+    right = jnp.concatenate([hl[high], hl[tab[base + g]]], axis=0)
     out = out + dot(left, right)
     return out[:, :width] + out[:, width:]
+
+
+def shifted(value, shift, t):
+    return value if shift == 0.0 else value - shift * t
 
 
 def offsets(count):
@@ -126,27 +136,27 @@
             tab[cross + 3 * side * (1 + NAMED) + i] = jnp.int32(chains[side][i])
         for j in range(NAMED):
             at = cross + 3 * (side * (1 + NAMED) + 1 + j)
-            tab[at] = jnp.where(j < used, rows[1, j], count)
+            tab[at] = jnp.where(j < used, rows[1, j], 0)
             tab[at + 1] = jnp.int32(3)
             tab[at + 2] = jnp.where(j < used, rows[2, j], 2 * NAMED)
     for j in range(1 + NAMED):
         at = cross + 3 * (1 + NAMED + j)
         tab[high + 3 * j] = tab[at]
         tab[high + 3 * j + 1] = tab[at + 1]
-        tab[high + 3 * j + 2] = tab[at + 2] - up_base
-
-
-def pack(tab, shift, t, y, send, base):
+        tab[high + 3 * j + 2] = jnp.where(tab[at + 2] < 2 * NAMED, tab[at + 2] - up_base, NAMED)
+
+
+def pack(tab, shift, aff, t, hl, send, base):
+    width = t.shape[2]
     for j in range(NAMED):
         g = tab[base + j]
-        value = t[g]
-        send[j] = value.astype(BF)
-        send[NAMED + j] = (y[g] - shift * value).astype(BF)
+        send[j] = hl[g, :, :width]
+        send[NAMED + j] = shifted(row_product(aff, tab, 0, g, hl), shift, t[g]).astype(BF)
 
 
 def first_kernel(
-    desc, queries, affinity, tile_col, t0, y0, send_a, send_b, aff, tab,
-    hl, buf, wide, tall, cols, up_rows, low_rows, sems, *, chunks, axis,
+    desc, queries, affinity, tile_col, t0, hl, send_a, send_b, aff, tab,
+    buf, wide, tall, cols, up_rows, low_rows, sems, *, chunks, axis,
 ):
     count, rows = t0.shape[0], t0.shape[1]
     per = count // chunks
@@ -168,9 +178,10 @@
     load_q.wait()
     tall[...] = wide[...].T
     load_c.wait()
-    fill_table(cols, tab, up_rows, low_rows, axis)
     for c in range(chunks):
         copies[c].wait()
+        if c == 0:
+            fill_table(cols, tab, up_rows, low_rows, axis)
         value = jnp.maximum(dot(buf[c], tall[...]), 0.0)
         value = value * value * value
         for i in range(per):
@@ -178,85 +189,100 @@
             t0[c * per + i] = block
             put_split(hl, c * per + i, block)
     load_a.wait()
-    for g in range(count):
-        y0[g] = row_product(aff, tab, 0, g, hl)
-    pack(tab, SHIFTS[0], t0, y0, send_b, lists + NAMED)
-    pack(tab, SHIFTS[0], t0, y0, send_a, lists)
-
-
-def two_steps(tab, aff, t, y, recv_a, recv_b, t1, t2, hl, hl2, acc, hacc, step):
-    count, width = t.shape[0], t.shape[2]
-    full, _, cross, _, _ = offsets(count)
-    zero = count + 2 * NAMED
-    hl[zero] = jnp.zeros(hl.shape[1:], BF)
-    hl2[zero] = jnp.zeros(hl.shape[1:], BF)
+    pack(tab, SHIFTS[0], aff, t0, hl, send_b, lists + NAMED)
+    pack(tab, SHIFTS[0], aff, t0, hl, send_a, lists)
+
+
+def add_products(sums, pairs, fields):
+    count, rows, _ = fields[0].shape
+    group = 32
+
+    def body(i, sums):
+        sums = list(sums)
+        g = i // (rows // group)
+        start = (i % (rows // group)) * group
+        for part in range(group // 8):
+            at = pl.ds(pl.multiple_of(start + 8 * part, 8), 8)
+            v = [f[g, at, :] for f in fields]
+            for n, (a, b) in enumerate(pairs):
+                sums[n] = sums[n] + v[a] * v[b]
+        return tuple(sums)
+
+    return list(lax.fori_loop(0, count * rows // group, body, tuple(sums)))
+
+
+def rest_kernel(tab, aff, t, hl, *refs, step):
+    count = t.shape[0]
+    fields, (part, hl_next, *gram) = refs[: 2 * (step > 0)], refs[2 * (step > 0) :]
+    hl_next[count + 2 * NAMED] = jnp.zeros(hl.shape[1:], BF)
+    for g in range(count):
+        value = shifted(row_product(aff, tab, 0, g, hl), SHIFTS[step], t[g])
+        part[g] = value
+        put_split(hl_next, g, value)
+    if gram:
+        width = t.shape[2]
+        sums = [jnp.zeros((8, width), F32) for _ in EARLY]
+        sums = add_products(sums, EARLY, (*fields, t))
+        for n, total in enumerate(sums):
+            gram[0][pl.ds(n, 1), :] = jnp.sum(total, axis=0, keepdims=True)
+
+
+def two_steps(tab, aff, hl, hl1, t1, recv_a, recv_b, t2, hl2, halo, hacc, step):
+    count, _, width = t2.shape
+    full, lists, cross, _, _ = offsets(count)
+    halo[2 * NAMED] = jnp.zeros(halo.shape[1:], BF)
+    hacc[2 * NAMED] = jnp.zeros(hacc.shape[1:], F32)
     for h in range(NAMED):
-        hl[count + h, :, :width] = recv_a[h]
-        hl[count + NAMED + h, :, :width] = recv_b[h]
+        halo[h] = recv_a[h]
+        halo[NAMED + h] = recv_b[h]
         hacc[h] = recv_a[NAMED + h].astype(F32)
         hacc[NAMED + h] = recv_b[NAMED + h].astype(F32)
-    for g in range(count):
-        acc[g] = y[g] - SHIFTS[step] * t[g]
     for e in range(ENTRIES):
         g, slot, h = (tab[cross + 3 * e + i] for i in range(3))
-        row = jnp.minimum(g, count - 1)
-        tile = aff[row, slot]
-        acc[g] += dot(tile, hl[count + h, :, :width])
-        hacc[h] += dot_t(tile, t[row].astype(BF))
-    for g in range(count):
-        value = acc[g]
-        t1[g] = value
-        put_split(hl, g, value)
+        tile = aff[g, slot]
+        t1[g] += dot(tile, halo[h])
+        hacc[h] += dot_t(tile, hl[g, :, :width])
+    for j in range(2 * NAMED):
+        g = tab[lists + j]
+        put_split(hl1, g, t1[g])
     for h in range(2 * NAMED):
-        put_split(hl, count + h, hacc[h])
-    for g in range(count):
-        value = row_product(aff, tab, full, g, hl) - SHIFTS[step + 1] * t1[g]
+        put_split(hl1, count + h, hacc[h])
+    for g in range(count):
+        value = shifted(row_product(aff, tab, full, g, hl1), SHIFTS[step + 1], t1[g])
         t2[g] = value
         put_split(hl2, g, value)
 
 
 def middle_kernel(
-    tab, aff, t, y, recv_a, recv_b, t1, t2, y2, send_a, send_b, hl, hl2, acc, hacc
+    tab, aff, hl, _, __, recv_a, recv_b, hl1, t1, t2, hl2, send_a, send_b, halo, hacc
 ):
-    _, lists, _, _, _ = offsets(t.shape[0])
-    two_steps(tab, aff, t, y, recv_a, recv_b, t1, t2, hl, hl2, acc, hacc, 0)
-    for g in range(t.shape[0]):
-        y2[g] = row_product(aff, tab, 0, g, hl2)
-    pack(tab, SHIFTS[2], t2, y2, send_b, lists + NAMED)
-    pack(tab, SHIFTS[2], t2, y2, send_a, lists)
-
-
-def last_kernel(tab, aff, t, y, recv_a, recv_b, t3, t4, send, hl, hl2, acc, hacc):
-    _, lists, _, _, _ = offsets(t.shape[0])
-    two_steps(tab, aff, t, y, recv_a, recv_b, t3, t4, hl, hl2, acc, hacc, 2)
+    _, lists, _, _, _ = offsets(t1.shape[0])
+    hl2[t1.shape[0] + 2 * NAMED] = jnp.zeros(hl2.shape[1:], BF)
+    two_steps(tab, aff, hl, hl1, t1, recv_a, recv_b, t2, hl2, halo, hacc, 0)
+    pack(tab, SHIFTS[2], aff, t2, hl2, send_b, lists + NAMED)
+    pack(tab, SHIFTS[2], aff, t2, hl2, send_a, lists)
+
+
+def last_kernel(tab, aff, hl, _, __, recv_a, recv_b, hl3, t3, t4, hl4, send, halo, hacc):
+    count, _, width = t3.shape
+    _, lists, _, _, _ = offsets(count)
+    hl4[count + 2 * NAMED] = jnp.zeros(hl4.shape[1:], BF)
+    two_steps(tab, aff, hl, hl3, t3, recv_a, recv_b, t4, hl4, halo, hacc, 2)
     for j in range(NAMED):
-        send[j] = t4[tab[lists + 2 * NAMED + j]].astype(BF)
-
-
-def gram_kernel(tab, aff, t0, t1, t2, t3, t4, out, hl):
+        send[j] = hl4[tab[lists + 2 * NAMED + j], :, :width]
+
+
+def gram_kernel(tab, aff, t0, t1, t2, t3, t4, hl, early, out):
     count, rows, width = t0.shape
-    hl[count + 2 * NAMED] = jnp.zeros(hl.shape[1:], BF)
-    for g in range(count):
-        put_split(hl, g, t4[g])
-    fields = (t0, t1, t2, t3, t4)
-    sums = [jnp.zeros((8, width), F32) for _ in range(ROWS)]
+    sums = [jnp.zeros((8, width), F32) for _ in LATE]
+    last = jnp.zeros((8, width), F32)
     for g in range(count):
         local = row_product(aff, tab, 0, g, hl)
-        sums[-1] = sums[-1] + (t4[g] * local).reshape(rows // 8, 8, width).sum(0)
-
-    def body(i, sums):
-        sums = list(sums)
-        g = i // (rows // 32)
-        start = pl.multiple_of((i % (rows // 32)) * 32, 32)
-        for part in range(4):
-            v = [f[g, pl.ds(pl.multiple_of(start + 8 * part, 8), 8), :] for f in fields]
-            for n, (a, b) in enumerate(PAIRS):
-                sums[n] = sums[n] + v[a] * v[b]
-        return tuple(sums)
-
-    sums = lax.fori_loop(0, count * rows // 32, body, tuple(sums))
-    for n in range(ROWS):
-        out[pl.ds(n, 1), :] = jnp.sum(sums[n], axis=0, keepdims=True)
+        last = last + (t4[g] * local).reshape(rows // 8, 8, width).sum(0)
+    sums = add_products(sums, LATE, (t0, t1, t2, t3, t4)) + [last]
+    out[pl.ds(0, len(EARLY)), :] = early[...]
+    for n, total in enumerate(sums):
+        out[pl.ds(len(EARLY) + n, 1), :] = jnp.sum(total, axis=0, keepdims=True)
 
 
 def cross_kernel(tab, aff, t4, recv, gram, out):
@@ -265,10 +291,9 @@
     total = jnp.zeros((8, gram.shape[1]), F32)
     for e in range(1 + NAMED):
         g, slot, h = (tab[high + 3 * e + i] for i in range(3))
-        row = jnp.minimum(g, count - 1)
-        part = t4[row] * dot(aff[row, slot], recv[jnp.minimum(h, NAMED - 1)])
+        part = t4[g] * dot(aff[g, slot], recv[jnp.minimum(h, NAMED - 1)])
         part = part.reshape(-1, 8, part.shape[-1]).sum(0)
-        total = total + jnp.where(g < count, part, 0.0)
+        total = total + jnp.where(h < NAMED, part, 0.0)
     value = gram[...]
     extra = 2.0 * jnp.sum(total, axis=0, keepdims=True)
     index = lax.broadcasted_iota(jnp.int32, value.shape, 0)
@@ -350,28 +375,44 @@
     size = 128 * pl.cdiv(offsets(count)[-1], 128)
     blocks = count + 2 * NAMED + 1
     field = jax.ShapeDtypeStruct((count, rows, width), F32)
+    split = jax.ShapeDtypeStruct((blocks, rows, 2 * width), BF)
     edge = jax.ShapeDtypeStruct((2 * NAMED, rows, width), BF)
     half = jax.ShapeDtypeStruct((NAMED, rows, width), BF)
-    split = pltpu.VMEM((blocks, rows, 2 * width), BF)
+    early = jax.ShapeDtypeStruct((len(EARLY), width), F32)
     work = [
-        split,
-        split,
-        pltpu.VMEM((count + 1, rows, width), F32),
+        pltpu.VMEM((2 * NAMED + 1, rows, width), BF),
         pltpu.VMEM((2 * NAMED + 1, rows, width), F32),
     ]
-    chunks = 4
+    chunks = count // 2
     flops = 2 * count * rows * 4 * rows * 2 * width
 
-    def cost(products, extra=0, bytes_accessed=4 << 20):
-        return pl.CostEstimate(
-            flops=products * flops + extra, bytes_accessed=bytes_accessed, transcendentals=0
-        )
-
-    t0, y0, send_a, send_b, aff, tab = pl.pallas_call(
+    def call(kernel, out_shape, products, scratch=(), aliases=None, name=None, limit=24):
+        outs = out_shape if isinstance(out_shape, tuple) else (out_shape,)
+
+        def run(*args):
+            specs = [SMEM if x.dtype == jnp.int32 else VMEM for x in args]
+            return pl.pallas_call(
+                kernel,
+                out_shape=out_shape,
+                in_specs=specs,
+                out_specs=(VMEM,) * len(outs) if isinstance(out_shape, tuple) else VMEM,
+                scratch_shapes=list(scratch),
+                input_output_aliases=aliases or {},
+                compiler_params=params(limit),
+                cost_estimate=pl.CostEstimate(
+                    flops=int(products * flops), bytes_accessed=4 << 20, transcendentals=0
+                ),
+                name=name,
+            )(*args)
+
+        return run
+
+    operands = (descriptors, queries, affinity, tile_col.T)
+    t0, hl0, send_a, send_b, aff, tab = pl.pallas_call(
         functools.partial(first_kernel, chunks=chunks, axis=axis),
         out_shape=(
             field,
-            field,
+            split,
             edge,
             edge,
             jax.ShapeDtypeStruct(affinity.shape, BF),
@@ -380,7 +421,6 @@
         in_specs=[HBM] * 4,
         out_specs=(VMEM,) * 5 + (SMEM,),
         scratch_shapes=[
-            split,
             pltpu.VMEM((chunks, count * rows // chunks, depth), BF),
             pltpu.VMEM((width, depth), BF),
             pltpu.VMEM((depth, width), BF),
@@ -390,58 +430,47 @@
             pltpu.SemaphoreType.DMA((chunks + 3,)),
         ],
         compiler_params=params(24),
-        cost_estimate=cost(1, 2 * count * rows * depth * width),
+        cost_estimate=pl.CostEstimate(flops=flops, bytes_accessed=4 << 20, transcendentals=0),
         name="first",
-    )(*(pltpu.with_memory_space_constraint(x, pltpu.HBM) for x in (descriptors, queries, affinity, tile_col.T)))
+    )(*(pltpu.with_memory_space_constraint(x, pltpu.HBM) for x in operands))
     recv_a, recv_b = swap(send_a, send_b, axis)
-    t1, t2, y2, send_a, send_b = pl.pallas_call(
+    part, hl1 = call(
+        functools.partial(rest_kernel, step=0), (field, split), 1, name="rest0"
+    )(tab, aff, t0, hl0)
+    _, t1, t2, hl2, send_a, send_b = call(
         middle_kernel,
-        out_shape=(field, field, field, edge, edge),
-        in_specs=[SMEM] + [VMEM] * 5,
-        out_specs=(VMEM,) * 5,
-        scratch_shapes=work,
-        compiler_params=params(24),
-        cost_estimate=cost(2),
+        (split, field, field, split, edge, edge),
+        2,
+        work,
+        {3: 0, 4: 1},
         name="middle",
-    )(tab, aff, t0, y0, recv_a, recv_b)
+    )(tab, aff, hl0, hl1, part, recv_a, recv_b)
     recv_a, recv_b = swap(send_a, send_b, axis)
-    t3, t4, send = pl.pallas_call(
+    part, hl3, gram = call(
+        functools.partial(rest_kernel, step=2), (field, split, early), 1, name="rest2"
+    )(tab, aff, t2, hl2, t0, t1)
+    _, t3, t4, hl4, send = call(
         last_kernel,
-        out_shape=(field, field, half),
-        in_specs=[SMEM] + [VMEM] * 5,
-        out_specs=(VMEM,) * 3,
-        scratch_shapes=work,
-        compiler_params=params(24),
-        cost_estimate=cost(2),
+        (split, field, field, split, half),
+        2,
+        work,
+        {3: 0, 4: 1},
         name="last",
-    )(tab, aff, t2, y2, recv_a, recv_b)
+    )(tab, aff, hl2, hl3, part, recv_a, recv_b)
     recv = lax.ppermute(send, axis, [(i, (i - 1) % devices) for i in range(devices)])
-    gram = pl.pallas_call(
-        gram_kernel,
-        out_shape=jax.ShapeDtypeStruct((ROWS, width), F32),
-        in_specs=[SMEM] + [VMEM] * 6,
-        out_specs=VMEM,
-        scratch_shapes=[split],
-        compiler_params=params(24),
-        cost_estimate=cost(1),
-        name="gram",
-    )(tab, aff, t0, t1, t2, t3, t4)
-    parts = pl.pallas_call(
+    gram = call(
+        gram_kernel, jax.ShapeDtypeStruct((ROWS, width), F32), 1, name="gram"
+    )(tab, aff, t0, t1, t2, t3, t4, hl4, gram)
+    parts = call(
         cross_kernel,
-        out_shape=jax.ShapeDtypeStruct((devices, ROWS, width), F32),
-        in_specs=[SMEM] + [VMEM] * 4,
-        out_specs=VMEM,
-        compiler_params=params(8),
+        jax.ShapeDtypeStruct((devices, ROWS, width), F32),
+        0.1,
         name="cross",
+        limit=8,
     )(tab, aff, t4, recv, gram)
     parts = lax.all_to_all(parts, axis, 0, 0)
-    return pl.pallas_call(
-        final_kernel,
-        out_shape=jax.ShapeDtypeStruct((count * rows, width), F32),
-        in_specs=[VMEM] * 6,
-        out_specs=VMEM,
-        compiler_params=params(24),
-        name="final",
+    return call(
+        final_kernel, jax.ShapeDtypeStruct((count * rows, width), F32), 0.1, name="final"
     )(parts, t0, t1, t2, t3, t4)
 
 

time: 48.6 us -> 47.3 us (0.973)
  waiting for transfers between devices: 6.74 us -> 3.66 us
  Pallas kernels: 13.2 us -> 14.5 us
    ppermute x2, waiting for transfers between devices: 6.73 us -> 3.63 us  [swap(): got_b = lax.ppermute(block_b, axis, pairs_b)]
    pallas_call x5 -> x7, Pallas kernels: 8.8 us -> 10.8 us  [run(): pl.pallas_call(kernel, out_shape=out_shape, in_specs=specs, out_specs=(VM...]
    pallas_call x1, Pallas kernels: 4.4 us -> 3.72 us  [shards(): pl.pallas_call(functools.partial(first_kernel, chunks=chunks, axis=axis),...]
  transfers between devices with their start and end apart: 5 -> 5, of which waited for: 2 -> 2; matrix products, arithmetic and copies ran while one was open for 0% -> 0% of each run, Pallas kernels for 5% -> 11%
where the time goes in v4:
time: 47.3 us; the launch traced here: 47.1 us
  starting transfers between devices  15.3 us (32%)
  Pallas kernels  14.5 us (31%)
  blocking collectives  13.6 us (29%)
  waiting for transfers between devices  3.66 us (8%)
    all_to_all x1, blocking collectives, shards(): parts = lax.all_to_all(parts, axis, 0, 0)  13.6 us
    pallas_call x7, Pallas kernels, run(): pl.pallas_call(kernel, out_shape=out_shape, in_specs=specs, out_specs=(VM...  10.8 us
    ppermute x2, starting transfers between devices, swap(): got_b = lax.ppermute(block_b, axis, pairs_b)  10.2 us
    ppermute x1, starting transfers between devices, shards(): lax.ppermute(send, axis, [(i, (i - 1) % devices) for i in range(devices)])  4.47 us
    pallas_call x1, Pallas kernels, shards(): pl.pallas_call(functools.partial(first_kernel, chunks=chunks, axis=axis),...  3.72 us
    ppermute x2, waiting for transfers between devices, swap(): got_b = lax.ppermute(block_b, axis, pairs_b)  3.63 us
  transfers between devices with their start and end apart: 5, of which 2 were waited for; matrix products, arithmetic and copies ran while one was open for 0% of the time, Pallas kernels for 11%

profile of v4, /device:TPU:0, one launch (start us, length us, event | category | flops | bytes accessed | tf_op | source)
XLA Modules:
  0.0 47.1 jit_solution(9169542786278988660)
XLA Ops:
  0.0 3.7 %first.1 = (f32[12,128,128]{2,1,0:T(8,128)S(1)}, bf16[19,128,256]{2,1,0:T(8,128)(2,1)S(1)}, bf16[6,128,128]{2,1,0:T(8,128)(2,1)S(1)}, bf16[6,128,128]{2,1,0:T(8,...) custom-call(bf16[1536,768]{1,0:T(8,128)(2,1)} %desc.1, bf16[128,768]{1,0:T(8,128)(2,1)} %queries.1, ...), custom_call_target="tpu_custom_call" | custom-call | flops 402653184 | bytes 4194304 | tf_op jit(solution)/shard_map/first/pallas_call | solution.py:411
  3.7 0.6 %collective-permute-start = (bf16[6,128,128]{2,1,0:T(8,128)(2,1)S(1)}, bf16[6,128,128]{2,1,0:T(8,128)(2,1)S(1)}, u32[]{:S(2)}, u32[]{:S(2)}) collective-permute-start(bf16[6,128,128]{2,1,0:T(8,128)(2,1)S(1)} %get-tuple-element.31), channel_id=1, source_target_pairs={{0,1},{1,0},{2,3},{3,2},{4,5},{5,4},{6,7},{7,6},{8,9},{9,8},{10,11... | collective-permute-start | bytes 589832 | tf_op jit(solution)/shard_map/ppermute | solution.py:365
  4.3 5.7 %collective-permute-start.1 = (bf16[6,128,128]{2,1,0:T(8,128)(2,1)S(1)}, bf16[6,128,128]{2,1,0:T(8,128)(2,1)S(1)}, u32[]{:S(2)}, u32[]{:S(2)}) collective-permute-start(bf16[6,128,128]{2,1,0:T(8,128)(2,1)S(1)} %get-tuple-element.32), channel_id=1, source_target_pairs={{0,15},{1,2},{2,1},{3,4},{4,3},{5,6},{6,5},{7,8},{8,7},{9,10},{10,... | collective-permute-start | bytes 589832 | tf_op jit(solution)/shard_map/ppermute | solution.py:364
  9.9 1.1 %rest0.1 = (f32[12,128,128]{2,1,0:T(8,128)S(1)}, bf16[19,128,256]{2,1,0:T(8,128)(2,1)S(1)}) custom-call(s32[128]{0:T(128)S(1)} %get-tuple-element.25.tab, bf16[12,4,128,128]{3,2,1,0:T(8,128)(2,1)S(1)} %get-tuple-element.26.aff, f32[12,128,128]{2,1,0:T(8,128)S(1)} %get-tuple-element.28.t.refs_0_.t0, bf16[19,128,256]{2,1,0:T(8,128)(2,1)S(1)} %get-tuple-element.27.hl), custom_call_target="tpu_custom_call" | custom-call | flops 402653184 | bytes 4194304 | tf_op jit(solution)/shard_map/rest0/pallas_call | solution.py:394
  11.1 0.0 collective-permute-done.recv_a
  11.1 2.2 %collective-permute-done.1.recv_b = bf16[6,128,128]{2,1,0:T(8,128)(2,1)S(1)} collective-permute-done((bf16[6,128,128]{2,1,0:T(8,128)(2,1)S(1)}, bf16[6,128,128]{2,1,0:T(8,128)(2,1)S(1)}, u32[]{:S(2)}, u32[]{:S(2)}) %collective-permute-start.1) | collective-permute-done | bytes 196640 | tf_op jit(solution)/shard_map/ppermute | solution.py:364
  13.3 2.0 %middle.1 = (bf16[19,128,256]{2,1,0:T(8,128)(2,1)S(1)}, f32[12,128,128]{2,1,0:T(8,128)S(1)}, f32[12,128,128]{2,1,0:T(8,128)S(1)}, bf16[19,128,256]{2,1,0:T(8,128...) custom-call(s32[128]{0:T(128)S(1)} %get-tuple-element.25.tab, ...), custom_call_target="tpu_custom_call", output_to_operand_aliasing={{0}: (3, {}), {1}: (4, {})} | custom-call | flops 805306368 | bytes 4194304 | tf_op jit(solution)/shard_map/middle/pallas_call | solution.py:394
  15.3 0.1 collective-permute-start.2
  15.3 4.5 %collective-permute-start.3 = (bf16[6,128,128]{2,1,0:T(8,128)(2,1)S(1)}, bf16[6,128,128]{2,1,0:T(8,128)(2,1)S(1)}, u32[]{:S(2)}, u32[]{:S(2)}) collective-permute-start(bf16[6,128,128]{2,1,0:T(8,128)(2,1)S(1)} %get-tuple-element.39), channel_id=1, source_target_pairs={{0,15},{1,2},{2,1},{3,4},{4,3},{5,6},{6,5},{7,8},{8,7},{9,10},{10,... | collective-permute-start | bytes 589832 | tf_op jit(solution)/shard_map/ppermute | solution.py:364
  19.8 1.9 %rest2.1 = (f32[12,128,128]{2,1,0:T(8,128)S(1)}, bf16[19,128,256]{2,1,0:T(8,128)(2,1)S(1)}, f32[6,128]{1,0:T(8,128)S(1)}) custom-call(s32[128]{0:T(128)S(1)} %get-tuple-element.25.tab, bf16[12,4,128,128]{3,2,1,0:T(8,128)(2,1)S(1)} %get-tuple-element.26.aff, f32[12,128,128]{2,1,0:T(8,128)S(1)} %get-tuple-element.34.t.t2, ...), custom_call_target="tpu_custom_call" | custom-call | flops 402653184 | bytes 4194304 | tf_op jit(solution)/shard_map/rest2/pallas_call | solution.py:394
  21.8 0.0 collective-permute-done.2.recv_a
  21.8 1.4 %collective-permute-done.3.recv_b = bf16[6,128,128]{2,1,0:T(8,128)(2,1)S(1)} collective-permute-done((bf16[6,128,128]{2,1,0:T(8,128)(2,1)S(1)}, bf16[6,128,128]{2,1,0:T(8,128)(2,1)S(1)}, u32[]{:S(2)}, u32[]{:S(2)}) %collective-permute-start.3) | collective-permute-done | bytes 196640 | tf_op jit(solution)/shard_map/ppermute | solution.py:364
  23.2 1.6 %last.1 = (bf16[19,128,256]{2,1,0:T(8,128)(2,1)S(1)}, f32[12,128,128]{2,1,0:T(8,128)S(1)}, f32[12,128,128]{2,1,0:T(8,128)S(1)}, bf16[19,128,256]{2,1,0:T(8,128)(2,1)S(1)}, bf16[3,128,128]{2,1,0:T(8,128)(2,1)S(1)}) custom-call(s32[128]{0:T(128)S(1)} %get-tuple-element.25.tab, ...), custom_call_target="tpu_custom_call", output_to_operand_aliasing={{0}: (3, {}), {1}: (4, {})} | custom-call | flops 805306368 | bytes 4194304 | tf_op jit(solution)/shard_map/last/pallas_call | solution.py:394
  24.8 4.5 %collective-permute-start.4 = (bf16[3,128,128]{2,1,0:T(8,128)(2,1)S(1)}, bf16[3,128,128]{2,1,0:T(8,128)(2,1)S(1)}, u32[]{:S(2)}, u32[]{:S(2)}) collective-permute-start(bf16[3,128,128]{2,1,0:T(8,128)(2,1)S(1)} %get-tuple-element.41), channel_id=1, source_target_pairs={{0,15},{1,0},{2,1},{3,2},{4,3},{5,4},{6,5},{7,6},{8,7},{9,8},{10,9... | collective-permute-start | bytes 294920 | tf_op jit(solution)/shard_map/ppermute | solution.py:460
  29.3 2.2 %gram.1 = f32[16,128]{1,0:T(8,128)S(1)} custom-call(s32[128]{0:T(128)S(1)} %get-tuple-element.25.tab, bf16[12,4,128,128]{3,2,1,0:T(8,128)(2,1)S(1)} %get-tuple-element.26.aff, f32[12,128,128]{2,1,0:T(8,128)S(1)} %get-tuple-element.28.t.refs_0_.t0, f32[12,128,128]{2,1,0:T(8,128)S(1)} %get-tuple-element.35.refs_1_.t1, ...), custom_call_target="tpu_custom_call" | custom-call | flops 402653184 | bytes 4194304 | tf_op jit(solution)/shard_map/gram/pallas_call | solution.py:394
  31.5 0.0 collective-permute-done.4.recv
  31.5 0.7 %cross.1 = f32[16,16,128]{2,1,0:T(8,128)S(1)} custom-call(s32[128]{0:T(128)S(1)} %get-tuple-element.25.tab, bf16[12,4,128,128]{3,2,1,0:T(8,128)(2,1)S(1)} %get-tuple-element.26.aff, f32[12,128,128]{2,1,0:T(8,128)S(1)} %get-tuple-element.40.t4, bf16[3,128,128]{2,1,0:T(8,128)(2,1)S(1)} %collective-permute-done.4.recv, f32[16,128]{1,0:T(8,128)S(1)} %gram.1), custom_call_target="tpu_custom_call" | custom-call | flops 40265320 | bytes 4194304 | tf_op jit(solution)/shard_map/cross/pallas_call | solution.py:394
  32.3 13.6 %all_to_all.5.parts = f32[16,16,128]{2,1,0:T(8,128)S(1)} all-to-all(f32[16,16,128]{2,1,0:T(8,128)S(1)} %cross.1), channel_id=1, replica_groups=mesh['region'=2,'dom'=16] {'dom'}, dimensions={0} | all-to-all | bytes 262144 | tf_op jit(solution)/shard_map/all_to_all | solution.py:471
  45.9 1.3 %final.1 = f32[1536,128]{1,0:T(8,128)} custom-call(f32[16,16,128]{2,1,0:T(8,128)S(1)} %all_to_all.5.parts, f32[12,128,128]{2,1,0:T(8,128)S(1)} %get-tuple-element.28.t.refs_0_.t0, f32[12,128,128]{2,1,0:T(8,128)S(1)} %get-tuple-element.35.refs_1_.t1, f32[12,128,128]{2,1,0:T(8,128)S(1)} %get-tuple-element.34.t.t2, f32[12,128,128]{2,1,0:T(8,128)S(1)} %get-tuple-element.42.t3, ...), custom_call_target="tpu_custom_call" | custom-call | flops 40265320 | bytes 4194304 | tf_op jit(solution)/shard_map/final/pallas_call | solution.py:394
Async XLA Ops:
  3.7 7.4 %collective-permute-start = (bf16[6,128,128]{2,1,0:T(8,128)(2,1)S(1)}, bf16[6,128,128]{2,1,0:T(8,128)(2,1)S(1)}, u32[]{:S(2)}, u32[]{:S(2)}) collective-permute-start(bf16[6,128,128]{2,1,0:T(8,128)(2,1)S(1)} %get-tuple-element.31), channel_id=1, source_target_pairs={{0,1},{1,0},{2,3},{3,2},{4,5},{5,4},{6,7},{7,6},{8,9},{9,8},{10,11... | collective-permute-start | bytes 589832 | tf_op jit(solution)/shard_map/ppermute | solution.py:365
  4.3 9.0 %collective-permute-start.1 = (bf16[6,128,128]{2,1,0:T(8,128)(2,1)S(1)}, bf16[6,128,128]{2,1,0:T(8,128)(2,1)S(1)}, u32[]{:S(2)}, u32[]{:S(2)}) collective-permute-start(bf16[6,128,128]{2,1,0:T(8,128)(2,1)S(1)} %get-tuple-element.32), channel_id=1, source_target_pairs={{0,15},{1,2},{2,1},{3,4},{4,3},{5,6},{6,5},{7,8},{8,7},{9,10},{10,... | collective-permute-start | bytes 589832 | tf_op jit(solution)/shard_map/ppermute | solution.py:364
  15.3 6.5 %collective-permute-start.2 = (bf16[6,128,128]{2,1,0:T(8,128)(2,1)S(1)}, bf16[6,128,128]{2,1,0:T(8,128)(2,1)S(1)}, u32[]{:S(2)}, u32[]{:S(2)}) collective-permute-start(bf16[6,128,128]{2,1,0:T(8,128)(2,1)S(1)} %get-tuple-element.38), channel_id=1, source_target_pairs={{0,1},{1,0},{2,3},{3,2},{4,5},{5,4},{6,7},{7,6},{8,9},{9,8},{10,11... | collective-permute-start | bytes 589832 | tf_op jit(solution)/shard_map/ppermute | solution.py:365
  15.3 7.9 %collective-permute-start.3 = (bf16[6,128,128]{2,1,0:T(8,128)(2,1)S(1)}, bf16[6,128,128]{2,1,0:T(8,128)(2,1)S(1)}, u32[]{:S(2)}, u32[]{:S(2)}) collective-permute-start(bf16[6,128,128]{2,1,0:T(8,128)(2,1)S(1)} %get-tuple-element.39), channel_id=1, source_target_pairs={{0,15},{1,2},{2,1},{3,4},{4,3},{5,6},{6,5},{7,8},{8,7},{9,10},{10,... | collective-permute-start | bytes 589832 | tf_op jit(solution)/shard_map/ppermute | solution.py:364
  24.8 6.7 %collective-permute-start.4 = (bf16[3,128,128]{2,1,0:T(8,128)(2,1)S(1)}, bf16[3,128,128]{2,1,0:T(8,128)(2,1)S(1)}, u32[]{:S(2)}, u32[]{:S(2)}) collective-permute-start(bf16[3,128,128]{2,1,0:T(8,128)(2,1)S(1)} %get-tuple-element.41), channel_id=1, source_target_pairs={{0,15},{1,0},{2,1},{3,2},{4,3},{5,4},{6,5},{7,6},{8,7},{9,8},{10,9... | collective-permute-start | bytes 294920 | tf_op jit(solution)/shard_map/ppermute | solution.py:460

commit v5 on v4

--- a/solution.py
+++ b/solution.py
@@ -178,16 +178,25 @@
     load_q.wait()
     tall[...] = wide[...].T
     load_c.wait()
-    for c in range(chunks):
-        copies[c].wait()
-        if c == 0:
-            fill_table(cols, tab, up_rows, low_rows, axis)
-        value = jnp.maximum(dot(buf[c], tall[...]), 0.0)
+
+    def finish(scores, c):
+        value = jnp.maximum(scores, 0.0)
         value = value * value * value
         for i in range(per):
             block = value[i * rows : (i + 1) * rows]
             t0[c * per + i] = block
             put_split(hl, c * per + i, block)
+
+    scores = None
+    for c in range(chunks):
+        copies[c].wait()
+        if c == 0:
+            fill_table(cols, tab, up_rows, low_rows, axis)
+        ahead = dot(buf[c], tall[...])
+        if c > 0:
+            finish(scores, c - 1)
+        scores = ahead
+    finish(scores, chunks - 1)
     load_a.wait()
     pack(tab, SHIFTS[0], aff, t0, hl, send_b, lists + NAMED)
     pack(tab, SHIFTS[0], aff, t0, hl, send_a, lists)
@@ -212,41 +221,46 @@
 
 
 def rest_kernel(tab, aff, t, hl, *refs, step):
-    count = t.shape[0]
-    fields, (part, hl_next, *gram) = refs[: 2 * (step > 0)], refs[2 * (step > 0) :]
+    count, _, width = t.shape
+    fields, (part, hl_next, halo_part, *gram, sums_h) = refs[: 2 * (step > 0)], refs[2 * (step > 0) :]
+    _, _, cross, _, _ = offsets(count)
     hl_next[count + 2 * NAMED] = jnp.zeros(hl.shape[1:], BF)
+    sums_h[...] = jnp.zeros(sums_h.shape, F32)
     for g in range(count):
         value = shifted(row_product(aff, tab, 0, g, hl), SHIFTS[step], t[g])
         part[g] = value
         put_split(hl_next, g, value)
+    for e in range(ENTRIES):
+        g, slot, h = (tab[cross + 3 * e + i] for i in range(3))
+        both = dot_t(aff[g, slot], hl[g])
+        sums_h[h] += both[:, :width] + both[:, width:]
+    for h in range(2 * NAMED):
+        halo_part[h] = sums_h[h]
     if gram:
-        width = t.shape[2]
         sums = [jnp.zeros((8, width), F32) for _ in EARLY]
         sums = add_products(sums, EARLY, (*fields, t))
         for n, total in enumerate(sums):
             gram[0][pl.ds(n, 1), :] = jnp.sum(total, axis=0, keepdims=True)
 
 
-def two_steps(tab, aff, hl, hl1, t1, recv_a, recv_b, t2, hl2, halo, hacc, step):
+def two_steps(tab, aff, hl1, t1, halo_part, recv_a, recv_b, t2, hl2, halo, step):
     count, _, width = t2.shape
     full, lists, cross, _, _ = offsets(count)
-    halo[2 * NAMED] = jnp.zeros(halo.shape[1:], BF)
-    hacc[2 * NAMED] = jnp.zeros(hacc.shape[1:], F32)
+    zeros = jnp.zeros(hl2.shape[1:], BF)
+    hl2[count + 2 * NAMED] = zeros
+    halo[2 * NAMED] = zeros[:, :width]
     for h in range(NAMED):
         halo[h] = recv_a[h]
         halo[NAMED + h] = recv_b[h]
-        hacc[h] = recv_a[NAMED + h].astype(F32)
-        hacc[NAMED + h] = recv_b[NAMED + h].astype(F32)
+        low, high = h, NAMED + h
+        put_split(hl1, count + low, recv_a[NAMED + h].astype(F32) + halo_part[low])
+        put_split(hl1, count + high, recv_b[NAMED + h].astype(F32) + halo_part[high])
     for e in range(ENTRIES):
         g, slot, h = (tab[cross + 3 * e + i] for i in range(3))
-        tile = aff[g, slot]
-        t1[g] += dot(tile, halo[h])
-        hacc[h] += dot_t(tile, hl[g, :, :width])
+        t1[g] += dot(aff[g, slot], halo[h])
     for j in range(2 * NAMED):
         g = tab[lists + j]
         put_split(hl1, g, t1[g])
-    for h in range(2 * NAMED):
-        put_split(hl1, count + h, hacc[h])
     for g in range(count):
         value = shifted(row_product(aff, tab, full, g, hl1), SHIFTS[step + 1], t1[g])
         t2[g] = value
@@ -254,28 +268,34 @@
 
 
 def middle_kernel(
-    tab, aff, hl, _, __, recv_a, recv_b, hl1, t1, t2, hl2, send_a, send_b, halo, hacc
+    tab, aff, _, __, halo_part, recv_a, recv_b, hl1, t1, t2, hl2, send_a, send_b, halo
 ):
     _, lists, _, _, _ = offsets(t1.shape[0])
-    hl2[t1.shape[0] + 2 * NAMED] = jnp.zeros(hl2.shape[1:], BF)
-    two_steps(tab, aff, hl, hl1, t1, recv_a, recv_b, t2, hl2, halo, hacc, 0)
+    two_steps(tab, aff, hl1, t1, halo_part, recv_a, recv_b, t2, hl2, halo, 0)
     pack(tab, SHIFTS[2], aff, t2, hl2, send_b, lists + NAMED)
     pack(tab, SHIFTS[2], aff, t2, hl2, send_a, lists)
 
 
-def last_kernel(tab, aff, hl, _, __, recv_a, recv_b, hl3, t3, t4, hl4, send, halo, hacc):
+def last_kernel(tab, aff, _, __, halo_part, recv_a, recv_b, hl3, t3, t4, hl4, send, halo):
     count, _, width = t3.shape
     _, lists, _, _, _ = offsets(count)
-    hl4[count + 2 * NAMED] = jnp.zeros(hl4.shape[1:], BF)
-    two_steps(tab, aff, hl, hl3, t3, recv_a, recv_b, t4, hl4, halo, hacc, 2)
+    two_steps(tab, aff, hl3, t3, halo_part, recv_a, recv_b, t4, hl4, halo, 2)
     for j in range(NAMED):
         send[j] = hl4[tab[lists + 2 * NAMED + j], :, :width]
 
 
-def gram_kernel(tab, aff, t0, t1, t2, t3, t4, hl, early, out):
+def gram_kernel(tab, aff, t0, t1, t2, t3, t4, hl, early, out, weight, sums_h):
     count, rows, width = t0.shape
+    _, _, _, cross, _ = offsets(count)
     sums = [jnp.zeros((8, width), F32) for _ in LATE]
     last = jnp.zeros((8, width), F32)
+    sums_h[...] = jnp.zeros(sums_h.shape, F32)
+    for e in range(1 + NAMED):
+        g, slot, h = (tab[cross + 3 * e + i] for i in range(3))
+        both = dot_t(aff[g, slot], hl[g])
+        sums_h[h] += 2.0 * (both[:, :width] + both[:, width:])
+    for h in range(NAMED):
+        weight[h] = sums_h[h]
     for g in range(count):
         local = row_product(aff, tab, 0, g, hl)
         last = last + (t4[g] * local).reshape(rows // 8, 8, width).sum(0)
@@ -285,24 +305,21 @@
         out[pl.ds(len(EARLY) + n, 1), :] = jnp.sum(total, axis=0, keepdims=True)
 
 
-def cross_kernel(tab, aff, t4, recv, gram, out):
-    count = t4.shape[0]
-    _, _, _, high, _ = offsets(count)
-    total = jnp.zeros((8, gram.shape[1]), F32)
-    for e in range(1 + NAMED):
-        g, slot, h = (tab[high + 3 * e + i] for i in range(3))
-        part = t4[g] * dot(aff[g, slot], recv[jnp.minimum(h, NAMED - 1)])
-        part = part.reshape(-1, 8, part.shape[-1]).sum(0)
-        total = total + jnp.where(h < NAMED, part, 0.0)
+def cross_kernel(weight, recv, gram, out):
+    _, rows, width = weight.shape
+    total = jnp.zeros((8, width), F32)
+    for h in range(NAMED):
+        part = weight[h] * recv[h].astype(F32)
+        total = total + part.reshape(rows // 8, 8, width).sum(0)
     value = gram[...]
-    extra = 2.0 * jnp.sum(total, axis=0, keepdims=True)
+    extra = jnp.sum(total, axis=0, keepdims=True)
     index = lax.broadcasted_iota(jnp.int32, value.shape, 0)
     value = value + jnp.where(index == ROWS - 1, extra, 0.0)
     for d in range(out.shape[0]):
         out[d] = value
 
 
-def final_kernel(parts, t0, t1, t2, t3, t4, out):
+def final_kernel(parts, t0, t1, t2, t3, t4, out, buf, sems):
     n = ITERATIONS
     value = parts[0]
     for d in range(1, parts.shape[0]):
@@ -348,13 +365,22 @@
     coef = [coef[k] * scale[k] for k in range(n)]
     fields = (t0, t1, t2, t3, t4)
     count, rows, width = t0.shape
-    wide = [jnp.broadcast_to(c, (8, width)) for c in coef]
-    for g in range(count):
-        total = None
-        for f, c in zip(fields, coef):
-            term = f[g] * c
-            total = term if total is None else total + term
-        out[pl.ds(g * rows, rows), :] = total
+    chunks = sems.shape[0]
+    per = count // chunks
+    copies = []
+    for c in range(chunks):
+        for g in range(c * per, (c + 1) * per):
+            total = None
+            for f, k in zip(fields, coef):
+                term = f[g] * k
+                total = term if total is None else total + term
+            buf[pl.ds(g * rows, rows), :] = total
+        part = pl.ds(c * per * rows, per * rows)
+        copy = pltpu.make_async_copy(buf.at[part], out.at[part], sems.at[c])
+        copy.start()
+        copies.append(copy)
+    for copy in copies:
+        copy.wait()
 
 
 def swap(block_a, block_b, axis):
@@ -379,10 +405,10 @@
     edge = jax.ShapeDtypeStruct((2 * NAMED, rows, width), BF)
     half = jax.ShapeDtypeStruct((NAMED, rows, width), BF)
     early = jax.ShapeDtypeStruct((len(EARLY), width), F32)
-    work = [
-        pltpu.VMEM((2 * NAMED + 1, rows, width), BF),
-        pltpu.VMEM((2 * NAMED + 1, rows, width), F32),
-    ]
+    edge_sum = jax.ShapeDtypeStruct((2 * NAMED, rows, width), F32)
+    half_sum = jax.ShapeDtypeStruct((NAMED, rows, width), F32)
+    sums_h = pltpu.VMEM((2 * NAMED + 1, rows, width), F32)
+    work = [pltpu.VMEM((2 * NAMED + 1, rows, width), BF)]
     chunks = count // 2
     flops = 2 * count * rows * 4 * rows * 2 * width
 
@@ -391,6 +417,10 @@
 
         def run(*args):
             specs = [SMEM if x.dtype == jnp.int32 else VMEM for x in args]
+            args = [
+                pltpu.with_memory_space_constraint(x, pltpu.SMEM) if x.dtype == jnp.int32 else x
+                for x in args
+            ]
             return pl.pallas_call(
                 kernel,
                 out_shape=out_shape,
@@ -416,7 +446,7 @@
             edge,
             edge,
             jax.ShapeDtypeStruct(affinity.shape, BF),
-            jax.ShapeDtypeStruct((size,), jnp.int32),
+            pltpu.SMEM((size,), jnp.int32),
         ),
         in_specs=[HBM] * 4,
         out_specs=(VMEM,) * 5 + (SMEM,),
@@ -434,32 +464,40 @@
         name="first",
     )(*(pltpu.with_memory_space_constraint(x, pltpu.HBM) for x in operands))
     recv_a, recv_b = swap(send_a, send_b, axis)
-    part, hl1 = call(
-        functools.partial(rest_kernel, step=0), (field, split), 1, name="rest0"
+    part, hl1, halo_part = call(
+        functools.partial(rest_kernel, step=0), (field, split, edge_sum), 1, [sums_h], name="rest0"
     )(tab, aff, t0, hl0)
     _, t1, t2, hl2, send_a, send_b = call(
         middle_kernel,
         (split, field, field, split, edge, edge),
         2,
         work,
-        {3: 0, 4: 1},
+        {2: 0, 3: 1},
         name="middle",
-    )(tab, aff, hl0, hl1, part, recv_a, recv_b)
+    )(tab, aff, hl1, part, halo_part, recv_a, recv_b)
     recv_a, recv_b = swap(send_a, send_b, axis)
-    part, hl3, gram = call(
-        functools.partial(rest_kernel, step=2), (field, split, early), 1, name="rest2"
+    part, hl3, halo_part, gram = call(
+        functools.partial(rest_kernel, step=2),
+        (field, split, edge_sum, early),
+        1,
+        [sums_h],
+        name="rest2",
     )(tab, aff, t2, hl2, t0, t1)
     _, t3, t4, hl4, send = call(
         last_kernel,
         (split, field, field, split, half),
         2,
         work,
-        {3: 0, 4: 1},
+        {2: 0, 3: 1},
         name="last",
-    )(tab, aff, hl2, hl3, part, recv_a, recv_b)
+    )(tab, aff, hl3, part, halo_part, recv_a, recv_b)
     recv = lax.ppermute(send, axis, [(i, (i - 1) % devices) for i in range(devices)])
-    gram = call(
-        gram_kernel, jax.ShapeDtypeStruct((ROWS, width), F32), 1, name="gram"
+    gram, weight = call(
+        gram_kernel,
+        (jax.ShapeDtypeStruct((ROWS, width), F32), half_sum),
+        1,
+        [sums_h],
+        name="gram",
     )(tab, aff, t0, t1, t2, t3, t4, hl4, gram)
     parts = call(
         cross_kernel,
@@ -467,10 +505,19 @@
         0.1,
         name="cross",
         limit=8,
-    )(tab, aff, t4, recv, gram)
+    )(weight, recv, gram)
     parts = lax.all_to_all(parts, axis, 0, 0)
-    return call(
-        final_kernel, jax.ShapeDtypeStruct((count * rows, width), F32), 0.1, name="final"
+    return pl.pallas_call(
+        final_kernel,
+        out_shape=jax.ShapeDtypeStruct((count * rows, width), F32),
+        in_specs=[VMEM] * 6,
+        out_specs=HBM,
+        scratch_shapes=[
+            pltpu.VMEM((count * rows, width), F32),
+            pltpu.SemaphoreType.DMA((count // 3,)),
+        ],
+        compiler_params=params(24),
+        name="final",
     )(parts, t0, t1, t2, t3, t4)
 
 

time: 47.3 us -> 45 us (0.951)
  Pallas kernels: 14.5 us -> 11.1 us
  waiting for transfers between devices: 3.66 us -> 4.78 us
    pallas_call x7 -> x6, Pallas kernels: 10.8 us -> 6.55 us  [run(): pl.pallas_call(kernel, out_shape=out_shape, in_specs=specs, out_specs=(VM...]
    pallas_call x0 -> x1, Pallas kernels: none -> 1.09 us  [shards(): pl.pallas_call(final_kernel, out_shape=jax.ShapeDtypeStruct((count * rows...]
    ppermute x2, waiting for transfers between devices: 3.63 us -> 4.31 us  [swap(): got_b = lax.ppermute(block_b, axis, pairs_b)]
  transfers between devices with their start and end apart: 5 -> 5, of which waited for: 2 -> 3; matrix products, arithmetic and copies ran while one was open for 0% -> 0% of each run, Pallas kernels for 11% -> 9%
where the time goes in v5:
time: 45 us; the launch traced here: 44.8 us
  starting transfers between devices  15.2 us (34%)
  blocking collectives  13.6 us (30%)
  Pallas kernels  11.1 us (25%)
  waiting for transfers between devices  4.78 us (11%)
    all_to_all x1, blocking collectives, shards(): parts = lax.all_to_all(parts, axis, 0, 0)  13.6 us
    ppermute x2, starting transfers between devices, swap(): got_b = lax.ppermute(block_b, axis, pairs_b)  10.2 us
    pallas_call x6, Pallas kernels, run(): pl.pallas_call(kernel, out_shape=out_shape, in_specs=specs, out_specs=(VM...  6.55 us
    ppermute x1, starting transfers between devices, shards(): lax.ppermute(send, axis, [(i, (i - 1) % devices) for i in range(devices)])  4.46 us
    ppermute x2, waiting for transfers between devices, swap(): got_b = lax.ppermute(block_b, axis, pairs_b)  4.31 us
    pallas_call x1, Pallas kernels, shards(): pl.pallas_call(functools.partial(first_kernel, chunks=chunks, axis=axis),...  3.47 us
    pallas_call x1, Pallas kernels, shards(): pl.pallas_call(final_kernel, out_shape=jax.ShapeDtypeStruct((count * rows...  1.09 us
  transfers between devices with their start and end apart: 5, of which 3 were waited for; matrix products, arithmetic and copies ran while one was open for 0% of the time, Pallas kernels for 9%

profile of v5, /device:TPU:0, one launch (start us, length us, event | category | flops | bytes accessed | tf_op | source)
XLA Modules:
  0.0 44.8 jit_solution(3427634670805218457)
XLA Ops:
  0.0 3.5 %first.1 = (f32[12,128,128]{2,1,0:T(8,128)S(1)}, bf16[19,128,256]{2,1,0:T(8,128)(2,1)S(1)}, bf16[6,128,128]{2,1,0:T(8,128)(2,1)S(1)}, bf16[6,128,128]{2,1,0:T(8,...) custom-call(bf16[1536,768]{1,0:T(8,128)(2,1)} %desc.1, bf16[128,768]{1,0:T(8,128)(2,1)} %queries.1, ...), custom_call_target="tpu_custom_call" | custom-call | flops 402653184 | bytes 4194304 | tf_op jit(solution)/shard_map/first/pallas_call | solution.py:441
  3.5 0.6 %collective-permute-start = (bf16[6,128,128]{2,1,0:T(8,128)(2,1)S(1)}, bf16[6,128,128]{2,1,0:T(8,128)(2,1)S(1)}, u32[]{:S(2)}, u32[]{:S(2)}) collective-permute-start(bf16[6,128,128]{2,1,0:T(8,128)(2,1)S(1)} %get-tuple-element.36), channel_id=1, source_target_pairs={{0,1},{1,0},{2,3},{3,2},{4,5},{5,4},{6,7},{7,6},{8,9},{9,8},{10,11... | collective-permute-start | bytes 589832 | tf_op jit(solution)/shard_map/ppermute | solution.py:391
  4.0 5.7 %collective-permute-start.1 = (bf16[6,128,128]{2,1,0:T(8,128)(2,1)S(1)}, bf16[6,128,128]{2,1,0:T(8,128)(2,1)S(1)}, u32[]{:S(2)}, u32[]{:S(2)}) collective-permute-start(bf16[6,128,128]{2,1,0:T(8,128)(2,1)S(1)} %get-tuple-element.37), channel_id=1, source_target_pairs={{0,15},{1,2},{2,1},{3,4},{4,3},{5,6},{6,5},{7,8},{8,7},{9,10},{10,... | collective-permute-start | bytes 589832 | tf_op jit(solution)/shard_map/ppermute | solution.py:390
  9.7 0.8 %rest0.1 = (f32[12,128,128]{2,1,0:T(8,128)S(1)}, bf16[19,128,256]{2,1,0:T(8,128)(2,1)S(1)}, f32[6,128,128]{2,1,0:T(8,128)S(1)}) custom-call(s32[128]{0:T(128)S(4)} %get-tuple-element.29.tab, bf16[12,4,128,128]{3,2,1,0:T(8,128)(2,1)S(1)} %get-tuple-element.30.aff, f32[12,128,128]{2,1,0:T(8,128)S(1)} %get-tuple-element.31.t.refs_0_.t0, ...), custom_call_target="tpu_custom_call" | custom-call | flops 402653184 | bytes 4194304 | tf_op jit(solution)/shard_map/rest0/pallas_call | solution.py:424
  10.5 0.0 collective-permute-done.recv_a
  10.5 2.6 %collective-permute-done.1.recv_b = bf16[6,128,128]{2,1,0:T(8,128)(2,1)S(1)} collective-permute-done((bf16[6,128,128]{2,1,0:T(8,128)(2,1)S(1)}, bf16[6,128,128]{2,1,0:T(8,128)(2,1)S(1)}, u32[]{:S(2)}, u32[]{:S(2)}) %collective-permute-start.1) | collective-permute-done | bytes 196640 | tf_op jit(solution)/shard_map/ppermute | solution.py:390
  13.0 1.4 %middle.1 = (bf16[19,128,256]{2,1,0:T(8,128)(2,1)S(1)}, f32[12,128,128]{2,1,0:T(8,128)S(1)}, f32[12,128,128]{2,1,0:T(8,128)S(1)}, bf16[19,128,256]{2,1,0:T(8,128...) custom-call(s32[128]{0:T(128)S(4)} %get-tuple-element.29.tab, ...), custom_call_target="tpu_custom_call", output_to_operand_aliasing={{0}: (2, {}), {1}: (3, {})} | custom-call | flops 805306368 | bytes 4194304 | tf_op jit(solution)/shard_map/middle/pallas_call | solution.py:424
  14.4 0.1 collective-permute-start.2
  14.5 4.5 %collective-permute-start.3 = (bf16[6,128,128]{2,1,0:T(8,128)(2,1)S(1)}, bf16[6,128,128]{2,1,0:T(8,128)(2,1)S(1)}, u32[]{:S(2)}, u32[]{:S(2)}) collective-permute-start(bf16[6,128,128]{2,1,0:T(8,128)(2,1)S(1)} %get-tuple-element.45), channel_id=1, source_target_pairs={{0,15},{1,2},{2,1},{3,4},{4,3},{5,6},{6,5},{7,8},{8,7},{9,10},{10,... | collective-permute-start | bytes 589832 | tf_op jit(solution)/shard_map/ppermute | solution.py:390
  19.0 1.6 %rest2.1 = (f32[12,128,128]{2,1,0:T(8,128)S(1)}, bf16[19,128,256]{2,1,0:T(8,128)(2,1)S(1)}, f32[6,128,128]{2,1,0:T(8,128)S(1)}, f32[6,128]{1,0:T(8,128)S(1)}) custom-call(s32[128]{0:T(128)S(4)} %get-tuple-element.29.tab, bf16[12,4,128,128]{3,2,1,0:T(8,128)(2,1)S(1)} %get-tuple-element.30.aff, f32[12,128,128]{2,1,0:T(8,128)S(1)} %get-tuple-element.39.t.t2, ...), custom_call_target="tpu_custom_call" | custom-call | flops 402653184 | bytes 4194304 | tf_op jit(solution)/shard_map/rest2/pallas_call | solution.py:424
  20.6 0.0 collective-permute-done.2.recv_a
  20.6 1.8 %collective-permute-done.3.recv_b = bf16[6,128,128]{2,1,0:T(8,128)(2,1)S(1)} collective-permute-done((bf16[6,128,128]{2,1,0:T(8,128)(2,1)S(1)}, bf16[6,128,128]{2,1,0:T(8,128)(2,1)S(1)}, u32[]{:S(2)}, u32[]{:S(2)}) %collective-permute-start.3) | collective-permute-done | bytes 196640 | tf_op jit(solution)/shard_map/ppermute | solution.py:390
  22.4 1.0 %last.1 = (bf16[19,128,256]{2,1,0:T(8,128)(2,1)S(1)}, f32[12,128,128]{2,1,0:T(8,128)S(1)}, f32[12,128,128]{2,1,0:T(8,128)S(1)}, bf16[19,128,256]{2,1,0:T(8,128)(2,1)S(1)}, bf16[3,128,128]{2,1,0:T(8,128)(2,1)S(1)}) custom-call(s32[128]{0:T(128)S(4)} %get-tuple-element.29.tab, ...), custom_call_target="tpu_custom_call", output_to_operand_aliasing={{0}: (2, {}), {1}: (3, {})} | custom-call | flops 805306368 | bytes 4194304 | tf_op jit(solution)/shard_map/last/pallas_call | solution.py:424
  23.4 4.5 %collective-permute-start.4 = (bf16[3,128,128]{2,1,0:T(8,128)(2,1)S(1)}, bf16[3,128,128]{2,1,0:T(8,128)(2,1)S(1)}, u32[]{:S(2)}, u32[]{:S(2)}) collective-permute-start(bf16[3,128,128]{2,1,0:T(8,128)(2,1)S(1)} %get-tuple-element.51), channel_id=1, source_target_pairs={{0,15},{1,0},{2,1},{3,2},{4,3},{5,4},{6,5},{7,6},{8,7},{9,8},{10,9... | collective-permute-start | bytes 294920 | tf_op jit(solution)/shard_map/ppermute | solution.py:494
  27.9 1.7 %gram.1 = (f32[16,128]{1,0:T(8,128)S(1)}, f32[3,128,128]{2,1,0:T(8,128)S(1)}) custom-call(s32[128]{0:T(128)S(4)} %get-tuple-element.29.tab, bf16[12,4,128,128]{3,2,1,0:T(8,128)(2,1)S(1)} %get-tuple-element.30.aff, f32[12,128,128]{2,1,0:T(8,128)S(1)} %get-tuple-element.31.t.refs_0_.t0, f32[12,128,128]{2,1,0:T(8,128)S(1)} %get-tuple-element.38.refs_1_.t1, ...), custom_call_target="tpu_custom_call" | custom-call | flops 402653184 | bytes 4194304 | tf_op jit(solution)/shard_map/gram/pallas_call | solution.py:424
  29.6 0.5 %collective-permute-done.4.recv = bf16[3,128,128]{2,1,0:T(8,128)(2,1)S(1)} collective-permute-done((bf16[3,128,128]{2,1,0:T(8,128)(2,1)S(1)}, bf16[3,128,128]{2,1,0:T(8,128)(2,1)S(1)}, u32[]{:S(2)}, u32[]{:S(2)}) %collective-permute-start.4) | collective-permute-done | bytes 98336 | tf_op jit(solution)/shard_map/ppermute | solution.py:494
  30.1 13.6 %all_to_all.5.parts = f32[16,16,128]{2,1,0:T(8,128)S(1)} all-to-all(f32[16,16,128]{2,1,0:T(8,128)S(1)} %cross.1), channel_id=1, replica_groups=mesh['region'=2,'dom'=16] {'dom'}, dimensions={0} | all-to-all | bytes 262144 | tf_op jit(solution)/shard_map/all_to_all | solution.py:509
  43.7 1.1 %final.1 = f32[1536,128]{1,0:T(8,128)} custom-call(f32[16,16,128]{2,1,0:T(8,128)S(1)} %all_to_all.5.parts, f32[12,128,128]{2,1,0:T(8,128)S(1)} %get-tuple-element.31.t.refs_0_.t0, f32[12,128,128]{2,1,0:T(8,128)S(1)} %get-tuple-element.38.refs_1_.t1, f32[12,128,128]{2,1,0:T(8,128)S(1)} %get-tuple-element.39.t.t2, f32[12,128,128]{2,1,0:T(8,128)S(1)} %get-tuple-element.46.t3, ...), custom_call_target="tpu_custom_call" | custom-call | tf_op jit(solution)/shard_map/final/pallas_call | solution.py:510
  (1 shorter events, 0.0 us)
Async XLA Ops:
  3.5 7.0 %collective-permute-start = (bf16[6,128,128]{2,1,0:T(8,128)(2,1)S(1)}, bf16[6,128,128]{2,1,0:T(8,128)(2,1)S(1)}, u32[]{:S(2)}, u32[]{:S(2)}) collective-permute-start(bf16[6,128,128]{2,1,0:T(8,128)(2,1)S(1)} %get-tuple-element.36), channel_id=1, source_target_pairs={{0,1},{1,0},{2,3},{3,2},{4,5},{5,4},{6,7},{7,6},{8,9},{9,8},{10,11... | collective-permute-start | bytes 589832 | tf_op jit(solution)/shard_map/ppermute | solution.py:391
  4.0 9.0 %collective-permute-start.1 = (bf16[6,128,128]{2,1,0:T(8,128)(2,1)S(1)}, bf16[6,128,128]{2,1,0:T(8,128)(2,1)S(1)}, u32[]{:S(2)}, u32[]{:S(2)}) collective-permute-start(bf16[6,128,128]{2,1,0:T(8,128)(2,1)S(1)} %get-tuple-element.37), channel_id=1, source_target_pairs={{0,15},{1,2},{2,1},{3,4},{4,3},{5,6},{6,5},{7,8},{8,7},{9,10},{10,... | collective-permute-start | bytes 589832 | tf_op jit(solution)/shard_map/ppermute | solution.py:390
  14.4 6.2 %collective-permute-start.2 = (bf16[6,128,128]{2,1,0:T(8,128)(2,1)S(1)}, bf16[6,128,128]{2,1,0:T(8,128)(2,1)S(1)}, u32[]{:S(2)}, u32[]{:S(2)}) collective-permute-start(bf16[6,128,128]{2,1,0:T(8,128)(2,1)S(1)} %get-tuple-element.44), channel_id=1, source_target_pairs={{0,1},{1,0},{2,3},{3,2},{4,5},{5,4},{6,7},{7,6},{8,9},{9,8},{10,11... | collective-permute-start | bytes 589832 | tf_op jit(solution)/shard_map/ppermute | solution.py:391
  14.5 7.9 %collective-permute-start.3 = (bf16[6,128,128]{2,1,0:T(8,128)(2,1)S(1)}, bf16[6,128,128]{2,1,0:T(8,128)(2,1)S(1)}, u32[]{:S(2)}, u32[]{:S(2)}) collective-permute-start(bf16[6,128,128]{2,1,0:T(8,128)(2,1)S(1)} %get-tuple-element.45), channel_id=1, source_target_pairs={{0,15},{1,2},{2,1},{3,4},{4,3},{5,6},{6,5},{7,8},{8,7},{9,10},{10,... | collective-permute-start | bytes 589832 | tf_op jit(solution)/shard_map/ppermute | solution.py:390
  23.4 6.7 %collective-permute-start.4 = (bf16[3,128,128]{2,1,0:T(8,128)(2,1)S(1)}, bf16[3,128,128]{2,1,0:T(8,128)(2,1)S(1)}, u32[]{:S(2)}, u32[]{:S(2)}) collective-permute-start(bf16[3,128,128]{2,1,0:T(8,128)(2,1)S(1)} %get-tuple-element.51), channel_id=1, source_target_pairs={{0,15},{1,0},{2,1},{3,2},{4,3},{5,4},{6,5},{7,6},{8,7},{9,8},{10,9... | collective-permute-start | bytes 294920 | tf_op jit(solution)/shard_map/ppermute | solution.py:494

commit v6 on v5

--- a/solution.py
+++ b/solution.py
@@ -70,9 +70,8 @@
 def offsets(count):
     full = count + 2
     lists = 2 * full
-    cross = lists + 3 * NAMED
-    high = cross + 3 * ENTRIES
-    return full, lists, cross, high, high + 3 * (1 + NAMED)
+    cross = lists + 2 * NAMED
+    return full, lists, cross, cross + 3 * ENTRIES
 
 
 def fill_table(tile_col, tab, up_rows, low_rows, axis):
@@ -80,7 +79,7 @@
     total = count * lax.axis_size(axis)
     me = lax.axis_index(axis)
     even = lax.rem(me, 2) == 0
-    full, lists, cross, high, _ = offsets(count)
+    full, lists, cross, _ = offsets(count)
     zero = count + 2 * NAMED
     up_base = jnp.where(even, 0, NAMED)
     low_base = NAMED - up_base
@@ -129,7 +128,6 @@
         up, low = up_rows[0, j], low_rows[0, j]
         tab[lists + j] = jnp.where(even, up, low)
         tab[lists + NAMED + j] = jnp.where(even, low, up)
-        tab[lists + 2 * NAMED + j] = low
     chains = ((0, 1, low_base + NAMED - 1), (count - 1, 2, up_base))
     for side, (rows, used) in enumerate(((low_rows, low_cross), (up_rows, up_cross))):
         for i in range(3):
@@ -139,11 +137,6 @@
             tab[at] = jnp.where(j < used, rows[1, j], 0)
             tab[at + 1] = jnp.int32(3)
             tab[at + 2] = jnp.where(j < used, rows[2, j], 2 * NAMED)
-    for j in range(1 + NAMED):
-        at = cross + 3 * (1 + NAMED + j)
-        tab[high + 3 * j] = tab[at]
-        tab[high + 3 * j + 1] = tab[at + 1]
-        tab[high + 3 * j + 2] = jnp.where(tab[at + 2] < 2 * NAMED, tab[at + 2] - up_base, NAMED)
 
 
 def pack(tab, shift, aff, t, hl, send, base):
@@ -155,12 +148,12 @@
 
 
 def first_kernel(
-    desc, queries, affinity, tile_col, t0, hl, send_a, send_b, aff, tab,
+    desc, queries, affinity, tile_col, t0, hl, send_b, aff, tab,
     buf, wide, tall, cols, up_rows, low_rows, sems, *, chunks, axis,
 ):
     count, rows = t0.shape[0], t0.shape[1]
     per = count // chunks
-    _, lists, _, _, _ = offsets(count)
+    _, lists, _, _ = offsets(count)
     load_q = pltpu.make_async_copy(queries, wide, sems.at[chunks])
     load_c = pltpu.make_async_copy(tile_col, cols, sems.at[chunks + 1])
     load_q.start()
@@ -199,7 +192,6 @@
     finish(scores, chunks - 1)
     load_a.wait()
     pack(tab, SHIFTS[0], aff, t0, hl, send_b, lists + NAMED)
-    pack(tab, SHIFTS[0], aff, t0, hl, send_a, lists)
 
 
 def add_products(sums, pairs, fields):
@@ -220,32 +212,41 @@
     return list(lax.fori_loop(0, count * rows // group, body, tuple(sums)))
 
 
-def rest_kernel(tab, aff, t, hl, *refs, step):
-    count, _, width = t.shape
-    fields, (part, hl_next, halo_part, *gram, sums_h) = refs[: 2 * (step > 0)], refs[2 * (step > 0) :]
-    _, _, cross, _, _ = offsets(count)
+def halo_products(tab, aff, hl, sums, factor):
+    count = aff.shape[0]
+    width = sums.shape[2]
+    _, _, cross, _ = offsets(count)
+    sums[...] = jnp.zeros(sums.shape, F32)
+    for e in range(ENTRIES):
+        g, slot, h = (tab[cross + 3 * e + i] for i in range(3))
+        both = dot_t(aff[g, slot], hl[g])
+        both = both[:, :width] + both[:, width:]
+        sums[h] += both if factor == 1.0 else factor * both
+
+
+def rest_kernel(tab, aff, t, hl, part, hl_next, halo_part, send_a, sums, *, step):
+    count = t.shape[0]
+    _, lists, _, _ = offsets(count)
+    pack(tab, SHIFTS[step], aff, t, hl, send_a, lists)
     hl_next[count + 2 * NAMED] = jnp.zeros(hl.shape[1:], BF)
-    sums_h[...] = jnp.zeros(sums_h.shape, F32)
     for g in range(count):
         value = shifted(row_product(aff, tab, 0, g, hl), SHIFTS[step], t[g])
         part[g] = value
         put_split(hl_next, g, value)
-    for e in range(ENTRIES):
-        g, slot, h = (tab[cross + 3 * e + i] for i in range(3))
-        both = dot_t(aff[g, slot], hl[g])
-        sums_h[h] += both[:, :width] + both[:, width:]
+    halo_products(tab, aff, hl, sums, 1.0)
     for h in range(2 * NAMED):
-        halo_part[h] = sums_h[h]
-    if gram:
-        sums = [jnp.zeros((8, width), F32) for _ in EARLY]
-        sums = add_products(sums, EARLY, (*fields, t))
-        for n, total in enumerate(sums):
-            gram[0][pl.ds(n, 1), :] = jnp.sum(total, axis=0, keepdims=True)
+        halo_part[h] = sums[h]
+
+
+def early_kernel(t0, t1, t2, out):
+    sums = [jnp.zeros((8, t0.shape[2]), F32) for _ in EARLY]
+    for n, total in enumerate(add_products(sums, EARLY, (t0, t1, t2))):
+        out[pl.ds(n, 1), :] = jnp.sum(total, axis=0, keepdims=True)
 
 
 def two_steps(tab, aff, hl1, t1, halo_part, recv_a, recv_b, t2, hl2, halo, step):
     count, _, width = t2.shape
-    full, lists, cross, _, _ = offsets(count)
+    full, lists, cross, _ = offsets(count)
     zeros = jnp.zeros(hl2.shape[1:], BF)
     hl2[count + 2 * NAMED] = zeros
     halo[2 * NAMED] = zeros[:, :width]
@@ -268,33 +269,30 @@
 
 
 def middle_kernel(
-    tab, aff, _, __, halo_part, recv_a, recv_b, hl1, t1, t2, hl2, send_a, send_b, halo
+    tab, aff, _, __, halo_part, recv_a, recv_b, hl1, t1, t2, hl2, send_b, halo
 ):
-    _, lists, _, _, _ = offsets(t1.shape[0])
+    _, lists, _, _ = offsets(t1.shape[0])
     two_steps(tab, aff, hl1, t1, halo_part, recv_a, recv_b, t2, hl2, halo, 0)
     pack(tab, SHIFTS[2], aff, t2, hl2, send_b, lists + NAMED)
-    pack(tab, SHIFTS[2], aff, t2, hl2, send_a, lists)
 
 
 def last_kernel(tab, aff, _, __, halo_part, recv_a, recv_b, hl3, t3, t4, hl4, send, halo):
     count, _, width = t3.shape
-    _, lists, _, _, _ = offsets(count)
+    _, lists, _, _ = offsets(count)
     two_steps(tab, aff, hl3, t3, halo_part, recv_a, recv_b, t4, hl4, halo, 2)
     for j in range(NAMED):
-        send[j] = hl4[tab[lists + 2 * NAMED + j], :, :width]
-
-
-def gram_kernel(tab, aff, t0, t1, t2, t3, t4, hl, early, out, weight, sums_h):
+        send[j] = hl4[tab[lists + NAMED + j], :, :width]
+
+
+def gram_kernel(tab, aff, t0, t1, t2, t3, t4, hl, early, out, weight, send_a, sums_h):
     count, rows, width = t0.shape
-    _, _, _, cross, _ = offsets(count)
+    _, lists, _, _ = offsets(count)
+    for j in range(NAMED):
+        send_a[j] = hl[tab[lists + j], :, :width]
     sums = [jnp.zeros((8, width), F32) for _ in LATE]
     last = jnp.zeros((8, width), F32)
-    sums_h[...] = jnp.zeros(sums_h.shape, F32)
-    for e in range(1 + NAMED):
-        g, slot, h = (tab[cross + 3 * e + i] for i in range(3))
-        both = dot_t(aff[g, slot], hl[g])
-        sums_h[h] += 2.0 * (both[:, :width] + both[:, width:])
-    for h in range(NAMED):
+    halo_products(tab, aff, hl, sums_h, 2.0)
+    for h in range(2 * NAMED):
         weight[h] = sums_h[h]
     for g in range(count):
         local = row_product(aff, tab, 0, g, hl)
@@ -305,13 +303,13 @@
         out[pl.ds(len(EARLY) + n, 1), :] = jnp.sum(total, axis=0, keepdims=True)
 
 
-def cross_kernel(weight, recv, gram, out):
+def cross_kernel(weight, recv_a, recv_b, gram, other, out):
     _, rows, width = weight.shape
     total = jnp.zeros((8, width), F32)
     for h in range(NAMED):
-        part = weight[h] * recv[h].astype(F32)
+        part = weight[h] * recv_a[h].astype(F32) + weight[NAMED + h] * recv_b[h].astype(F32)
         total = total + part.reshape(rows // 8, 8, width).sum(0)
-    value = gram[...]
+    value = gram[...] + other[...]
     extra = jnp.sum(total, axis=0, keepdims=True)
     index = lax.broadcasted_iota(jnp.int32, value.shape, 0)
     value = value + jnp.where(index == ROWS - 1, extra, 0.0)
@@ -364,7 +362,7 @@
         coef[k] = rest * inverse[k]
     coef = [coef[k] * scale[k] for k in range(n)]
     fields = (t0, t1, t2, t3, t4)
-    count, rows, width = t0.shape
+    count, rows, _ = t0.shape
     chunks = sems.shape[0]
     per = count // chunks
     copies = []
@@ -383,13 +381,13 @@
         copy.wait()
 
 
-def swap(block_a, block_b, axis):
+def to_chip_partner(block, axis):
+    return lax.ppermute(block, axis, [(i, i ^ 1) for i in range(lax.axis_size(axis))])
+
+
+def to_other_chip(block, axis):
     n = lax.axis_size(axis)
-    pairs_a = [(i, i ^ 1) for i in range(n)]
-    pairs_b = [(i, (i + 1) % n if i % 2 else (i - 1) % n) for i in range(n)]
-    got_b = lax.ppermute(block_b, axis, pairs_b)
-    got_a = lax.ppermute(block_a, axis, pairs_a)
-    return got_a, got_b
+    return lax.ppermute(block, axis, [(i, (i + 1) % n if i % 2 else (i - 1) % n) for i in range(n)])
 
 
 def shards(descriptors, queries, affinity, tile_col):
@@ -406,13 +404,12 @@
     half = jax.ShapeDtypeStruct((NAMED, rows, width), BF)
     early = jax.ShapeDtypeStruct((len(EARLY), width), F32)
     edge_sum = jax.ShapeDtypeStruct((2 * NAMED, rows, width), F32)
-    half_sum = jax.ShapeDtypeStruct((NAMED, rows, width), F32)
     sums_h = pltpu.VMEM((2 * NAMED + 1, rows, width), F32)
     work = [pltpu.VMEM((2 * NAMED + 1, rows, width), BF)]
     chunks = count // 2
     flops = 2 * count * rows * 4 * rows * 2 * width
 
-    def call(kernel, out_shape, products, scratch=(), aliases=None, name=None, limit=24):
+    def call(kernel, out_shape, products, scratch=(), aliases=None, limit=24):
         outs = out_shape if isinstance(out_shape, tuple) else (out_shape,)
 
         def run(*args):
@@ -432,24 +429,22 @@
                 cost_estimate=pl.CostEstimate(
                     flops=int(products * flops), bytes_accessed=4 << 20, transcendentals=0
                 ),
-                name=name,
             )(*args)
 
         return run
 
     operands = (descriptors, queries, affinity, tile_col.T)
-    t0, hl0, send_a, send_b, aff, tab = pl.pallas_call(
+    t0, hl0, send_b, aff, tab = pl.pallas_call(
         functools.partial(first_kernel, chunks=chunks, axis=axis),
         out_shape=(
             field,
             split,
             edge,
-            edge,
             jax.ShapeDtypeStruct(affinity.shape, BF),
             pltpu.SMEM((size,), jnp.int32),
         ),
         in_specs=[HBM] * 4,
-        out_specs=(VMEM,) * 5 + (SMEM,),
+        out_specs=(VMEM,) * 4 + (SMEM,),
         scratch_shapes=[
             pltpu.VMEM((chunks, count * rows // chunks, depth), BF),
             pltpu.VMEM((width, depth), BF),
@@ -463,50 +458,34 @@
         cost_estimate=pl.CostEstimate(flops=flops, bytes_accessed=4 << 20, transcendentals=0),
         name="first",
     )(*(pltpu.with_memory_space_constraint(x, pltpu.HBM) for x in operands))
-    recv_a, recv_b = swap(send_a, send_b, axis)
-    part, hl1, halo_part = call(
-        functools.partial(rest_kernel, step=0), (field, split, edge_sum), 1, [sums_h], name="rest0"
+    recv_b = to_other_chip(send_b, axis)
+    part, hl1, halo_part, send_a = call(
+        functools.partial(rest_kernel, step=0), (field, split, edge_sum, edge), 1, [sums_h]
     )(tab, aff, t0, hl0)
-    _, t1, t2, hl2, send_a, send_b = call(
-        middle_kernel,
-        (split, field, field, split, edge, edge),
-        2,
-        work,
-        {2: 0, 3: 1},
-        name="middle",
+    recv_a = to_chip_partner(send_a, axis)
+    _, t1, t2, hl2, send_b = call(
+        middle_kernel, (split, field, field, split, edge), 2, work, {2: 0, 3: 1}
     )(tab, aff, hl1, part, halo_part, recv_a, recv_b)
-    recv_a, recv_b = swap(send_a, send_b, axis)
-    part, hl3, halo_part, gram = call(
-        functools.partial(rest_kernel, step=2),
-        (field, split, edge_sum, early),
-        1,
-        [sums_h],
-        name="rest2",
-    )(tab, aff, t2, hl2, t0, t1)
-    _, t3, t4, hl4, send = call(
-        last_kernel,
-        (split, field, field, split, half),
-        2,
-        work,
-        {2: 0, 3: 1},
-        name="last",
+    recv_b = to_other_chip(send_b, axis)
+    part, hl3, halo_part, send_a = call(
+        functools.partial(rest_kernel, step=2), (field, split, edge_sum, edge), 1, [sums_h]
+    )(tab, aff, t2, hl2)
+    recv_a = to_chip_partner(send_a, axis)
+    gram = call(early_kernel, early, 0.1)(t0, t1, t2)
+    _, t3, t4, hl4, send_b = call(
+        last_kernel, (split, field, field, split, half), 2, work, {2: 0, 3: 1}
     )(tab, aff, hl3, part, halo_part, recv_a, recv_b)
-    recv = lax.ppermute(send, axis, [(i, (i - 1) % devices) for i in range(devices)])
-    gram, weight = call(
-        gram_kernel,
-        (jax.ShapeDtypeStruct((ROWS, width), F32), half_sum),
-        1,
-        [sums_h],
-        name="gram",
+    recv_b = to_other_chip(send_b, axis)
+    gram, weight, send_a = call(
+        gram_kernel, (jax.ShapeDtypeStruct((ROWS, width), F32), edge_sum, half), 1, [sums_h]
     )(tab, aff, t0, t1, t2, t3, t4, hl4, gram)
+    recv_a = to_chip_partner(send_a, axis)
+    other = to_chip_partner(gram, axis)
     parts = call(
-        cross_kernel,
-        jax.ShapeDtypeStruct((devices, ROWS, width), F32),
-        0.1,
-        name="cross",
-        limit=8,
-    )(weight, recv, gram)
-    parts = lax.all_to_all(parts, axis, 0, 0)
+        cross_kernel, jax.ShapeDtypeStruct((devices // 2, ROWS, width), F32), 0.1, limit=8
+    )(weight, recv_a, recv_b, gram, other)
+    groups = [list(range(core, devices, 2)) for core in range(2)]
+    parts = lax.all_to_all(parts, axis, 0, 0, axis_index_groups=groups)
     return pl.pallas_call(
         final_kernel,
         out_shape=jax.ShapeDtypeStruct((count * rows, width), F32),

time: 45 us -> 46.1 us (1.024)
  the two profiles are of different devices: /device:TPU:0 before, /device:TPU:1 now
where the time goes in v6:
time: 46.1 us; the launch traced here: 46 us
  starting transfers between devices  12.4 us (27%)
  blocking collectives  12.3 us (27%)
  Pallas kernels  11.4 us (25%)
  waiting for transfers between devices  9.71 us (21%)
    all_to_all x1, blocking collectives, shards(): parts = lax.all_to_all(parts, axis, 0, 0, axis_index_groups=groups)  12.3 us
    ppermute x4, starting transfers between devices, to_chip_partner(): lax.ppermute(block, axis, [(i, i ^ 1) for i in range(lax.axis_size(axis))])  9.3 us
    ppermute x3, waiting for transfers between devices, to_other_chip(): lax.ppermute(block, axis, [(i, (i + 1) % n if i % 2 else (i - 1) % n) for...  8.87 us
    pallas_call x7, Pallas kernels, run(): pl.pallas_call(kernel, out_shape=out_shape, in_specs=specs, out_specs=(VM...  6.91 us
    pallas_call x1, Pallas kernels, shards(): pl.pallas_call(functools.partial(first_kernel, chunks=chunks, axis=axis),...  3.31 us
    ppermute x3, starting transfers between devices, to_other_chip(): lax.ppermute(block, axis, [(i, (i + 1) % n if i % 2 else (i - 1) % n) for...  3.13 us
    pallas_call x1, Pallas kernels, shards(): pl.pallas_call(final_kernel, out_shape=jax.ShapeDtypeStruct((count * rows...  1.2 us
  transfers between devices with their start and end apart: 7, of which 3 were waited for; matrix products, arithmetic and copies ran while one was open for 0% of the time, Pallas kernels for 2%

profile of v6, /device:TPU:1, one launch (start us, length us, event | category | flops | bytes accessed | tf_op | source)
XLA Modules:
  0.0 46.0 jit_solution(2257662368269236321)
XLA Ops:
  0.0 3.3 %first.1 = (f32[12,128,128]{2,1,0:T(8,128)S(1)}, bf16[19,128,256]{2,1,0:T(8,128)(2,1)S(1)}, bf16[6,128,128]{2,1,0:T(8,128)(2,1)S(1)}, bf16[12,4,128,128]{3,2,1,0:T(8,128)(2,1)S(1)}, s32[128]{0:T(128)S(4)}) custom-call(bf16[1536,768]{1,0:T(8,128)(2,1)} %desc.1, bf16[128,768]{1,0:T(8,128)(2,1)} %queries.1, bf16[12,4,128,128]{3,2,1,0:T(8,128)(2,1)} %affinity.1, ...), custom_call_target="tpu_custom_call" | custom-call | flops 402653184 | bytes 4194304 | tf_op jit(solution)/shard_map/first/pallas_call | solution.py:437
  3.3 0.9 %shard_map.46 = (f32[12,128,128]{2,1,0:T(8,128)S(1)}, bf16[19,128,256]{2,1,0:T(8,128)(2,1)S(1)}, f32[6,128,128]{2,1,0:T(8,128)S(1)}, bf16[6,128,128]{2,1,0:T(8,128)(2,1)S(1)}) custom-call(s32[128]{0:T(128)S(4)} %get-tuple-element.29.tab, bf16[12,4,128,128]{3,2,1,0:T(8,128)(2,1)S(1)} %get-tuple-element.30.aff, f32[12,128,128]{2,1,0:T(8,128)S(1)} %get-tuple-element.31.t.t0, ...), custom_call_target="tpu_custom_call" | custom-call | flops 402653184 | bytes 4194304 | tf_op jit(solution)/shard_map/pallas_call | solution.py:421
  4.3 0.1 collective-permute-start
  4.3 2.7 %collective-permute-start.1 = (bf16[6,128,128]{2,1,0:T(8,128)(2,1)S(1)}, bf16[6,128,128]{2,1,0:T(8,128)(2,1)S(1)}, u32[]{:S(2)}, u32[]{:S(2)}) collective-permute-start(bf16[6,128,128]{2,1,0:T(8,128)(2,1)S(1)} %get-tuple-element.37), channel_id=1, source_target_pairs={{0,15},{1,2},{2,1},{3,4},{4,3},{5,6},{6,5},{7,8},{8,7},{9,10},{10,... | collective-permute-start | bytes 589832 | tf_op jit(solution)/shard_map/ppermute | solution.py:390
  7.0 0.0 collective-permute-done.recv_a
  7.0 4.7 %collective-permute-done.1.recv_b = bf16[6,128,128]{2,1,0:T(8,128)(2,1)S(1)} collective-permute-done((bf16[6,128,128]{2,1,0:T(8,128)(2,1)S(1)}, bf16[6,128,128]{2,1,0:T(8,128)(2,1)S(1)}, u32[]{:S(2)}, u32[]{:S(2)}) %collective-permute-start.1) | collective-permute-done | bytes 196640 | tf_op jit(solution)/shard_map/ppermute | solution.py:390
  11.7 1.3 %shard_map.47 = (bf16[19,128,256]{2,1,0:T(8,128)(2,1)S(1)}, f32[12,128,128]{2,1,0:T(8,128)S(1)}, f32[12,128,128]{2,1,0:T(8,128)S(1)}, bf16[19,128,256]{2,1,0:T(8,128)(2,1)S(1)}, bf16[6,128,128]{2,1,0:T(8,128)(2,1)S(1)}) custom-call(s32[128]{0:T(128)S(4)} %get-tuple-element.29.tab, ...), custom_call_target="tpu_custom_call", output_to_operand_aliasing={{0}: (2, {}), {1}: (3, {})} | custom-call | flops 805306368 | bytes 4194304 | tf_op jit(solution)/shard_map/pallas_call | solution.py:421
  13.1 1.0 %shard_map.48 = (f32[12,128,128]{2,1,0:T(8,128)S(1)}, bf16[19,128,256]{2,1,0:T(8,128)(2,1)S(1)}, f32[6,128,128]{2,1,0:T(8,128)S(1)}, bf16[6,128,128]{2,1,0:T(8,128)(2,1)S(1)}) custom-call(s32[128]{0:T(128)S(4)} %get-tuple-element.29.tab, bf16[12,4,128,128]{3,2,1,0:T(8,128)(2,1)S(1)} %get-tuple-element.30.aff, f32[12,128,128]{2,1,0:T(8,128)S(1)} %get-tuple-element.39.t.t2, ...), custom_call_target="tpu_custom_call" | custom-call | flops 402653184 | bytes 4194304 | tf_op jit(solution)/shard_map/pallas_call | solution.py:421
  14.0 2.2 %collective-permute-start.2 = (bf16[6,128,128]{2,1,0:T(8,128)(2,1)S(1)}, bf16[6,128,128]{2,1,0:T(8,128)(2,1)S(1)}, u32[]{:S(2)}, u32[]{:S(2)}) collective-permute-start(bf16[6,128,128]{2,1,0:T(8,128)(2,1)S(1)} %get-tuple-element.44), channel_id=1, source_target_pairs={{0,1},{1,0},{2,3},{3,2},{4,5},{5,4},{6,7},{7,6},{8,9},{9,8},{10,11... | collective-permute-start | bytes 589832 | tf_op jit(solution)/shard_map/ppermute | solution.py:385
  16.2 0.5 collective-permute-start.3
  16.7 0.8 %shard_map.50.early = f32[6,128]{1,0:T(8,128)S(1)} custom-call(f32[12,128,128]{2,1,0:T(8,128)S(1)} %get-tuple-element.31.t.t0, f32[12,128,128]{2,1,0:T(8,128)S(1)} %get-tuple-element.38.t1, f32[12,128,128]{2,1,0:T(8,128)S(1)} %get-tuple-element.39.t.t2), custom_call_target="tpu_custom_call" | custom-call | flops 40265320 | bytes 4194304 | tf_op jit(solution)/shard_map/pallas_call | solution.py:421
  17.5 0.0 collective-permute-done.2.recv_a
  17.5 4.1 %collective-permute-done.3.recv_b = bf16[6,128,128]{2,1,0:T(8,128)(2,1)S(1)} collective-permute-done((bf16[6,128,128]{2,1,0:T(8,128)(2,1)S(1)}, bf16[6,128,128]{2,1,0:T(8,128)(2,1)S(1)}, u32[]{:S(2)}, u32[]{:S(2)}) %collective-permute-start.3) | collective-permute-done | bytes 196640 | tf_op jit(solution)/shard_map/ppermute | solution.py:390
  21.6 1.0 %shard_map.49 = (bf16[19,128,256]{2,1,0:T(8,128)(2,1)S(1)}, f32[12,128,128]{2,1,0:T(8,128)S(1)}, f32[12,128,128]{2,1,0:T(8,128)S(1)}, bf16[19,128,256]{2,1,0:T(8,128)(2,1)S(1)}, bf16[3,128,128]{2,1,0:T(8,128)(2,1)S(1)}) custom-call(s32[128]{0:T(128)S(4)} %get-tuple-element.29.tab, ...), custom_call_target="tpu_custom_call", output_to_operand_aliasing={{0}: (2, {}), {1}: (3, {})} | custom-call | flops 805306368 | bytes 4194304 | tf_op jit(solution)/shard_map/pallas_call | solution.py:421
  22.6 1.9 %shard_map.51 = (f32[16,128]{1,0:T(8,128)S(1)}, f32[6,128,128]{2,1,0:T(8,128)S(1)}, bf16[3,128,128]{2,1,0:T(8,128)(2,1)S(1)}) custom-call(s32[128]{0:T(128)S(4)} %get-tuple-element.29.tab, bf16[12,4,128,128]{3,2,1,0:T(8,128)(2,1)S(1)} %get-tuple-element.30.aff, f32[12,128,128]{2,1,0:T(8,128)S(1)} %get-tuple-element.31.t.t0, ...), custom_call_target="tpu_custom_call" | custom-call | flops 402653184 | bytes 4194304 | tf_op jit(solution)/shard_map/pallas_call | solution.py:421
  24.5 2.6 %collective-permute-start.4 = (bf16[3,128,128]{2,1,0:T(8,128)(2,1)S(1)}, bf16[3,128,128]{2,1,0:T(8,128)(2,1)S(1)}, u32[]{:S(2)}, u32[]{:S(2)}) collective-permute-start(bf16[3,128,128]{2,1,0:T(8,128)(2,1)S(1)} %get-tuple-element.50), channel_id=1, source_target_pairs={{0,1},{1,0},{2,3},{3,2},{4,5},{5,4},{6,7},{7,6},{8,9},{9,8},{10,11... | collective-permute-start | bytes 294920 | tf_op jit(solution)/shard_map/ppermute | solution.py:385
  27.0 0.0 collective-permute-start.5
  27.0 4.5 %collective-permute-start.6 = (f32[16,128]{1,0:T(8,128)S(1)}, f32[16,128]{1,0:T(8,128)S(1)}, u32[]{:S(2)}, u32[]{:S(2)}) collective-permute-start(f32[16,128]{1,0:T(8,128)S(1)} %get-tuple-element.52.gram), channel_id=1, source_target_pairs={{0,1},{1,0},{2,3},{3,2},{4,5},{5,4},{6,7},{7,6},{8,9},{9,8},{10,11... | collective-permute-start | bytes 24584 | tf_op jit(solution)/shard_map/ppermute | solution.py:385
  31.5 0.8 %collective-permute-done.6.other = f32[16,128]{1,0:T(8,128)S(1)} collective-permute-done((f32[16,128]{1,0:T(8,128)S(1)}, f32[16,128]{1,0:T(8,128)S(1)}, u32[]{:S(2)}, u32[]{:S(2)}) %collective-permute-start.6) | collective-permute-done | bytes 8224 | tf_op jit(solution)/shard_map/ppermute | solution.py:385
  32.4 0.0 collective-permute-done.4.recv_a
  32.4 0.0 collective-permute-done.5.recv_b
  32.4 0.1 shard_map.52
  32.4 12.3 %all_to_all.5.parts = f32[8,16,128]{2,1,0:T(8,128)S(1)} all-to-all(f32[8,16,128]{2,1,0:T(8,128)S(1)} %shard_map.52), channel_id=1, replica_groups={{0,2,4,6,8,10,12,14},{1,3,5,7,9,11,13,15},{16,18,20,22,24,26,28,30},{17..., dimensions={0} | all-to-all | bytes 131072 | tf_op jit(solution)/shard_map/all_to_all | solution.py:488
  44.8 1.2 %final.1 = f32[1536,128]{1,0:T(8,128)} custom-call(f32[8,16,128]{2,1,0:T(8,128)S(1)} %all_to_all.5.parts, f32[12,128,128]{2,1,0:T(8,128)S(1)} %get-tuple-element.31.t.t0, f32[12,128,128]{2,1,0:T(8,128)S(1)} %get-tuple-element.38.t1, f32[12,128,128]{2,1,0:T(8,128)S(1)} %get-tuple-element.39.t.t2, f32[12,128,128]{2,1,0:T(8,128)S(1)} %get-tuple-element.46.t3, ...), custom_call_target="tpu_custom_call" | custom-call | tf_op jit(solution)/shard_map/final/pallas_call | solution.py:489
Async XLA Ops:
  4.3 2.8 %collective-permute-start = (bf16[6,128,128]{2,1,0:T(8,128)(2,1)S(1)}, bf16[6,128,128]{2,1,0:T(8,128)(2,1)S(1)}, u32[]{:S(2)}, u32[]{:S(2)}) collective-permute-start(bf16[6,128,128]{2,1,0:T(8,128)(2,1)S(1)} %get-tuple-element.36), channel_id=1, source_target_pairs={{0,1},{1,0},{2,3},{3,2},{4,5},{5,4},{6,7},{7,6},{8,9},{9,8},{10,11... | collective-permute-start | bytes 589832 | tf_op jit(solution)/shard_map/ppermute | solution.py:385
  4.3 7.4 %collective-permute-start.1 = (bf16[6,128,128]{2,1,0:T(8,128)(2,1)S(1)}, bf16[6,128,128]{2,1,0:T(8,128)(2,1)S(1)}, u32[]{:S(2)}, u32[]{:S(2)}) collective-permute-start(bf16[6,128,128]{2,1,0:T(8,128)(2,1)S(1)} %get-tuple-element.37), channel_id=1, source_target_pairs={{0,15},{1,2},{2,1},{3,4},{4,3},{5,6},{6,5},{7,8},{8,7},{9,10},{10,... | collective-permute-start | bytes 589832 | tf_op jit(solution)/shard_map/ppermute | solution.py:390
  14.0 3.4 %collective-permute-start.2 = (bf16[6,128,128]{2,1,0:T(8,128)(2,1)S(1)}, bf16[6,128,128]{2,1,0:T(8,128)(2,1)S(1)}, u32[]{:S(2)}, u32[]{:S(2)}) collective-permute-start(bf16[6,128,128]{2,1,0:T(8,128)(2,1)S(1)} %get-tuple-element.44), channel_id=1, source_target_pairs={{0,1},{1,0},{2,3},{3,2},{4,5},{5,4},{6,7},{7,6},{8,9},{9,8},{10,11... | collective-permute-start | bytes 589832 | tf_op jit(solution)/shard_map/ppermute | solution.py:385
  16.2 5.4 %collective-permute-start.3 = (bf16[6,128,128]{2,1,0:T(8,128)(2,1)S(1)}, bf16[6,128,128]{2,1,0:T(8,128)(2,1)S(1)}, u32[]{:S(2)}, u32[]{:S(2)}) collective-permute-start(bf16[6,128,128]{2,1,0:T(8,128)(2,1)S(1)} %get-tuple-element.45), channel_id=1, source_target_pairs={{0,15},{1,2},{2,1},{3,4},{4,3},{5,6},{6,5},{7,8},{8,7},{9,10},{10,... | collective-permute-start | bytes 589832 | tf_op jit(solution)/shard_map/ppermute | solution.py:390
  24.5 7.9 %collective-permute-start.4 = (bf16[3,128,128]{2,1,0:T(8,128)(2,1)S(1)}, bf16[3,128,128]{2,1,0:T(8,128)(2,1)S(1)}, u32[]{:S(2)}, u32[]{:S(2)}) collective-permute-start(bf16[3,128,128]{2,1,0:T(8,128)(2,1)S(1)} %get-tuple-element.50), channel_id=1, source_target_pairs={{0,1},{1,0},{2,3},{3,2},{4,5},{5,4},{6,7},{7,6},{8,9},{9,8},{10,11... | collective-permute-start | bytes 294920 | tf_op jit(solution)/shard_map/ppermute | solution.py:385
  27.0 5.3 %collective-permute-start.5 = (bf16[3,128,128]{2,1,0:T(8,128)(2,1)S(1)}, bf16[3,128,128]{2,1,0:T(8,128)(2,1)S(1)}, u32[]{:S(2)}, u32[]{:S(2)}) collective-permute-start(bf16[3,128,128]{2,1,0:T(8,128)(2,1)S(1)} %get-tuple-element.51), channel_id=1, source_target_pairs={{0,15},{1,2},{2,1},{3,4},{4,3},{5,6},{6,5},{7,8},{8,7},{9,10},{10,... | collective-permute-start | bytes 294920 | tf_op jit(solution)/shard_map/ppermute | solution.py:390
  27.0 5.3 %collective-permute-start.6 = (f32[16,128]{1,0:T(8,128)S(1)}, f32[16,128]{1,0:T(8,128)S(1)}, u32[]{:S(2)}, u32[]{:S(2)}) collective-permute-start(f32[16,128]{1,0:T(8,128)S(1)} %get-tuple-element.52.gram), channel_id=1, source_target_pairs={{0,1},{1,0},{2,3},{3,2},{4,5},{5,4},{6,7},{7,6},{8,9},{9,8},{10,11... | collective-permute-start | bytes 24584 | tf_op jit(solution)/shard_map/ppermute | solution.py:385

commit v7 on v6

--- a/solution.py
+++ b/solution.py
@@ -268,20 +268,38 @@
         put_split(hl2, g, value)
 
 
-def middle_kernel(
-    tab, aff, _, __, halo_part, recv_a, recv_b, hl1, t1, t2, hl2, send_b, halo
-):
+def middle_kernel(tab, aff, *refs, parity, axis):
+    halo_part, recv_a, recv_b = refs[-9:-6]
+    hl1, t1, t2, hl2, send_b, halo = refs[-6:]
     _, lists, _, _ = offsets(t1.shape[0])
-    two_steps(tab, aff, hl1, t1, halo_part, recv_a, recv_b, t2, hl2, halo, 0)
-    pack(tab, SHIFTS[2], aff, t2, hl2, send_b, lists + NAMED)
-
-
-def last_kernel(tab, aff, _, __, halo_part, recv_a, recv_b, hl3, t3, t4, hl4, send, halo):
-    count, _, width = t3.shape
-    _, lists, _, _ = offsets(count)
-    two_steps(tab, aff, hl3, t3, halo_part, recv_a, recv_b, t4, hl4, halo, 2)
-    for j in range(NAMED):
-        send[j] = hl4[tab[lists + NAMED + j], :, :width]
+    active = lax.rem(lax.axis_index(axis), 2) == parity
+
+    @pl.when(active)
+    def _():
+        two_steps(tab, aff, hl1, t1, halo_part, recv_a, recv_b, t2, hl2, halo, 0)
+        pack(tab, SHIFTS[2], aff, t2, hl2, send_b, lists + NAMED)
+
+    @pl.when(jnp.logical_not(active))
+    def _():
+        send_b[...] = jnp.zeros(send_b.shape, BF)
+
+
+def last_kernel(tab, aff, *refs, parity, axis):
+    halo_part, recv_a, recv_b = refs[-9:-6]
+    hl3, t3, t4, hl4, send_b, halo = refs[-6:]
+    width = t3.shape[2]
+    _, lists, _, _ = offsets(t3.shape[0])
+    active = lax.rem(lax.axis_index(axis), 2) == parity
+
+    @pl.when(active)
+    def _():
+        two_steps(tab, aff, hl3, t3, halo_part, recv_a, recv_b, t4, hl4, halo, 2)
+        for j in range(NAMED):
+            send_b[j] = hl4[tab[lists + NAMED + j], :, :width]
+
+    @pl.when(jnp.logical_not(active))
+    def _():
+        send_b[...] = jnp.zeros(send_b.shape, BF)
 
 
 def gram_kernel(tab, aff, t0, t1, t2, t3, t4, hl, early, out, weight, send_a, sums_h):
@@ -303,8 +321,18 @@
         out[pl.ds(len(EARLY) + n, 1), :] = jnp.sum(total, axis=0, keepdims=True)
 
 
-def cross_kernel(weight, recv_a, recv_b, gram, other, out):
+def cross_kernel(weight, recv_a, recv_even, recv_odd, gram, other, out, recv_b, *, axis):
     _, rows, width = weight.shape
+    even = lax.rem(lax.axis_index(axis), 2) == 0
+
+    @pl.when(even)
+    def _():
+        recv_b[...] = recv_even[...]
+
+    @pl.when(jnp.logical_not(even))
+    def _():
+        recv_b[...] = recv_odd[...]
+
     total = jnp.zeros((8, width), F32)
     for h in range(NAMED):
         part = weight[h] * recv_a[h].astype(F32) + weight[NAMED + h] * recv_b[h].astype(F32)
@@ -385,9 +413,9 @@
     return lax.ppermute(block, axis, [(i, i ^ 1) for i in range(lax.axis_size(axis))])
 
 
-def to_other_chip(block, axis):
+def shift(block, by, axis):
     n = lax.axis_size(axis)
-    return lax.ppermute(block, axis, [(i, (i + 1) % n if i % 2 else (i - 1) % n) for i in range(n)])
+    return lax.ppermute(block, axis, [(i, (i + by) % n) for i in range(n)])
 
 
 def shards(descriptors, queries, affinity, tile_col):
@@ -458,32 +486,56 @@
         cost_estimate=pl.CostEstimate(flops=flops, bytes_accessed=4 << 20, transcendentals=0),
         name="first",
     )(*(pltpu.with_memory_space_constraint(x, pltpu.HBM) for x in operands))
-    recv_b = to_other_chip(send_b, axis)
+    recv_even = shift(send_b, 1, axis)
+    recv_odd = shift(send_b, -1, axis)
     part, hl1, halo_part, send_a = call(
         functools.partial(rest_kernel, step=0), (field, split, edge_sum, edge), 1, [sums_h]
     )(tab, aff, t0, hl0)
     recv_a = to_chip_partner(send_a, axis)
-    _, t1, t2, hl2, send_b = call(
-        middle_kernel, (split, field, field, split, edge), 2, work, {2: 0, 3: 1}
-    )(tab, aff, hl1, part, halo_part, recv_a, recv_b)
-    recv_b = to_other_chip(send_b, axis)
+
+    def by_parity(kernel, parity, edges, aliased):
+        fields = (split, field, field, split)
+        return call(
+            functools.partial(kernel, parity=parity, axis=axis),
+            fields + (edges,),
+            2,
+            work,
+            {2 + i: i for i in range(aliased)},
+        )
+
+    hl1, t1, t2, hl2, send = by_parity(middle_kernel, 0, edge, 2)(
+        tab, aff, hl1, part, halo_part, recv_a, recv_even
+    )
+    got_odd = shift(send, -1, axis)
+    hl1, t1, t2, hl2, send = by_parity(middle_kernel, 1, edge, 4)(
+        tab, aff, hl1, t1, t2, hl2, halo_part, recv_a, recv_odd
+    )
+    got_even = shift(send, 1, axis)
     part, hl3, halo_part, send_a = call(
         functools.partial(rest_kernel, step=2), (field, split, edge_sum, edge), 1, [sums_h]
     )(tab, aff, t2, hl2)
     recv_a = to_chip_partner(send_a, axis)
     gram = call(early_kernel, early, 0.1)(t0, t1, t2)
-    _, t3, t4, hl4, send_b = call(
-        last_kernel, (split, field, field, split, half), 2, work, {2: 0, 3: 1}
-    )(tab, aff, hl3, part, halo_part, recv_a, recv_b)
-    recv_b = to_other_chip(send_b, axis)
+    hl3, t3, t4, hl4, send = by_parity(last_kernel, 1, half, 2)(
+        tab, aff, hl3, part, halo_part, recv_a, got_odd
+    )
+    recv_even = shift(send, 1, axis)
+    hl3, t3, t4, hl4, send = by_parity(last_kernel, 0, half, 4)(
+        tab, aff, hl3, t3, t4, hl4, halo_part, recv_a, got_even
+    )
+    recv_odd = shift(send, -1, axis)
     gram, weight, send_a = call(
         gram_kernel, (jax.ShapeDtypeStruct((ROWS, width), F32), edge_sum, half), 1, [sums_h]
     )(tab, aff, t0, t1, t2, t3, t4, hl4, gram)
     recv_a = to_chip_partner(send_a, axis)
     other = to_chip_partner(gram, axis)
     parts = call(
-        cross_kernel, jax.ShapeDtypeStruct((devices // 2, ROWS, width), F32), 0.1, limit=8
-    )(weight, recv_a, recv_b, gram, other)
+        functools.partial(cross_kernel, axis=axis),
+        jax.ShapeDtypeStruct((devices // 2, ROWS, width), F32),
+        0.1,
+        [pltpu.VMEM((NAMED, rows, width), BF)],
+        limit=8,
+    )(weight, recv_a, recv_even, recv_odd, gram, other)
     groups = [list(range(core, devices, 2)) for core in range(2)]
     parts = lax.all_to_all(parts, axis, 0, 0, axis_index_groups=groups)
     return pl.pallas_call(

time: 46.1 us -> 50.5 us (1.095)
  starting transfers between devices: 12.4 us -> 15.8 us
  waiting for transfers between devices: 9.71 us -> 10.7 us
    ppermute x3 -> x6, starting transfers between devices: 3.13 us -> 4.97 us  [shift(): return lax.ppermute(block, axis, [(i, (i + by) % n) for i in range(n)])]
    ppermute x4, starting transfers between devices: 9.3 us -> 10.8 us  [to_chip_partner(): lax.ppermute(block, axis, [(i, i ^ 1) for i in range(lax.axis_size(axis))])]
    ppermute x3 -> x6, waiting for transfers between devices: 8.87 us -> 9.87 us  [shift(): return lax.ppermute(block, axis, [(i, (i + by) % n) for i in range(n)])]
    pallas_call x7 -> x9, Pallas kernels: 6.91 us -> 6.96 us  [run(): pl.pallas_call(kernel, out_shape=out_shape, in_specs=specs, out_specs=(VM...]
  transfers between devices with their start and end apart: 7 -> 10, of which waited for: 3 -> 5; matrix products, arithmetic and copies ran while one was open for 0% -> 0% of each run, Pallas kernels for 2% -> 4%
where the time goes in v7:
time: 50.5 us; the launch traced here: 50.3 us
  starting transfers between devices  15.8 us (31%)
  blocking collectives  12.3 us (24%)
  Pallas kernels  11.4 us (23%)
  waiting for transfers between devices  10.7 us (21%)
    all_to_all x1, blocking collectives, shards(): parts = lax.all_to_all(parts, axis, 0, 0, axis_index_groups=groups)  12.3 us
    ppermute x4, starting transfers between devices, to_chip_partner(): lax.ppermute(block, axis, [(i, i ^ 1) for i in range(lax.axis_size(axis))])  10.8 us
    ppermute x6, waiting for transfers between devices, shift(): return lax.ppermute(block, axis, [(i, (i + by) % n) for i in range(n)])  9.87 us
    pallas_call x9, Pallas kernels, run(): pl.pallas_call(kernel, out_shape=out_shape, in_specs=specs, out_specs=(VM...  6.96 us
    ppermute x6, starting transfers between devices, shift(): return lax.ppermute(block, axis, [(i, (i + by) % n) for i in range(n)])  4.97 us
    pallas_call x1, Pallas kernels, shards(): pl.pallas_call(functools.partial(first_kernel, chunks=chunks, axis=axis),...  3.31 us
    pallas_call x1, Pallas kernels, shards(): pl.pallas_call(final_kernel, out_shape=jax.ShapeDtypeStruct((count * rows...  1.14 us
  transfers between devices with their start and end apart: 10, of which 5 were waited for; matrix products, arithmetic and copies ran while one was open for 0% of the time, Pallas kernels for 4%

profile of v7, /device:TPU:1, one launch (start us, length us, event | category | flops | bytes accessed | tf_op | source)
XLA Modules:
  0.0 50.3 jit_solution(7058486088877330661)
XLA Ops:
  0.0 3.3 %first.1 = (f32[12,128,128]{2,1,0:T(8,128)S(1)}, bf16[19,128,256]{2,1,0:T(8,128)(2,1)S(1)}, bf16[6,128,128]{2,1,0:T(8,128)(2,1)S(1)}, bf16[12,4,128,128]{3,2,1,0:T(8,128)(2,1)S(1)}, s32[128]{0:T(128)S(4)}) custom-call(bf16[1536,768]{1,0:T(8,128)(2,1)} %desc.1, bf16[128,768]{1,0:T(8,128)(2,1)} %queries.1, bf16[12,4,128,128]{3,2,1,0:T(8,128)(2,1)} %affinity.1, ...), custom_call_target="tpu_custom_call" | custom-call | flops 402653184 | bytes 4194304 | tf_op jit(solution)/shard_map/first/pallas_call | solution.py:465
  3.3 0.9 %shard_map.46 = (f32[12,128,128]{2,1,0:T(8,128)S(1)}, bf16[19,128,256]{2,1,0:T(8,128)(2,1)S(1)}, f32[6,128,128]{2,1,0:T(8,128)S(1)}, bf16[6,128,128]{2,1,0:T(8,128)(2,1)S(1)}) custom-call(s32[128]{0:T(128)S(4)} %get-tuple-element.39.tab, bf16[12,4,128,128]{3,2,1,0:T(8,128)(2,1)S(1)} %get-tuple-element.40.aff, f32[12,128,128]{2,1,0:T(8,128)S(1)} %get-tuple-element.41.t.t0, ...), custom_call_target="tpu_custom_call" | custom-call | flops 402653184 | bytes 4194304 | tf_op jit(solution)/shard_map/pallas_call | solution.py:449
  4.3 0.1 collective-permute-start
  4.3 2.7 %collective-permute-start.1 = (bf16[6,128,128]{2,1,0:T(8,128)(2,1)S(1)}, bf16[6,128,128]{2,1,0:T(8,128)(2,1)S(1)}, u32[]{:S(2)}, u32[]{:S(2)}) collective-permute-start(bf16[6,128,128]{2,1,0:T(8,128)(2,1)S(1)} %get-tuple-element.47), channel_id=1, source_target_pairs={{0,1},{1,2},{2,3},{3,4},{4,5},{5,6},{6,7},{7,8},{8,9},{9,10},{10,1... | collective-permute-start | bytes 589832 | tf_op jit(solution)/shard_map/ppermute | solution.py:418
  7.0 0.0 collective-permute-done.refs_3_.refs_5_
  7.0 2.6 %collective-permute-done.1.refs_4_ = bf16[6,128,128]{2,1,0:T(8,128)(2,1)S(1)} collective-permute-done((bf16[6,128,128]{2,1,0:T(8,128)(2,1)S(1)}, bf16[6,128,128]{2,1,0:T(8,128)(2,1)S(1)}, u32[]{:S(2)}, u32[]{:S(2)}) %collective-permute-start.1) | collective-permute-done | bytes 196640 | tf_op jit(solution)/shard_map/ppermute | solution.py:418
  9.6 4.6 %collective-permute-done.2.refs_6_ = bf16[6,128,128]{2,1,0:T(8,128)(2,1)S(1)} collective-permute-done((bf16[6,128,128]{2,1,0:T(8,128)(2,1)S(1)}, bf16[6,128,128]{2,1,0:T(8,128)(2,1)S(1)}, u32[]{:S(2)}, u32[]{:S(2)}) %collective-permute-start.2) | collective-permute-done | bytes 196640 | tf_op jit(solution)/shard_map/ppermute | solution.py:418
  14.2 1.3 %shard_map.48 = (bf16[19,128,256]{2,1,0:T(8,128)(2,1)S(1)}, f32[12,128,128]{2,1,0:T(8,128)S(1)}, f32[12,128,128]{2,1,0:T(8,128)S(1)}, bf16[19,128,256]{2,1,0:T(8,128)(2,1)S(1)}, bf16[6,128,128]{2,1,0:T(8,128)(2,1)S(1)}) custom-call(s32[128]{0:T(128)S(4)} %get-tuple-element.39.tab, ...), custom_call_target="tpu_custom_call", output_to_operand_aliasing={{0}: (2, {}), {1}: (3, {}), {2}: (4, {}), {3}: (5, {})} | custom-call | flops 805306368 | bytes 4194304 | tf_op jit(solution)/shard_map/pallas_call | solution.py:449
  15.5 1.0 %shard_map.49 = (f32[12,128,128]{2,1,0:T(8,128)S(1)}, bf16[19,128,256]{2,1,0:T(8,128)(2,1)S(1)}, f32[6,128,128]{2,1,0:T(8,128)S(1)}, bf16[6,128,128]{2,1,0:T(8,128)(2,1)S(1)}) custom-call(s32[128]{0:T(128)S(4)} %get-tuple-element.39.tab, bf16[12,4,128,128]{3,2,1,0:T(8,128)(2,1)S(1)} %get-tuple-element.40.aff, f32[12,128,128]{2,1,0:T(8,128)S(1)} %get-tuple-element.53.t.t2, ...), custom_call_target="tpu_custom_call" | custom-call | flops 402653184 | bytes 4194304 | tf_op jit(solution)/shard_map/pallas_call | solution.py:449
  16.5 0.1 collective-permute-start.3
  16.6 0.5 collective-permute-start.4
  17.1 1.3 %collective-permute-start.5 = (bf16[6,128,128]{2,1,0:T(8,128)(2,1)S(1)}, bf16[6,128,128]{2,1,0:T(8,128)(2,1)S(1)}, u32[]{:S(2)}, u32[]{:S(2)}) collective-permute-start(bf16[6,128,128]{2,1,0:T(8,128)(2,1)S(1)} %get-tuple-element.64), channel_id=1, source_target_pairs={{0,1},{1,2},{2,3},{3,4},{4,5},{5,6},{6,7},{7,8},{8,9},{9,10},{10,1... | collective-permute-start | bytes 589832 | tf_op jit(solution)/shard_map/ppermute | solution.py:418
  18.4 0.8 %shard_map.52.early = f32[6,128]{1,0:T(8,128)S(1)} custom-call(f32[12,128,128]{2,1,0:T(8,128)S(1)} %get-tuple-element.41.t.t0, f32[12,128,128]{2,1,0:T(8,128)S(1)} %get-tuple-element.52.t1, f32[12,128,128]{2,1,0:T(8,128)S(1)} %get-tuple-element.53.t.t2), custom_call_target="tpu_custom_call" | custom-call | flops 40265320 | bytes 4194304 | tf_op jit(solution)/shard_map/pallas_call | solution.py:449
  19.2 2.6 %collective-permute-done.4.refs_4_ = bf16[6,128,128]{2,1,0:T(8,128)(2,1)S(1)} collective-permute-done((bf16[6,128,128]{2,1,0:T(8,128)(2,1)S(1)}, bf16[6,128,128]{2,1,0:T(8,128)(2,1)S(1)}, u32[]{:S(2)}, u32[]{:S(2)}) %collective-permute-start.4) | collective-permute-done | bytes 196640 | tf_op jit(solution)/shard_map/ppermute | solution.py:418
  21.7 1.0 %shard_map.50 = (bf16[19,128,256]{2,1,0:T(8,128)(2,1)S(1)}, f32[12,128,128]{2,1,0:T(8,128)S(1)}, f32[12,128,128]{2,1,0:T(8,128)S(1)}, bf16[19,128,256]{2,1,0:T(8,128)(2,1)S(1)}, bf16[3,128,128]{2,1,0:T(8,128)(2,1)S(1)}) custom-call(s32[128]{0:T(128)S(4)} %get-tuple-element.39.tab, ...), custom_call_target="tpu_custom_call", output_to_operand_aliasing={{0}: (2, {}), {1}: (3, {})} | custom-call | flops 805306368 | bytes 4194304 | tf_op jit(solution)/shard_map/pallas_call | solution.py:449
  22.7 0.1 collective-permute-done.5.refs_6_
  22.9 1.9 %shard_map.53 = (f32[16,128]{1,0:T(8,128)S(1)}, f32[6,128,128]{2,1,0:T(8,128)S(1)}, bf16[3,128,128]{2,1,0:T(8,128)(2,1)S(1)}) custom-call(s32[128]{0:T(128)S(4)} %get-tuple-element.39.tab, bf16[12,4,128,128]{3,2,1,0:T(8,128)(2,1)S(1)} %get-tuple-element.40.aff, f32[12,128,128]{2,1,0:T(8,128)S(1)} %get-tuple-element.41.t.t0, ...), custom_call_target="tpu_custom_call" | custom-call | flops 402653184 | bytes 4194304 | tf_op jit(solution)/shard_map/pallas_call | solution.py:449
  24.8 6.7 %collective-permute-start.6 = (bf16[3,128,128]{2,1,0:T(8,128)(2,1)S(1)}, bf16[3,128,128]{2,1,0:T(8,128)(2,1)S(1)}, u32[]{:S(2)}, u32[]{:S(2)}) collective-permute-start(bf16[3,128,128]{2,1,0:T(8,128)(2,1)S(1)} %get-tuple-element.69), channel_id=1, source_target_pairs={{0,1},{1,0},{2,3},{3,2},{4,5},{5,4},{6,7},{7,6},{8,9},{9,8},{10,11... | collective-permute-start | bytes 294920 | tf_op jit(solution)/shard_map/ppermute | solution.py:413
  31.4 0.5 %collective-permute-start.8 = (bf16[3,128,128]{2,1,0:T(8,128)(2,1)S(1)}, bf16[3,128,128]{2,1,0:T(8,128)(2,1)S(1)}, u32[]{:S(2)}, u32[]{:S(2)}) collective-permute-start(bf16[3,128,128]{2,1,0:T(8,128)(2,1)S(1)} %get-tuple-element.71), channel_id=1, source_target_pairs={{0,15},{1,0},{2,1},{3,2},{4,3},{5,4},{6,5},{7,6},{8,7},{9,8},{10,9... | collective-permute-start | bytes 294920 | tf_op jit(solution)/shard_map/ppermute | solution.py:418
  31.9 4.0 %collective-permute-start.9 = (f32[16,128]{1,0:T(8,128)S(1)}, f32[16,128]{1,0:T(8,128)S(1)}, u32[]{:S(2)}, u32[]{:S(2)}) collective-permute-start(f32[16,128]{1,0:T(8,128)S(1)} %get-tuple-element.72.gram), channel_id=1, source_target_pairs={{0,1},{1,0},{2,3},{3,2},{4,5},{5,4},{6,7},{7,6},{8,9},{9,8},{10,11... | collective-permute-start | bytes 24584 | tf_op jit(solution)/shard_map/ppermute | solution.py:413
  35.9 0.8 %collective-permute-done.9.other = f32[16,128]{1,0:T(8,128)S(1)} collective-permute-done((f32[16,128]{1,0:T(8,128)S(1)}, f32[16,128]{1,0:T(8,128)S(1)}, u32[]{:S(2)}, u32[]{:S(2)}) %collective-permute-start.9) | collective-permute-done | bytes 8224 | tf_op jit(solution)/shard_map/ppermute | solution.py:413
  36.8 0.1 shard_map.54
  36.9 12.3 %all_to_all.5.parts = f32[8,16,128]{2,1,0:T(8,128)S(1)} all-to-all(f32[8,16,128]{2,1,0:T(8,128)S(1)} %shard_map.54), channel_id=1, replica_groups={{0,2,4,6,8,10,12,14},{1,3,5,7,9,11,13,15},{16,18,20,22,24,26,28,30},{17..., dimensions={0} | all-to-all | bytes 131072 | tf_op jit(solution)/shard_map/all_to_all | solution.py:540
  49.2 1.1 %final.1 = f32[1536,128]{1,0:T(8,128)} custom-call(f32[8,16,128]{2,1,0:T(8,128)S(1)} %all_to_all.5.parts, f32[12,128,128]{2,1,0:T(8,128)S(1)} %get-tuple-element.41.t.t0, f32[12,128,128]{2,1,0:T(8,128)S(1)} %get-tuple-element.52.t1, f32[12,128,128]{2,1,0:T(8,128)S(1)} %get-tuple-element.53.t.t2, f32[12,128,128]{2,1,0:T(8,128)S(1)} %get-tuple-element.65.t3, ...), custom_call_target="tpu_custom_call" | custom-call | tf_op jit(solution)/shard_map/final/pallas_call | solution.py:541
  (8 shorter events, 0.1 us)
Async XLA Ops:
  4.3 2.8 %collective-permute-start = (bf16[6,128,128]{2,1,0:T(8,128)(2,1)S(1)}, bf16[6,128,128]{2,1,0:T(8,128)(2,1)S(1)}, u32[]{:S(2)}, u32[]{:S(2)}) collective-permute-start(bf16[6,128,128]{2,1,0:T(8,128)(2,1)S(1)} %get-tuple-element.46), channel_id=1, source_target_pairs={{0,1},{1,0},{2,3},{3,2},{4,5},{5,4},{6,7},{7,6},{8,9},{9,8},{10,11... | collective-permute-start | bytes 589832 | tf_op jit(solution)/shard_map/ppermute | solution.py:413
  4.3 5.3 %collective-permute-start.1 = (bf16[6,128,128]{2,1,0:T(8,128)(2,1)S(1)}, bf16[6,128,128]{2,1,0:T(8,128)(2,1)S(1)}, u32[]{:S(2)}, u32[]{:S(2)}) collective-permute-start(bf16[6,128,128]{2,1,0:T(8,128)(2,1)S(1)} %get-tuple-element.47), channel_id=1, source_target_pairs={{0,1},{1,2},{2,3},{3,4},{4,5},{5,6},{6,7},{7,8},{8,9},{9,10},{10,1... | collective-permute-start | bytes 589832 | tf_op jit(solution)/shard_map/ppermute | solution.py:418
  7.0 7.2 %collective-permute-start.2 = (bf16[6,128,128]{2,1,0:T(8,128)(2,1)S(1)}, bf16[6,128,128]{2,1,0:T(8,128)(2,1)S(1)}, u32[]{:S(2)}, u32[]{:S(2)}) collective-permute-start(bf16[6,128,128]{2,1,0:T(8,128)(2,1)S(1)} %get-tuple-element.47), channel_id=1, source_target_pairs={{0,15},{1,0},{2,1},{3,2},{4,3},{5,4},{6,5},{7,6},{8,7},{9,8},{10,9... | collective-permute-start | bytes 589832 | tf_op jit(solution)/shard_map/ppermute | solution.py:418
  16.5 2.7 %collective-permute-start.3 = (bf16[6,128,128]{2,1,0:T(8,128)(2,1)S(1)}, bf16[6,128,128]{2,1,0:T(8,128)(2,1)S(1)}, u32[]{:S(2)}, u32[]{:S(2)}) collective-permute-start(bf16[6,128,128]{2,1,0:T(8,128)(2,1)S(1)} %get-tuple-element.58), channel_id=1, source_target_pairs={{0,1},{1,0},{2,3},{3,2},{4,5},{5,4},{6,7},{7,6},{8,9},{9,8},{10,11... | collective-permute-start | bytes 589832 | tf_op jit(solution)/shard_map/ppermute | solution.py:413
  16.6 5.1 %collective-permute-start.4 = (bf16[6,128,128]{2,1,0:T(8,128)(2,1)S(1)}, bf16[6,128,128]{2,1,0:T(8,128)(2,1)S(1)}, u32[]{:S(2)}, u32[]{:S(2)}) collective-permute-start(bf16[6,128,128]{2,1,0:T(8,128)(2,1)S(1)} %get-tuple-element.59), channel_id=1, source_target_pairs={{0,15},{1,0},{2,1},{3,2},{4,3},{5,4},{6,5},{7,6},{8,7},{9,8},{10,9... | collective-permute-start | bytes 589832 | tf_op jit(solution)/shard_map/ppermute | solution.py:418
  17.1 5.8 %collective-permute-start.5 = (bf16[6,128,128]{2,1,0:T(8,128)(2,1)S(1)}, bf16[6,128,128]{2,1,0:T(8,128)(2,1)S(1)}, u32[]{:S(2)}, u32[]{:S(2)}) collective-permute-start(bf16[6,128,128]{2,1,0:T(8,128)(2,1)S(1)} %get-tuple-element.64), channel_id=1, source_target_pairs={{0,1},{1,2},{2,3},{3,4},{4,5},{5,6},{6,7},{7,8},{8,9},{9,10},{10,1... | collective-permute-start | bytes 589832 | tf_op jit(solution)/shard_map/ppermute | solution.py:418
  24.8 12.0 %collective-permute-start.6 = (bf16[3,128,128]{2,1,0:T(8,128)(2,1)S(1)}, bf16[3,128,128]{2,1,0:T(8,128)(2,1)S(1)}, u32[]{:S(2)}, u32[]{:S(2)}) collective-permute-start(bf16[3,128,128]{2,1,0:T(8,128)(2,1)S(1)} %get-tuple-element.69), channel_id=1, source_target_pairs={{0,1},{1,0},{2,3},{3,2},{4,5},{5,4},{6,7},{7,6},{8,9},{9,8},{10,11... | collective-permute-start | bytes 294920 | tf_op jit(solution)/shard_map/ppermute | solution.py:413
  31.4 5.3 %collective-permute-start.7 = (bf16[3,128,128]{2,1,0:T(8,128)(2,1)S(1)}, bf16[3,128,128]{2,1,0:T(8,128)(2,1)S(1)}, u32[]{:S(2)}, u32[]{:S(2)}) collective-permute-start(bf16[3,128,128]{2,1,0:T(8,128)(2,1)S(1)} %get-tuple-element.70), channel_id=1, source_target_pairs={{0,1},{1,2},{2,3},{3,4},{4,5},{5,6},{6,7},{7,8},{8,9},{9,10},{10,1... | collective-permute-start | bytes 294920 | tf_op jit(solution)/shard_map/ppermute | solution.py:418
  31.4 5.3 %collective-permute-start.8 = (bf16[3,128,128]{2,1,0:T(8,128)(2,1)S(1)}, bf16[3,128,128]{2,1,0:T(8,128)(2,1)S(1)}, u32[]{:S(2)}, u32[]{:S(2)}) collective-permute-start(bf16[3,128,128]{2,1,0:T(8,128)(2,1)S(1)} %get-tuple-element.71), channel_id=1, source_target_pairs={{0,15},{1,0},{2,1},{3,2},{4,3},{5,4},{6,5},{7,6},{8,7},{9,8},{10,9... | collective-permute-start | bytes 294920 | tf_op jit(solution)/shard_map/ppermute | solution.py:418
  31.9 4.8 %collective-permute-start.9 = (f32[16,128]{1,0:T(8,128)S(1)}, f32[16,128]{1,0:T(8,128)S(1)}, u32[]{:S(2)}, u32[]{:S(2)}) collective-permute-start(f32[16,128]{1,0:T(8,128)S(1)} %get-tuple-element.72.gram), channel_id=1, source_target_pairs={{0,1},{1,0},{2,3},{3,2},{4,5},{5,4},{6,7},{7,6},{8,9},{9,8},{10,11... | collective-permute-start | bytes 24584 | tf_op jit(solution)/shard_map/ppermute | solution.py:413

commit v8 on v7

--- a/solution.py
+++ b/solution.py
@@ -16,7 +16,7 @@
 BF = jnp.bfloat16
 F32 = jnp.float32
 EARLY = [(i, j) for i in range(3) for j in range(i, 3)]
-LATE = [(i, j) for j in range(3, ITERATIONS) for i in range(j + 1)]
+LATE = [(2, 3), (3, 3), (3, 4), (4, 4)]
 PAIRS = EARLY + LATE
 ROWS = len(PAIRS) + 1
 ENTRIES = 2 + 2 * NAMED
@@ -99,8 +99,11 @@
         relative.append((rel, place, bit))
         ups.append(up)
         lows.append(low)
+    yield
     up_count = low_count = up_cross = low_cross = jnp.int32(0)
     for g in range(count):
+        if g == count // 2:
+            yield
         rel, place, bit = relative[g]
         below = jnp.where(ups[g], up_mask, low_mask) & (bit - 1)
         rank = below & 1
@@ -137,6 +140,7 @@
             tab[at] = jnp.where(j < used, rows[1, j], 0)
             tab[at + 1] = jnp.int32(3)
             tab[at + 2] = jnp.where(j < used, rows[2, j], 2 * NAMED)
+    yield
 
 
 def pack(tab, shift, aff, t, hl, send, base):
@@ -172,24 +176,23 @@
     tall[...] = wide[...].T
     load_c.wait()
 
-    def finish(scores, c):
-        value = jnp.maximum(scores, 0.0)
-        value = value * value * value
-        for i in range(per):
-            block = value[i * rows : (i + 1) * rows]
-            t0[c * per + i] = block
-            put_split(hl, c * per + i, block)
-
-    scores = None
+    def finish(c):
+        for g in range(c * per, (c + 1) * per):
+            value = jnp.maximum(t0[g], 0.0)
+            value = value * value * value
+            t0[g] = value
+            put_split(hl, g, value)
+
+    stages = fill_table(cols, tab, up_rows, low_rows, axis)
     for c in range(chunks):
         copies[c].wait()
-        if c == 0:
-            fill_table(cols, tab, up_rows, low_rows, axis)
-        ahead = dot(buf[c], tall[...])
+        next(stages)
+        scores = dot(buf[c], tall[...])
+        for i in range(per):
+            t0[c * per + i] = scores[i * rows : (i + 1) * rows]
         if c > 0:
-            finish(scores, c - 1)
-        scores = ahead
-    finish(scores, chunks - 1)
+            finish(c - 1)
+    finish(chunks - 1)
     load_a.wait()
     pack(tab, SHIFTS[0], aff, t0, hl, send_b, lists + NAMED)
 
@@ -285,8 +288,8 @@
 
 
 def last_kernel(tab, aff, *refs, parity, axis):
-    halo_part, recv_a, recv_b = refs[-9:-6]
-    hl3, t3, t4, hl4, send_b, halo = refs[-6:]
+    halo_part, recv_a, recv_b = refs[-10:-7]
+    hl3, t3, t4, hl4, send_b, send_a, halo = refs[-7:]
     width = t3.shape[2]
     _, lists, _, _ = offsets(t3.shape[0])
     active = lax.rem(lax.axis_index(axis), 2) == parity
@@ -296,29 +299,32 @@
         two_steps(tab, aff, hl3, t3, halo_part, recv_a, recv_b, t4, hl4, halo, 2)
         for j in range(NAMED):
             send_b[j] = hl4[tab[lists + NAMED + j], :, :width]
+            send_a[j] = hl4[tab[lists + j], :, :width]
 
     @pl.when(jnp.logical_not(active))
     def _():
         send_b[...] = jnp.zeros(send_b.shape, BF)
 
 
-def gram_kernel(tab, aff, t0, t1, t2, t3, t4, hl, early, out, weight, send_a, sums_h):
-    count, rows, width = t0.shape
-    _, lists, _, _ = offsets(count)
-    for j in range(NAMED):
-        send_a[j] = hl[tab[lists + j], :, :width]
-    sums = [jnp.zeros((8, width), F32) for _ in LATE]
-    last = jnp.zeros((8, width), F32)
-    halo_products(tab, aff, hl, sums_h, 2.0)
-    for h in range(2 * NAMED):
-        weight[h] = sums_h[h]
+def gram_kernel(tab, aff, t2, t3, t4, hl, early, out):
+    count, rows, width = t2.shape
+    sums = [jnp.zeros((8, width), F32) for _ in range(len(LATE) + 1)]
+    fields = (None, None, t2, t3, t4)
     for g in range(count):
         local = row_product(aff, tab, 0, g, hl)
-        last = last + (t4[g] * local).reshape(rows // 8, 8, width).sum(0)
-    sums = add_products(sums, LATE, (t0, t1, t2, t3, t4)) + [last]
+        v = [None if f is None else f[g] for f in fields]
+        terms = [v[i] * v[j] for i, j in LATE] + [v[-1] * local]
+        for n, term in enumerate(terms):
+            sums[n] = sums[n] + term.reshape(rows // 8, 8, width).sum(0)
     out[pl.ds(0, len(EARLY)), :] = early[...]
     for n, total in enumerate(sums):
         out[pl.ds(len(EARLY) + n, 1), :] = jnp.sum(total, axis=0, keepdims=True)
+
+
+def weight_kernel(tab, aff, hl, weight, sums):
+    halo_products(tab, aff, hl, sums, 2.0)
+    for h in range(2 * NAMED):
+        weight[h] = sums[h]
 
 
 def cross_kernel(weight, recv_a, recv_even, recv_odd, gram, other, out, recv_b, *, axis):
@@ -353,17 +359,20 @@
     gram = {}
     for k, (i, j) in enumerate(PAIRS):
         gram[i, j] = gram[j, i] = value[k : k + 1]
+    for j in range(2, n - 1):
+        for i in range(n - 2):
+            if (i, j + 1) not in gram:
+                entry = gram[i + 1, j] + (SHIFTS[i] - SHIFTS[j]) * gram[i, j]
+                gram[i, j + 1] = gram[j + 1, i] = entry
     matrix = {}
     for i in range(n):
         for j in range(i, n):
-            terms = []
-            if j + 1 < n:
-                terms.append(gram[i, j + 1] + SHIFTS[j] * gram[i, j])
-            if i + 1 < n and i != j:
-                terms.append(gram[i + 1, j] + SHIFTS[i] * gram[i, j])
-            if not terms:
-                terms = [value[ROWS - 1 : ROWS]]
-            product = terms[0] if len(terms) == 1 else 0.5 * (terms[0] + terms[1])
+            if i + 1 < n and j + 1 == n:
+                product = gram[i + 1, j] + SHIFTS[i] * gram[i, j]
+            elif j + 1 < n:
+                product = gram[i, j + 1] + SHIFTS[j] * gram[i, j]
+            else:
+                product = value[ROWS - 1 : ROWS]
             matrix[i, j] = gram[i, j] - DAMP * product
     scale = [
         jnp.where(matrix[i, i] > 0.0, lax.rsqrt(jnp.maximum(matrix[i, i], 1e-37)), 0.0)
@@ -434,7 +443,7 @@
     edge_sum = jax.ShapeDtypeStruct((2 * NAMED, rows, width), F32)
     sums_h = pltpu.VMEM((2 * NAMED + 1, rows, width), F32)
     work = [pltpu.VMEM((2 * NAMED + 1, rows, width), BF)]
-    chunks = count // 2
+    chunks = 3
     flops = 2 * count * rows * 4 * rows * 2 * width
 
     def call(kernel, out_shape, products, scratch=(), aliases=None, limit=24):
@@ -493,21 +502,22 @@
     )(tab, aff, t0, hl0)
     recv_a = to_chip_partner(send_a, axis)
 
-    def by_parity(kernel, parity, edges, aliased):
-        fields = (split, field, field, split)
+    def by_parity(kernel, parity, edges, aliases):
         return call(
             functools.partial(kernel, parity=parity, axis=axis),
-            fields + (edges,),
+            (split, field, field, split, *edges),
             2,
             work,
-            {2 + i: i for i in range(aliased)},
+            dict(aliases),
         )
 
-    hl1, t1, t2, hl2, send = by_parity(middle_kernel, 0, edge, 2)(
+    first_half = {2: 0, 3: 1}
+    second_half = {2: 0, 3: 1, 4: 2, 5: 3}
+    hl1, t1, t2, hl2, send = by_parity(middle_kernel, 0, (edge,), first_half)(
         tab, aff, hl1, part, halo_part, recv_a, recv_even
     )
     got_odd = shift(send, -1, axis)
-    hl1, t1, t2, hl2, send = by_parity(middle_kernel, 1, edge, 4)(
+    hl1, t1, t2, hl2, send = by_parity(middle_kernel, 1, (edge,), second_half)(
         tab, aff, hl1, t1, t2, hl2, halo_part, recv_a, recv_odd
     )
     got_even = shift(send, 1, axis)
@@ -516,19 +526,21 @@
     )(tab, aff, t2, hl2)
     recv_a = to_chip_partner(send_a, axis)
     gram = call(early_kernel, early, 0.1)(t0, t1, t2)
-    hl3, t3, t4, hl4, send = by_parity(last_kernel, 1, half, 2)(
+    hl3, t3, t4, hl4, send, send_a = by_parity(last_kernel, 1, (half, half), first_half)(
         tab, aff, hl3, part, halo_part, recv_a, got_odd
     )
     recv_even = shift(send, 1, axis)
-    hl3, t3, t4, hl4, send = by_parity(last_kernel, 0, half, 4)(
-        tab, aff, hl3, t3, t4, hl4, halo_part, recv_a, got_even
+    last0 = by_parity(last_kernel, 0, (half, half), {**second_half, 6: 5})
+    _, t3, t4, hl4, send, send_a = last0(
+        tab, aff, hl3, t3, t4, hl4, send_a, halo_part, recv_a, got_even
     )
     recv_odd = shift(send, -1, axis)
-    gram, weight, send_a = call(
-        gram_kernel, (jax.ShapeDtypeStruct((ROWS, width), F32), edge_sum, half), 1, [sums_h]
-    )(tab, aff, t0, t1, t2, t3, t4, hl4, gram)
     recv_a = to_chip_partner(send_a, axis)
+    gram = call(
+        gram_kernel, jax.ShapeDtypeStruct((ROWS, width), F32), 1
+    )(tab, aff, t2, t3, t4, hl4, gram)
     other = to_chip_partner(gram, axis)
+    weight = call(weight_kernel, edge_sum, 0.2, [sums_h])(tab, aff, hl4)
     parts = call(
         functools.partial(cross_kernel, axis=axis),
         jax.ShapeDtypeStruct((devices // 2, ROWS, width), F32),

time: 50.5 us -> 48.4 us (0.958)
  blocking collectives: 12.3 us -> 10.9 us
  Pallas kernels: 11.4 us -> 10.3 us
    all_to_all x1, blocking collectives: 12.3 us -> 10.9 us  [shards(): parts = lax.all_to_all(parts, axis, 0, 0, axis_index_groups=groups)]
    pallas_call x9 -> x10, Pallas kernels: 6.96 us -> 5.93 us  [run(): pl.pallas_call(kernel, out_shape=out_shape, in_specs=specs, out_specs=(VM...]
    ppermute x6, waiting for transfers between devices: 9.87 us -> 10.6 us  [shift(): return lax.ppermute(block, axis, [(i, (i + by) % n) for i in range(n)])]
  transfers between devices with their start and end apart: 10 -> 10, of which waited for: 5 -> 5; matrix products, arithmetic and copies ran while one was open for 0% -> 0% of each run, Pallas kernels for 4% -> 6%
where the time goes in v8:
time: 48.4 us; the launch traced here: 48.2 us
  starting transfers between devices  15.9 us (33%)
  waiting for transfers between devices  11.1 us (23%)
  blocking collectives  10.9 us (23%)
  Pallas kernels  10.3 us (21%)
    ppermute x4, starting transfers between devices, to_chip_partner(): lax.ppermute(block, axis, [(i, i ^ 1) for i in range(lax.axis_size(axis))])  10.9 us
    all_to_all x1, blocking collectives, shards(): parts = lax.all_to_all(parts, axis, 0, 0, axis_index_groups=groups)  10.9 us
    ppermute x6, waiting for transfers between devices, shift(): return lax.ppermute(block, axis, [(i, (i + by) % n) for i in range(n)])  10.6 us
    pallas_call x10, Pallas kernels, run(): pl.pallas_call(kernel, out_shape=out_shape, in_specs=specs, out_specs=(VM...  5.93 us
    ppermute x6, starting transfers between devices, shift(): return lax.ppermute(block, axis, [(i, (i + by) % n) for i in range(n)])  4.98 us
    pallas_call x1, Pallas kernels, shards(): pl.pallas_call(functools.partial(first_kernel, chunks=chunks, axis=axis),...  3.25 us
    pallas_call x1, Pallas kernels, shards(): pl.pallas_call(final_kernel, out_shape=jax.ShapeDtypeStruct((count * rows...  1.07 us
  transfers between devices with their start and end apart: 10, of which 5 were waited for; matrix products, arithmetic and copies ran while one was open for 0% of the time, Pallas kernels for 6%

profile of v8, /device:TPU:1, one launch (start us, length us, event | category | flops | bytes accessed | tf_op | source)
XLA Modules:
  0.0 48.2 jit_solution(258371360824859502)
XLA Ops:
  0.0 3.3 %first.1 = (f32[12,128,128]{2,1,0:T(8,128)S(1)}, bf16[19,128,256]{2,1,0:T(8,128)(2,1)S(1)}, bf16[6,128,128]{2,1,0:T(8,128)(2,1)S(1)}, bf16[12,4,128,128]{3,2,1,0:T(8,128)(2,1)S(1)}, s32[128]{0:T(128)S(4)}) custom-call(bf16[1536,768]{1,0:T(8,128)(2,1)} %desc.1, bf16[128,768]{1,0:T(8,128)(2,1)} %queries.1, bf16[12,4,128,128]{3,2,1,0:T(8,128)(2,1)} %affinity.1, ...), custom_call_target="tpu_custom_call" | custom-call | flops 402653184 | bytes 4194304 | tf_op jit(solution)/shard_map/first/pallas_call | solution.py:474
  3.3 0.9 %shard_map.46 = (f32[12,128,128]{2,1,0:T(8,128)S(1)}, bf16[19,128,256]{2,1,0:T(8,128)(2,1)S(1)}, f32[6,128,128]{2,1,0:T(8,128)S(1)}, bf16[6,128,128]{2,1,0:T(8,128)(2,1)S(1)}) custom-call(s32[128]{0:T(128)S(4)} %get-tuple-element.38.tab, bf16[12,4,128,128]{3,2,1,0:T(8,128)(2,1)S(1)} %get-tuple-element.39.aff, f32[12,128,128]{2,1,0:T(8,128)S(1)} %get-tuple-element.40.t.t0, ...), custom_call_target="tpu_custom_call" | custom-call | flops 402653184 | bytes 4194304 | tf_op jit(solution)/shard_map/pallas_call | solution.py:458
  4.1 0.1 collective-permute-start
  4.2 2.7 %collective-permute-start.1 = (bf16[6,128,128]{2,1,0:T(8,128)(2,1)S(1)}, bf16[6,128,128]{2,1,0:T(8,128)(2,1)S(1)}, u32[]{:S(2)}, u32[]{:S(2)}) collective-permute-start(bf16[6,128,128]{2,1,0:T(8,128)(2,1)S(1)} %get-tuple-element.46), channel_id=1, source_target_pairs={{0,1},{1,2},{2,3},{3,4},{4,5},{5,6},{6,7},{7,8},{8,9},{9,10},{10,1... | collective-permute-start | bytes 589832 | tf_op jit(solution)/shard_map/ppermute | solution.py:427
  6.9 2.6 %collective-permute-done.1.refs_4_ = bf16[6,128,128]{2,1,0:T(8,128)(2,1)S(1)} collective-permute-done((bf16[6,128,128]{2,1,0:T(8,128)(2,1)S(1)}, bf16[6,128,128]{2,1,0:T(8,128)(2,1)S(1)}, u32[]{:S(2)}, u32[]{:S(2)}) %collective-permute-start.1) | collective-permute-done | bytes 196640 | tf_op jit(solution)/shard_map/ppermute | solution.py:427
  9.5 4.6 %collective-permute-done.2.refs_6_ = bf16[6,128,128]{2,1,0:T(8,128)(2,1)S(1)} collective-permute-done((bf16[6,128,128]{2,1,0:T(8,128)(2,1)S(1)}, bf16[6,128,128]{2,1,0:T(8,128)(2,1)S(1)}, u32[]{:S(2)}, u32[]{:S(2)}) %collective-permute-start.2) | collective-permute-done | bytes 196640 | tf_op jit(solution)/shard_map/ppermute | solution.py:427
  14.1 1.3 %shard_map.48 = (bf16[19,128,256]{2,1,0:T(8,128)(2,1)S(1)}, f32[12,128,128]{2,1,0:T(8,128)S(1)}, f32[12,128,128]{2,1,0:T(8,128)S(1)}, bf16[19,128,256]{2,1,0:T(8,128)(2,1)S(1)}, bf16[6,128,128]{2,1,0:T(8,128)(2,1)S(1)}) custom-call(s32[128]{0:T(128)S(4)} %get-tuple-element.38.tab, ...), custom_call_target="tpu_custom_call", output_to_operand_aliasing={{0}: (2, {}), {1}: (3, {}), {2}: (4, {}), {3}: (5, {})} | custom-call | flops 805306368 | bytes 4194304 | tf_op jit(solution)/shard_map/pallas_call | solution.py:458
  15.4 0.9 %shard_map.49 = (f32[12,128,128]{2,1,0:T(8,128)S(1)}, bf16[19,128,256]{2,1,0:T(8,128)(2,1)S(1)}, f32[6,128,128]{2,1,0:T(8,128)S(1)}, bf16[6,128,128]{2,1,0:T(8,128)(2,1)S(1)}) custom-call(s32[128]{0:T(128)S(4)} %get-tuple-element.38.tab, bf16[12,4,128,128]{3,2,1,0:T(8,128)(2,1)S(1)} %get-tuple-element.39.aff, f32[12,128,128]{2,1,0:T(8,128)S(1)} %get-tuple-element.51.t.t2, ...), custom_call_target="tpu_custom_call" | custom-call | flops 402653184 | bytes 4194304 | tf_op jit(solution)/shard_map/pallas_call | solution.py:458
  16.3 0.1 collective-permute-start.3
  16.4 0.5 %collective-permute-start.4 = (bf16[6,128,128]{2,1,0:T(8,128)(2,1)S(1)}, bf16[6,128,128]{2,1,0:T(8,128)(2,1)S(1)}, u32[]{:S(2)}, u32[]{:S(2)}) collective-permute-start(bf16[6,128,128]{2,1,0:T(8,128)(2,1)S(1)} %get-tuple-element.57), channel_id=1, source_target_pairs={{0,15},{1,0},{2,1},{3,2},{4,3},{5,4},{6,5},{7,6},{8,7},{9,8},{10,9... | collective-permute-start | bytes 589832 | tf_op jit(solution)/shard_map/ppermute | solution.py:427
  16.9 1.3 %collective-permute-start.5 = (bf16[6,128,128]{2,1,0:T(8,128)(2,1)S(1)}, bf16[6,128,128]{2,1,0:T(8,128)(2,1)S(1)}, u32[]{:S(2)}, u32[]{:S(2)}) collective-permute-start(bf16[6,128,128]{2,1,0:T(8,128)(2,1)S(1)} %get-tuple-element.63), channel_id=1, source_target_pairs={{0,1},{1,2},{2,3},{3,4},{4,5},{5,6},{6,7},{7,8},{8,9},{9,10},{10,1... | collective-permute-start | bytes 589832 | tf_op jit(solution)/shard_map/ppermute | solution.py:427
  18.2 3.3 %collective-permute-done.4.refs_4_ = bf16[6,128,128]{2,1,0:T(8,128)(2,1)S(1)} collective-permute-done((bf16[6,128,128]{2,1,0:T(8,128)(2,1)S(1)}, bf16[6,128,128]{2,1,0:T(8,128)(2,1)S(1)}, u32[]{:S(2)}, u32[]{:S(2)}) %collective-permute-start.4) | collective-permute-done | bytes 196640 | tf_op jit(solution)/shard_map/ppermute | solution.py:427
  21.5 1.0 %shard_map.50 = (bf16[19,128,256]{2,1,0:T(8,128)(2,1)S(1)}, f32[12,128,128]{2,1,0:T(8,128)S(1)}, f32[12,128,128]{2,1,0:T(8,128)S(1)}, bf16[19,128,256]{2,1,0:T(8...) custom-call(s32[128]{0:T(128)S(4)} %get-tuple-element.38.tab, ...), custom_call_target="tpu_custom_call", output_to_operand_aliasing={{0}: (2, {}), {1}: (3, {})} | custom-call | flops 805306368 | bytes 4194304 | tf_op jit(solution)/shard_map/pallas_call | solution.py:458
  22.5 0.1 collective-permute-done.5.refs_7_
  22.7 6.7 %collective-permute-start.6 = (bf16[3,128,128]{2,1,0:T(8,128)(2,1)S(1)}, bf16[3,128,128]{2,1,0:T(8,128)(2,1)S(1)}, u32[]{:S(2)}, u32[]{:S(2)}) collective-permute-start(bf16[3,128,128]{2,1,0:T(8,128)(2,1)S(1)} %get-tuple-element.65), channel_id=1, source_target_pairs={{0,1},{1,0},{2,3},{3,2},{4,5},{5,4},{6,7},{7,6},{8,9},{9,8},{10,11... | collective-permute-start | bytes 294920 | tf_op jit(solution)/shard_map/ppermute | solution.py:422
  29.4 0.5 %collective-permute-start.8 = (bf16[3,128,128]{2,1,0:T(8,128)(2,1)S(1)}, bf16[3,128,128]{2,1,0:T(8,128)(2,1)S(1)}, u32[]{:S(2)}, u32[]{:S(2)}) collective-permute-start(bf16[3,128,128]{2,1,0:T(8,128)(2,1)S(1)} %get-tuple-element.67), channel_id=1, source_target_pairs={{0,15},{1,0},{2,1},{3,2},{4,3},{5,4},{6,5},{7,6},{8,7},{9,8},{10,9... | collective-permute-start | bytes 294920 | tf_op jit(solution)/shard_map/ppermute | solution.py:427
  29.9 0.8 %shard_map.53.early = f32[6,128]{1,0:T(8,128)S(1)} custom-call(f32[12,128,128]{2,1,0:T(8,128)S(1)} %get-tuple-element.40.t.t0, f32[12,128,128]{2,1,0:T(8,128)S(1)} %get-tuple-element.70.t1, f32[12,128,128]{2,1,0:T(8,128)S(1)} %get-tuple-element.51.t.t2), custom_call_target="tpu_custom_call" | custom-call | flops 40265320 | bytes 4194304 | tf_op jit(solution)/shard_map/pallas_call | solution.py:458
  30.7 0.6 %shard_map.54.gram = f32[11,128]{1,0:T(8,128)S(1)} custom-call(s32[128]{0:T(128)S(4)} %get-tuple-element.38.tab, bf16[12,4,128,128]{3,2,1,0:T(8,128)(2,1)S(1)} %get-tuple-element.39.aff, f32[12,128,128]{2,1,0:T(8,128)S(1)} %get-tuple-element.51.t.t2, f32[12,128,128]{2,1,0:T(8,128)S(1)} %get-tuple-element.68.t3, f32[12,128,128]{2,1,0:T(8,128)S(1)} %get-tuple-element.69.t4, ...), custom_call_target="tpu_custom_call" | custom-call | flops 402653184 | bytes 4194304 | tf_op jit(solution)/shard_map/pallas_call | solution.py:458
  31.3 4.1 %collective-permute-start.9 = (f32[11,128]{1,0:T(8,128)S(1)}, f32[11,128]{1,0:T(8,128)S(1)}, u32[]{:S(2)}, u32[]{:S(2)}) collective-permute-start(f32[11,128]{1,0:T(8,128)S(1)} %shard_map.54.gram), channel_id=1, source_target_pairs={{0,1},{1,0},{2,3},{3,2},{4,5},{5,4},{6,7},{7,6},{8,9},{9,8},{10,11... | collective-permute-start | bytes 16904 | tf_op jit(solution)/shard_map/ppermute | solution.py:422
  35.3 0.4 shard_map.52.weight
  35.7 0.5 collective-permute-done.9.other
  36.2 0.1 shard_map.55
  36.3 10.9 %all_to_all.5.parts = f32[8,11,128]{2,1,0:T(8,128)S(1)} all-to-all(f32[8,11,128]{2,1,0:T(8,128)S(1)} %shard_map.55), channel_id=1, replica_groups={{0,2,4,6,8,10,12,14},{1,3,5,7,9,11,13,15},{16,18,20,22,24,26,28,30},{17..., dimensions={0} | all-to-all | bytes 90112 | tf_op jit(solution)/shard_map/all_to_all | solution.py:552
  47.1 1.1 %final.1 = f32[1536,128]{1,0:T(8,128)} custom-call(f32[8,11,128]{2,1,0:T(8,128)S(1)} %all_to_all.5.parts, f32[12,128,128]{2,1,0:T(8,128)S(1)} %get-tuple-element.40.t.t0, f32[12,128,128]{2,1,0:T(8,128)S(1)} %get-tuple-element.70.t1, f32[12,128,128]{2,1,0:T(8,128)S(1)} %get-tuple-element.51.t.t2, f32[12,128,128]{2,1,0:T(8,128)S(1)} %get-tuple-element.68.t3, ...), custom_call_target="tpu_custom_call" | custom-call | tf_op jit(solution)/shard_map/final/pallas_call | solution.py:553
  (9 shorter events, 0.1 us)
Async XLA Ops:
  4.1 2.8 %collective-permute-start = (bf16[6,128,128]{2,1,0:T(8,128)(2,1)S(1)}, bf16[6,128,128]{2,1,0:T(8,128)(2,1)S(1)}, u32[]{:S(2)}, u32[]{:S(2)}) collective-permute-start(bf16[6,128,128]{2,1,0:T(8,128)(2,1)S(1)} %get-tuple-element.45), channel_id=1, source_target_pairs={{0,1},{1,0},{2,3},{3,2},{4,5},{5,4},{6,7},{7,6},{8,9},{9,8},{10,11... | collective-permute-start | bytes 589832 | tf_op jit(solution)/shard_map/ppermute | solution.py:422
  4.2 5.3 %collective-permute-start.1 = (bf16[6,128,128]{2,1,0:T(8,128)(2,1)S(1)}, bf16[6,128,128]{2,1,0:T(8,128)(2,1)S(1)}, u32[]{:S(2)}, u32[]{:S(2)}) collective-permute-start(bf16[6,128,128]{2,1,0:T(8,128)(2,1)S(1)} %get-tuple-element.46), channel_id=1, source_target_pairs={{0,1},{1,2},{2,3},{3,4},{4,5},{5,6},{6,7},{7,8},{8,9},{9,10},{10,1... | collective-permute-start | bytes 589832 | tf_op jit(solution)/shard_map/ppermute | solution.py:427
  6.9 7.2 %collective-permute-start.2 = (bf16[6,128,128]{2,1,0:T(8,128)(2,1)S(1)}, bf16[6,128,128]{2,1,0:T(8,128)(2,1)S(1)}, u32[]{:S(2)}, u32[]{:S(2)}) collective-permute-start(bf16[6,128,128]{2,1,0:T(8,128)(2,1)S(1)} %get-tuple-element.46), channel_id=1, source_target_pairs={{0,15},{1,0},{2,1},{3,2},{4,3},{5,4},{6,5},{7,6},{8,7},{9,8},{10,9... | collective-permute-start | bytes 589832 | tf_op jit(solution)/shard_map/ppermute | solution.py:427
  16.3 1.9 %collective-permute-start.3 = (bf16[6,128,128]{2,1,0:T(8,128)(2,1)S(1)}, bf16[6,128,128]{2,1,0:T(8,128)(2,1)S(1)}, u32[]{:S(2)}, u32[]{:S(2)}) collective-permute-start(bf16[6,128,128]{2,1,0:T(8,128)(2,1)S(1)} %get-tuple-element.56), channel_id=1, source_target_pairs={{0,1},{1,0},{2,3},{3,2},{4,5},{5,4},{6,7},{7,6},{8,9},{9,8},{10,11... | collective-permute-start | bytes 589832 | tf_op jit(solution)/shard_map/ppermute | solution.py:422
  16.4 5.1 %collective-permute-start.4 = (bf16[6,128,128]{2,1,0:T(8,128)(2,1)S(1)}, bf16[6,128,128]{2,1,0:T(8,128)(2,1)S(1)}, u32[]{:S(2)}, u32[]{:S(2)}) collective-permute-start(bf16[6,128,128]{2,1,0:T(8,128)(2,1)S(1)} %get-tuple-element.57), channel_id=1, source_target_pairs={{0,15},{1,0},{2,1},{3,2},{4,3},{5,4},{6,5},{7,6},{8,7},{9,8},{10,9... | collective-permute-start | bytes 589832 | tf_op jit(solution)/shard_map/ppermute | solution.py:427
  16.9 5.8 %collective-permute-start.5 = (bf16[6,128,128]{2,1,0:T(8,128)(2,1)S(1)}, bf16[6,128,128]{2,1,0:T(8,128)(2,1)S(1)}, u32[]{:S(2)}, u32[]{:S(2)}) collective-permute-start(bf16[6,128,128]{2,1,0:T(8,128)(2,1)S(1)} %get-tuple-element.63), channel_id=1, source_target_pairs={{0,1},{1,2},{2,3},{3,4},{4,5},{5,6},{6,7},{7,8},{8,9},{9,10},{10,1... | collective-permute-start | bytes 589832 | tf_op jit(solution)/shard_map/ppermute | solution.py:427
  22.7 13.5 %collective-permute-start.6 = (bf16[3,128,128]{2,1,0:T(8,128)(2,1)S(1)}, bf16[3,128,128]{2,1,0:T(8,128)(2,1)S(1)}, u32[]{:S(2)}, u32[]{:S(2)}) collective-permute-start(bf16[3,128,128]{2,1,0:T(8,128)(2,1)S(1)} %get-tuple-element.65), channel_id=1, source_target_pairs={{0,1},{1,0},{2,3},{3,2},{4,5},{5,4},{6,7},{7,6},{8,9},{9,8},{10,11... | collective-permute-start | bytes 294920 | tf_op jit(solution)/shard_map/ppermute | solution.py:422
  29.4 6.8 %collective-permute-start.7 = (bf16[3,128,128]{2,1,0:T(8,128)(2,1)S(1)}, bf16[3,128,128]{2,1,0:T(8,128)(2,1)S(1)}, u32[]{:S(2)}, u32[]{:S(2)}) collective-permute-start(bf16[3,128,128]{2,1,0:T(8,128)(2,1)S(1)} %get-tuple-element.66), channel_id=1, source_target_pairs={{0,1},{1,2},{2,3},{3,4},{4,5},{5,6},{6,7},{7,8},{8,9},{9,10},{10,1... | collective-permute-start | bytes 294920 | tf_op jit(solution)/shard_map/ppermute | solution.py:427
  29.4 6.8 %collective-permute-start.8 = (bf16[3,128,128]{2,1,0:T(8,128)(2,1)S(1)}, bf16[3,128,128]{2,1,0:T(8,128)(2,1)S(1)}, u32[]{:S(2)}, u32[]{:S(2)}) collective-permute-start(bf16[3,128,128]{2,1,0:T(8,128)(2,1)S(1)} %get-tuple-element.67), channel_id=1, source_target_pairs={{0,15},{1,0},{2,1},{3,2},{4,3},{5,4},{6,5},{7,6},{8,7},{9,8},{10,9... | collective-permute-start | bytes 294920 | tf_op jit(solution)/shard_map/ppermute | solution.py:427
  31.3 4.9 %collective-permute-start.9 = (f32[11,128]{1,0:T(8,128)S(1)}, f32[11,128]{1,0:T(8,128)S(1)}, u32[]{:S(2)}, u32[]{:S(2)}) collective-permute-start(f32[11,128]{1,0:T(8,128)S(1)} %shard_map.54.gram), channel_id=1, source_target_pairs={{0,1},{1,0},{2,3},{3,2},{4,5},{5,4},{6,7},{7,6},{8,9},{9,8},{10,11... | collective-permute-start | bytes 16904 | tf_op jit(solution)/shard_map/ppermute | solution.py:422

commit v9 on v8

--- a/solution.py
+++ b/solution.py
@@ -38,16 +38,21 @@
     return lax.dot_general(a, b, (((0,), (0,)), ((), ())), preferred_element_type=F32)
 
 
-def put_split(ref, index, value):
+def put_rounded(ref, index, value):
     high = value.astype(BF)
     width = value.shape[-1]
     ref[index, :, :width] = high
-    ref[index, :, width:] = (value - high.astype(F32)).astype(BF)
+    if ref.shape[2] > width:
+        ref[index, :, width:] = (value - high.astype(F32)).astype(BF)
+
+
+def folded(out):
+    width = out.shape[0]
+    return out if out.shape[1] == width else out[:, :width] + out[:, width:]
 
 
 def row_product(aff, tab, base, g, hl):
     count = aff.shape[0]
-    width = hl.shape[2] // 2
     if isinstance(g, int):
         low = g - 1 if g > 0 else tab[base + count]
         high = g + 1 if g + 1 < count else tab[base + count + 1]
@@ -59,8 +64,7 @@
     out = dot(left, right)
     left = jnp.concatenate([aff[g, 2], aff[g, 3]], axis=1)
     right = jnp.concatenate([hl[high], hl[tab[base + g]]], axis=0)
-    out = out + dot(left, right)
-    return out[:, :width] + out[:, width:]
+    return folded(out + dot(left, right))
 
 
 def shifted(value, shift, t):
@@ -153,10 +157,11 @@
 
 def first_kernel(
     desc, queries, affinity, tile_col, t0, hl, send_b, aff, tab,
-    buf, wide, tall, cols, up_rows, low_rows, sems, *, chunks, axis,
+    buf, wide, tall, cols, up_rows, low_rows, sems, *, bounds, axis,
 ):
     count, rows = t0.shape[0], t0.shape[1]
-    per = count // chunks
+    chunks = len(bounds) - 1
+    parts = [pl.ds(a * rows, (b - a) * rows) for a, b in zip(bounds, bounds[1:])]
     _, lists, _, _ = offsets(count)
     load_q = pltpu.make_async_copy(queries, wide, sems.at[chunks])
     load_c = pltpu.make_async_copy(tile_col, cols, sems.at[chunks + 1])
@@ -164,9 +169,7 @@
     load_c.start()
     copies = []
     for c in range(chunks):
-        copy = pltpu.make_async_copy(
-            desc.at[pl.ds(c * per * rows, per * rows)], buf.at[c], sems.at[c]
-        )
+        copy = pltpu.make_async_copy(desc.at[parts[c]], buf.at[parts[c]], sems.at[c])
         copy.start()
         copies.append(copy)
     load_a = pltpu.make_async_copy(affinity, aff, sems.at[chunks + 2])
@@ -177,19 +180,19 @@
     load_c.wait()
 
     def finish(c):
-        for g in range(c * per, (c + 1) * per):
+        for g in range(bounds[c], bounds[c + 1]):
             value = jnp.maximum(t0[g], 0.0)
             value = value * value * value
             t0[g] = value
-            put_split(hl, g, value)
+            put_rounded(hl, g, value)
 
     stages = fill_table(cols, tab, up_rows, low_rows, axis)
     for c in range(chunks):
         copies[c].wait()
-        next(stages)
-        scores = dot(buf[c], tall[...])
-        for i in range(per):
-            t0[c * per + i] = scores[i * rows : (i + 1) * rows]
+        next(stages, None)
+        scores = dot(buf[parts[c], :], tall[...])
+        for i, g in enumerate(range(bounds[c], bounds[c + 1])):
+            t0[g] = scores[i * rows : (i + 1) * rows]
         if c > 0:
             finish(c - 1)
     finish(chunks - 1)
@@ -216,14 +219,11 @@
 
 
 def halo_products(tab, aff, hl, sums, factor):
-    count = aff.shape[0]
-    width = sums.shape[2]
-    _, _, cross, _ = offsets(count)
+    _, _, cross, _ = offsets(aff.shape[0])
     sums[...] = jnp.zeros(sums.shape, F32)
     for e in range(ENTRIES):
         g, slot, h = (tab[cross + 3 * e + i] for i in range(3))
-        both = dot_t(aff[g, slot], hl[g])
-        both = both[:, :width] + both[:, width:]
+        both = folded(dot_t(aff[g, slot], hl[g]))
         sums[h] += both if factor == 1.0 else factor * both
 
 
@@ -231,11 +231,11 @@
     count = t.shape[0]
     _, lists, _, _ = offsets(count)
     pack(tab, SHIFTS[step], aff, t, hl, send_a, lists)
-    hl_next[count + 2 * NAMED] = jnp.zeros(hl.shape[1:], BF)
+    hl_next[count + 2 * NAMED] = jnp.zeros(hl_next.shape[1:], BF)
     for g in range(count):
         value = shifted(row_product(aff, tab, 0, g, hl), SHIFTS[step], t[g])
         part[g] = value
-        put_split(hl_next, g, value)
+        put_rounded(hl_next, g, value)
     halo_products(tab, aff, hl, sums, 1.0)
     for h in range(2 * NAMED):
         halo_part[h] = sums[h]
@@ -248,27 +248,27 @@
 
 
 def two_steps(tab, aff, hl1, t1, halo_part, recv_a, recv_b, t2, hl2, halo, step):
-    count, _, width = t2.shape
+    count, _, _ = t2.shape
     full, lists, cross, _ = offsets(count)
-    zeros = jnp.zeros(hl2.shape[1:], BF)
-    hl2[count + 2 * NAMED] = zeros
-    halo[2 * NAMED] = zeros[:, :width]
+    hl1[count + 2 * NAMED] = jnp.zeros(hl1.shape[1:], BF)
+    hl2[count + 2 * NAMED] = jnp.zeros(hl2.shape[1:], BF)
+    halo[2 * NAMED] = jnp.zeros(halo.shape[1:], BF)
     for h in range(NAMED):
         halo[h] = recv_a[h]
         halo[NAMED + h] = recv_b[h]
         low, high = h, NAMED + h
-        put_split(hl1, count + low, recv_a[NAMED + h].astype(F32) + halo_part[low])
-        put_split(hl1, count + high, recv_b[NAMED + h].astype(F32) + halo_part[high])
+        put_rounded(hl1, count + low, recv_a[NAMED + h].astype(F32) + halo_part[low])
+        put_rounded(hl1, count + high, recv_b[NAMED + h].astype(F32) + halo_part[high])
     for e in range(ENTRIES):
         g, slot, h = (tab[cross + 3 * e + i] for i in range(3))
         t1[g] += dot(aff[g, slot], halo[h])
     for j in range(2 * NAMED):
         g = tab[lists + j]
-        put_split(hl1, g, t1[g])
+        put_rounded(hl1, g, t1[g])
     for g in range(count):
         value = shifted(row_product(aff, tab, full, g, hl1), SHIFTS[step + 1], t1[g])
         t2[g] = value
-        put_split(hl2, g, value)
+        put_rounded(hl2, g, value)
 
 
 def middle_kernel(tab, aff, *refs, parity, axis):
@@ -436,6 +436,7 @@
     size = 128 * pl.cdiv(offsets(count)[-1], 128)
     blocks = count + 2 * NAMED + 1
     field = jax.ShapeDtypeStruct((count, rows, width), F32)
+    rounded = jax.ShapeDtypeStruct((blocks, rows, width), BF)
     split = jax.ShapeDtypeStruct((blocks, rows, 2 * width), BF)
     edge = jax.ShapeDtypeStruct((2 * NAMED, rows, width), BF)
     half = jax.ShapeDtypeStruct((NAMED, rows, width), BF)
@@ -443,7 +444,7 @@
     edge_sum = jax.ShapeDtypeStruct((2 * NAMED, rows, width), F32)
     sums_h = pltpu.VMEM((2 * NAMED + 1, rows, width), F32)
     work = [pltpu.VMEM((2 * NAMED + 1, rows, width), BF)]
-    chunks = 3
+    bounds = (0, count // 6, count // 2, count - count // 6, count)
     flops = 2 * count * rows * 4 * rows * 2 * width
 
     def call(kernel, out_shape, products, scratch=(), aliases=None, limit=24):
@@ -472,10 +473,10 @@
 
     operands = (descriptors, queries, affinity, tile_col.T)
     t0, hl0, send_b, aff, tab = pl.pallas_call(
-        functools.partial(first_kernel, chunks=chunks, axis=axis),
+        functools.partial(first_kernel, bounds=bounds, axis=axis),
         out_shape=(
             field,
-            split,
+            rounded,
             edge,
             jax.ShapeDtypeStruct(affinity.shape, BF),
             pltpu.SMEM((size,), jnp.int32),
@@ -483,13 +484,13 @@
         in_specs=[HBM] * 4,
         out_specs=(VMEM,) * 4 + (SMEM,),
         scratch_shapes=[
-            pltpu.VMEM((chunks, count * rows // chunks, depth), BF),
+            pltpu.VMEM((count * rows, depth), BF),
             pltpu.VMEM((width, depth), BF),
             pltpu.VMEM((depth, width), BF),
             pltpu.SMEM((4, count), jnp.int32),
             pltpu.SMEM((3, count + 1), jnp.int32),
             pltpu.SMEM((3, count + 1), jnp.int32),
-            pltpu.SemaphoreType.DMA((chunks + 3,)),
+            pltpu.SemaphoreType.DMA((len(bounds) + 2,)),
         ],
         compiler_params=params(24),
         cost_estimate=pl.CostEstimate(flops=flops, bytes_accessed=4 << 20, transcendentals=0),
@@ -502,10 +503,10 @@
     )(tab, aff, t0, hl0)
     recv_a = to_chip_partner(send_a, axis)
 
-    def by_parity(kernel, parity, edges, aliases):
+    def by_parity(kernel, parity, before, edges, aliases):
         return call(
             functools.partial(kernel, parity=parity, axis=axis),
-            (split, field, field, split, *edges),
+            (before, field, field, rounded, *edges),
             2,
             work,
             dict(aliases),
@@ -513,24 +514,25 @@
 
     first_half = {2: 0, 3: 1}
     second_half = {2: 0, 3: 1, 4: 2, 5: 3}
-    hl1, t1, t2, hl2, send = by_parity(middle_kernel, 0, (edge,), first_half)(
+    hl1, t1, t2, hl2, send = by_parity(middle_kernel, 0, split, (edge,), first_half)(
         tab, aff, hl1, part, halo_part, recv_a, recv_even
     )
     got_odd = shift(send, -1, axis)
-    hl1, t1, t2, hl2, send = by_parity(middle_kernel, 1, (edge,), second_half)(
+    hl1, t1, t2, hl2, send = by_parity(middle_kernel, 1, split, (edge,), second_half)(
         tab, aff, hl1, t1, t2, hl2, halo_part, recv_a, recv_odd
     )
     got_even = shift(send, 1, axis)
     part, hl3, halo_part, send_a = call(
-        functools.partial(rest_kernel, step=2), (field, split, edge_sum, edge), 1, [sums_h]
+        functools.partial(rest_kernel, step=2), (field, rounded, edge_sum, edge), 1, [sums_h]
     )(tab, aff, t2, hl2)
     recv_a = to_chip_partner(send_a, axis)
     gram = call(early_kernel, early, 0.1)(t0, t1, t2)
-    hl3, t3, t4, hl4, send, send_a = by_parity(last_kernel, 1, (half, half), first_half)(
+    last1 = by_parity(last_kernel, 1, rounded, (half, half), first_half)
+    hl3, t3, t4, hl4, send, send_a = last1(
         tab, aff, hl3, part, halo_part, recv_a, got_odd
     )
     recv_even = shift(send, 1, axis)
-    last0 = by_parity(last_kernel, 0, (half, half), {**second_half, 6: 5})
+    last0 = by_parity(last_kernel, 0, rounded, (half, half), {**second_half, 6: 5})
     _, t3, t4, hl4, send, send_a = last0(
         tab, aff, hl3, t3, t4, hl4, send_a, halo_part, recv_a, got_even
     )

time: 48.4 us -> 47.8 us (0.988)
  Pallas kernels: 10.3 us -> 9.62 us
    pallas_call x10, Pallas kernels: 5.93 us -> 5.42 us  [run(): pl.pallas_call(kernel, out_shape=out_shape, in_specs=specs, out_specs=(VM...]
  transfers between devices with their start and end apart: 10 -> 10, of which waited for: 5 -> 5; matrix products, arithmetic and copies ran while one was open for 0% -> 0% of each run, Pallas kernels for 6% -> 5%
where the time goes in v9:
time: 47.8 us; the launch traced here: 47.6 us
  starting transfers between devices  15.8 us (33%)
  waiting for transfers between devices  11.3 us (24%)
  blocking collectives  10.9 us (23%)
  Pallas kernels  9.62 us (20%)
    all_to_all x1, blocking collectives, shards(): parts = lax.all_to_all(parts, axis, 0, 0, axis_index_groups=groups)  10.9 us
    ppermute x4, starting transfers between devices, to_chip_partner(): lax.ppermute(block, axis, [(i, i ^ 1) for i in range(lax.axis_size(axis))])  10.8 us
    ppermute x6, waiting for transfers between devices, shift(): return lax.ppermute(block, axis, [(i, (i + by) % n) for i in range(n)])  10.8 us
    pallas_call x10, Pallas kernels, run(): pl.pallas_call(kernel, out_shape=out_shape, in_specs=specs, out_specs=(VM...  5.42 us
    ppermute x6, starting transfers between devices, shift(): return lax.ppermute(block, axis, [(i, (i + by) % n) for i in range(n)])  4.98 us
    pallas_call x1, Pallas kernels, shards(): pl.pallas_call(functools.partial(first_kernel, bounds=bounds, axis=axis),...  3.13 us
    pallas_call x1, Pallas kernels, shards(): pl.pallas_call(final_kernel, out_shape=jax.ShapeDtypeStruct((count * rows...  1.07 us
  transfers between devices with their start and end apart: 10, of which 5 were waited for; matrix products, arithmetic and copies ran while one was open for 0% of the time, Pallas kernels for 5%

profile of v9, /device:TPU:1, one launch (start us, length us, event | category | flops | bytes accessed | tf_op | source)
XLA Modules:
  0.0 47.6 jit_solution(2242830878045374330)
XLA Ops:
  0.0 3.1 %first.1 = (f32[12,128,128]{2,1,0:T(8,128)S(1)}, bf16[19,128,128]{2,1,0:T(8,128)(2,1)S(1)}, bf16[6,128,128]{2,1,0:T(8,128)(2,1)S(1)}, bf16[12,4,128,128]{3,2,1,0:T(8,128)(2,1)S(1)}, s32[128]{0:T(128)S(4)}) custom-call(bf16[1536,768]{1,0:T(8,128)(2,1)} %desc.1, bf16[128,768]{1,0:T(8,128)(2,1)} %queries.1, bf16[12,4,128,128]{3,2,1,0:T(8,128)(2,1)} %affinity.1, ...), custom_call_target="tpu_custom_call" | custom-call | flops 402653184 | bytes 4194304 | tf_op jit(solution)/shard_map/first/pallas_call | solution.py:475
  3.1 0.8 %shard_map.46 = (f32[12,128,128]{2,1,0:T(8,128)S(1)}, bf16[19,128,256]{2,1,0:T(8,128)(2,1)S(1)}, f32[6,128,128]{2,1,0:T(8,128)S(1)}, bf16[6,128,128]{2,1,0:T(8,128)(2,1)S(1)}) custom-call(s32[128]{0:T(128)S(4)} %get-tuple-element.38.tab, bf16[12,4,128,128]{3,2,1,0:T(8,128)(2,1)S(1)} %get-tuple-element.39.aff, f32[12,128,128]{2,1,0:T(8,128)S(1)} %get-tuple-element.40.t.t0, ...), custom_call_target="tpu_custom_call" | custom-call | flops 402653184 | bytes 4194304 | tf_op jit(solution)/shard_map/pallas_call | solution.py:459
  3.9 0.1 collective-permute-start
  4.0 2.7 %collective-permute-start.1 = (bf16[6,128,128]{2,1,0:T(8,128)(2,1)S(1)}, bf16[6,128,128]{2,1,0:T(8,128)(2,1)S(1)}, u32[]{:S(2)}, u32[]{:S(2)}) collective-permute-start(bf16[6,128,128]{2,1,0:T(8,128)(2,1)S(1)} %get-tuple-element.46), channel_id=1, source_target_pairs={{0,1},{1,2},{2,3},{3,4},{4,5},{5,6},{6,7},{7,8},{8,9},{9,10},{10,1... | collective-permute-start | bytes 589832 | tf_op jit(solution)/shard_map/ppermute | solution.py:427
  6.7 2.6 %collective-permute-done.1.refs_4_ = bf16[6,128,128]{2,1,0:T(8,128)(2,1)S(1)} collective-permute-done((bf16[6,128,128]{2,1,0:T(8,128)(2,1)S(1)}, bf16[6,128,128]{2,1,0:T(8,128)(2,1)S(1)}, u32[]{:S(2)}, u32[]{:S(2)}) %collective-permute-start.1) | collective-permute-done | bytes 196640 | tf_op jit(solution)/shard_map/ppermute | solution.py:427
  9.3 4.6 %collective-permute-done.2.refs_6_ = bf16[6,128,128]{2,1,0:T(8,128)(2,1)S(1)} collective-permute-done((bf16[6,128,128]{2,1,0:T(8,128)(2,1)S(1)}, bf16[6,128,128]{2,1,0:T(8,128)(2,1)S(1)}, u32[]{:S(2)}, u32[]{:S(2)}) %collective-permute-start.2) | collective-permute-done | bytes 196640 | tf_op jit(solution)/shard_map/ppermute | solution.py:427
  13.9 1.2 %shard_map.48 = (bf16[19,128,256]{2,1,0:T(8,128)(2,1)S(1)}, f32[12,128,128]{2,1,0:T(8,128)S(1)}, f32[12,128,128]{2,1,0:T(8,128)S(1)}, bf16[19,128,128]{2,1,0:T(8,128)(2,1)S(1)}, bf16[6,128,128]{2,1,0:T(8,128)(2,1)S(1)}) custom-call(s32[128]{0:T(128)S(4)} %get-tuple-element.38.tab, ...), custom_call_target="tpu_custom_call", output_to_operand_aliasing={{0}: (2, {}), {1}: (3, {}), {2}: (4, {}), {3}: (5, {})} | custom-call | flops 805306368 | bytes 4194304 | tf_op jit(solution)/shard_map/pallas_call | solution.py:459
  15.1 0.8 %shard_map.49 = (f32[12,128,128]{2,1,0:T(8,128)S(1)}, bf16[19,128,128]{2,1,0:T(8,128)(2,1)S(1)}, f32[6,128,128]{2,1,0:T(8,128)S(1)}, bf16[6,128,128]{2,1,0:T(8,128)(2,1)S(1)}) custom-call(s32[128]{0:T(128)S(4)} %get-tuple-element.38.tab, bf16[12,4,128,128]{3,2,1,0:T(8,128)(2,1)S(1)} %get-tuple-element.39.aff, f32[12,128,128]{2,1,0:T(8,128)S(1)} %get-tuple-element.51.t.t2, ...), custom_call_target="tpu_custom_call" | custom-call | flops 402653184 | bytes 4194304 | tf_op jit(solution)/shard_map/pallas_call | solution.py:459
  15.9 0.1 collective-permute-start.3
  16.0 0.5 %collective-permute-start.4 = (bf16[6,128,128]{2,1,0:T(8,128)(2,1)S(1)}, bf16[6,128,128]{2,1,0:T(8,128)(2,1)S(1)}, u32[]{:S(2)}, u32[]{:S(2)}) collective-permute-start(bf16[6,128,128]{2,1,0:T(8,128)(2,1)S(1)} %get-tuple-element.57), channel_id=1, source_target_pairs={{0,15},{1,0},{2,1},{3,2},{4,3},{5,4},{6,5},{7,6},{8,7},{9,8},{10,9... | collective-permute-start | bytes 589832 | tf_op jit(solution)/shard_map/ppermute | solution.py:427
  16.5 1.3 %collective-permute-start.5 = (bf16[6,128,128]{2,1,0:T(8,128)(2,1)S(1)}, bf16[6,128,128]{2,1,0:T(8,128)(2,1)S(1)}, u32[]{:S(2)}, u32[]{:S(2)}) collective-permute-start(bf16[6,128,128]{2,1,0:T(8,128)(2,1)S(1)} %get-tuple-element.63), channel_id=1, source_target_pairs={{0,1},{1,2},{2,3},{3,4},{4,5},{5,6},{6,7},{7,8},{8,9},{9,10},{10,1... | collective-permute-start | bytes 589832 | tf_op jit(solution)/shard_map/ppermute | solution.py:427
  17.8 3.3 %collective-permute-done.4.refs_4_ = bf16[6,128,128]{2,1,0:T(8,128)(2,1)S(1)} collective-permute-done((bf16[6,128,128]{2,1,0:T(8,128)(2,1)S(1)}, bf16[6,128,128]{2,1,0:T(8,128)(2,1)S(1)}, u32[]{:S(2)}, u32[]{:S(2)}) %collective-permute-start.4) | collective-permute-done | bytes 196640 | tf_op jit(solution)/shard_map/ppermute | solution.py:427
  21.1 0.9 %shard_map.50 = (bf16[19,128,128]{2,1,0:T(8,128)(2,1)S(1)}, f32[12,128,128]{2,1,0:T(8,128)S(1)}, f32[12,128,128]{2,1,0:T(8,128)S(1)}, bf16[19,128,128]{2,1,0:T(8...) custom-call(s32[128]{0:T(128)S(4)} %get-tuple-element.38.tab, ...), custom_call_target="tpu_custom_call", output_to_operand_aliasing={{0}: (2, {}), {1}: (3, {})} | custom-call | flops 805306368 | bytes 4194304 | tf_op jit(solution)/shard_map/pallas_call | solution.py:459
  22.0 0.3 collective-permute-done.5.refs_7_
  22.3 6.6 %collective-permute-start.6 = (bf16[3,128,128]{2,1,0:T(8,128)(2,1)S(1)}, bf16[3,128,128]{2,1,0:T(8,128)(2,1)S(1)}, u32[]{:S(2)}, u32[]{:S(2)}) collective-permute-start(bf16[3,128,128]{2,1,0:T(8,128)(2,1)S(1)} %get-tuple-element.65), channel_id=1, source_target_pairs={{0,1},{1,0},{2,3},{3,2},{4,5},{5,4},{6,7},{7,6},{8,9},{9,8},{10,11... | collective-permute-start | bytes 294920 | tf_op jit(solution)/shard_map/ppermute | solution.py:422
  28.8 0.5 %collective-permute-start.8 = (bf16[3,128,128]{2,1,0:T(8,128)(2,1)S(1)}, bf16[3,128,128]{2,1,0:T(8,128)(2,1)S(1)}, u32[]{:S(2)}, u32[]{:S(2)}) collective-permute-start(bf16[3,128,128]{2,1,0:T(8,128)(2,1)S(1)} %get-tuple-element.67), channel_id=1, source_target_pairs={{0,15},{1,0},{2,1},{3,2},{4,3},{5,4},{6,5},{7,6},{8,7},{9,8},{10,9... | collective-permute-start | bytes 294920 | tf_op jit(solution)/shard_map/ppermute | solution.py:427
  29.3 0.8 %shard_map.53.early = f32[6,128]{1,0:T(8,128)S(1)} custom-call(f32[12,128,128]{2,1,0:T(8,128)S(1)} %get-tuple-element.40.t.t0, f32[12,128,128]{2,1,0:T(8,128)S(1)} %get-tuple-element.70.t1, f32[12,128,128]{2,1,0:T(8,128)S(1)} %get-tuple-element.51.t.t2), custom_call_target="tpu_custom_call" | custom-call | flops 40265320 | bytes 4194304 | tf_op jit(solution)/shard_map/pallas_call | solution.py:459
  30.1 0.6 %shard_map.54.gram = f32[11,128]{1,0:T(8,128)S(1)} custom-call(s32[128]{0:T(128)S(4)} %get-tuple-element.38.tab, bf16[12,4,128,128]{3,2,1,0:T(8,128)(2,1)S(1)} %get-tuple-element.39.aff, f32[12,128,128]{2,1,0:T(8,128)S(1)} %get-tuple-element.51.t.t2, f32[12,128,128]{2,1,0:T(8,128)S(1)} %get-tuple-element.68.t3, f32[12,128,128]{2,1,0:T(8,128)S(1)} %get-tuple-element.69.t4, ...), custom_call_target="tpu_custom_call" | custom-call | flops 402653184 | bytes 4194304 | tf_op jit(solution)/shard_map/pallas_call | solution.py:459
  30.7 4.1 %collective-permute-start.9 = (f32[11,128]{1,0:T(8,128)S(1)}, f32[11,128]{1,0:T(8,128)S(1)}, u32[]{:S(2)}, u32[]{:S(2)}) collective-permute-start(f32[11,128]{1,0:T(8,128)S(1)} %shard_map.54.gram), channel_id=1, source_target_pairs={{0,1},{1,0},{2,3},{3,2},{4,5},{5,4},{6,7},{7,6},{8,9},{9,8},{10,11... | collective-permute-start | bytes 16904 | tf_op jit(solution)/shard_map/ppermute | solution.py:422
  34.8 0.3 shard_map.52.weight
  35.1 0.5 %collective-permute-done.9.other = f32[11,128]{1,0:T(8,128)S(1)} collective-permute-done((f32[11,128]{1,0:T(8,128)S(1)}, f32[11,128]{1,0:T(8,128)S(1)}, u32[]{:S(2)}, u32[]{:S(2)}) %collective-permute-start.9) | collective-permute-done | bytes 5664 | tf_op jit(solution)/shard_map/ppermute | solution.py:422
  35.6 0.1 shard_map.55
  35.7 10.9 %all_to_all.5.parts = f32[8,11,128]{2,1,0:T(8,128)S(1)} all-to-all(f32[8,11,128]{2,1,0:T(8,128)S(1)} %shard_map.55), channel_id=1, replica_groups={{0,2,4,6,8,10,12,14},{1,3,5,7,9,11,13,15},{16,18,20,22,24,26,28,30},{17..., dimensions={0} | all-to-all | bytes 90112 | tf_op jit(solution)/shard_map/all_to_all | solution.py:554
  46.6 1.1 %final.1 = f32[1536,128]{1,0:T(8,128)} custom-call(f32[8,11,128]{2,1,0:T(8,128)S(1)} %all_to_all.5.parts, f32[12,128,128]{2,1,0:T(8,128)S(1)} %get-tuple-element.40.t.t0, f32[12,128,128]{2,1,0:T(8,128)S(1)} %get-tuple-element.70.t1, f32[12,128,128]{2,1,0:T(8,128)S(1)} %get-tuple-element.51.t.t2, f32[12,128,128]{2,1,0:T(8,128)S(1)} %get-tuple-element.68.t3, ...), custom_call_target="tpu_custom_call" | custom-call | tf_op jit(solution)/shard_map/final/pallas_call | solution.py:555
  (9 shorter events, 0.1 us)
Async XLA Ops:
  3.9 2.8 %collective-permute-start = (bf16[6,128,128]{2,1,0:T(8,128)(2,1)S(1)}, bf16[6,128,128]{2,1,0:T(8,128)(2,1)S(1)}, u32[]{:S(2)}, u32[]{:S(2)}) collective-permute-start(bf16[6,128,128]{2,1,0:T(8,128)(2,1)S(1)} %get-tuple-element.45), channel_id=1, source_target_pairs={{0,1},{1,0},{2,3},{3,2},{4,5},{5,4},{6,7},{7,6},{8,9},{9,8},{10,11... | collective-permute-start | bytes 589832 | tf_op jit(solution)/shard_map/ppermute | solution.py:422
  4.0 5.3 %collective-permute-start.1 = (bf16[6,128,128]{2,1,0:T(8,128)(2,1)S(1)}, bf16[6,128,128]{2,1,0:T(8,128)(2,1)S(1)}, u32[]{:S(2)}, u32[]{:S(2)}) collective-permute-start(bf16[6,128,128]{2,1,0:T(8,128)(2,1)S(1)} %get-tuple-element.46), channel_id=1, source_target_pairs={{0,1},{1,2},{2,3},{3,4},{4,5},{5,6},{6,7},{7,8},{8,9},{9,10},{10,1... | collective-permute-start | bytes 589832 | tf_op jit(solution)/shard_map/ppermute | solution.py:427
  6.7 7.2 %collective-permute-start.2 = (bf16[6,128,128]{2,1,0:T(8,128)(2,1)S(1)}, bf16[6,128,128]{2,1,0:T(8,128)(2,1)S(1)}, u32[]{:S(2)}, u32[]{:S(2)}) collective-permute-start(bf16[6,128,128]{2,1,0:T(8,128)(2,1)S(1)} %get-tuple-element.46), channel_id=1, source_target_pairs={{0,15},{1,0},{2,1},{3,2},{4,3},{5,4},{6,5},{7,6},{8,7},{9,8},{10,9... | collective-permute-start | bytes 589832 | tf_op jit(solution)/shard_map/ppermute | solution.py:427
  15.9 1.9 %collective-permute-start.3 = (bf16[6,128,128]{2,1,0:T(8,128)(2,1)S(1)}, bf16[6,128,128]{2,1,0:T(8,128)(2,1)S(1)}, u32[]{:S(2)}, u32[]{:S(2)}) collective-permute-start(bf16[6,128,128]{2,1,0:T(8,128)(2,1)S(1)} %get-tuple-element.56), channel_id=1, source_target_pairs={{0,1},{1,0},{2,3},{3,2},{4,5},{5,4},{6,7},{7,6},{8,9},{9,8},{10,11... | collective-permute-start | bytes 589832 | tf_op jit(solution)/shard_map/ppermute | solution.py:422
  16.0 5.1 %collective-permute-start.4 = (bf16[6,128,128]{2,1,0:T(8,128)(2,1)S(1)}, bf16[6,128,128]{2,1,0:T(8,128)(2,1)S(1)}, u32[]{:S(2)}, u32[]{:S(2)}) collective-permute-start(bf16[6,128,128]{2,1,0:T(8,128)(2,1)S(1)} %get-tuple-element.57), channel_id=1, source_target_pairs={{0,15},{1,0},{2,1},{3,2},{4,3},{5,4},{6,5},{7,6},{8,7},{9,8},{10,9... | collective-permute-start | bytes 589832 | tf_op jit(solution)/shard_map/ppermute | solution.py:427
  16.5 5.8 %collective-permute-start.5 = (bf16[6,128,128]{2,1,0:T(8,128)(2,1)S(1)}, bf16[6,128,128]{2,1,0:T(8,128)(2,1)S(1)}, u32[]{:S(2)}, u32[]{:S(2)}) collective-permute-start(bf16[6,128,128]{2,1,0:T(8,128)(2,1)S(1)} %get-tuple-element.63), channel_id=1, source_target_pairs={{0,1},{1,2},{2,3},{3,4},{4,5},{5,6},{6,7},{7,8},{8,9},{9,10},{10,1... | collective-permute-start | bytes 589832 | tf_op jit(solution)/shard_map/ppermute | solution.py:427
  22.3 13.3 %collective-permute-start.6 = (bf16[3,128,128]{2,1,0:T(8,128)(2,1)S(1)}, bf16[3,128,128]{2,1,0:T(8,128)(2,1)S(1)}, u32[]{:S(2)}, u32[]{:S(2)}) collective-permute-start(bf16[3,128,128]{2,1,0:T(8,128)(2,1)S(1)} %get-tuple-element.65), channel_id=1, source_target_pairs={{0,1},{1,0},{2,3},{3,2},{4,5},{5,4},{6,7},{7,6},{8,9},{9,8},{10,11... | collective-permute-start | bytes 294920 | tf_op jit(solution)/shard_map/ppermute | solution.py:422
  28.8 6.8 %collective-permute-start.7 = (bf16[3,128,128]{2,1,0:T(8,128)(2,1)S(1)}, bf16[3,128,128]{2,1,0:T(8,128)(2,1)S(1)}, u32[]{:S(2)}, u32[]{:S(2)}) collective-permute-start(bf16[3,128,128]{2,1,0:T(8,128)(2,1)S(1)} %get-tuple-element.66), channel_id=1, source_target_pairs={{0,1},{1,2},{2,3},{3,4},{4,5},{5,6},{6,7},{7,8},{8,9},{9,10},{10,1... | collective-permute-start | bytes 294920 | tf_op jit(solution)/shard_map/ppermute | solution.py:427
  28.8 6.8 %collective-permute-start.8 = (bf16[3,128,128]{2,1,0:T(8,128)(2,1)S(1)}, bf16[3,128,128]{2,1,0:T(8,128)(2,1)S(1)}, u32[]{:S(2)}, u32[]{:S(2)}) collective-permute-start(bf16[3,128,128]{2,1,0:T(8,128)(2,1)S(1)} %get-tuple-element.67), channel_id=1, source_target_pairs={{0,15},{1,0},{2,1},{3,2},{4,3},{5,4},{6,5},{7,6},{8,7},{9,8},{10,9... | collective-permute-start | bytes 294920 | tf_op jit(solution)/shard_map/ppermute | solution.py:427
  30.7 4.9 %collective-permute-start.9 = (f32[11,128]{1,0:T(8,128)S(1)}, f32[11,128]{1,0:T(8,128)S(1)}, u32[]{:S(2)}, u32[]{:S(2)}) collective-permute-start(f32[11,128]{1,0:T(8,128)S(1)} %shard_map.54.gram), channel_id=1, source_target_pairs={{0,1},{1,0},{2,3},{3,2},{4,5},{5,4},{6,7},{7,6},{8,9},{9,8},{10,11... | collective-permute-start | bytes 16904 | tf_op jit(solution)/shard_map/ppermute | solution.py:422

commit v10 on v9

--- a/solution.py
+++ b/solution.py
@@ -103,11 +103,8 @@
         relative.append((rel, place, bit))
         ups.append(up)
         lows.append(low)
-    yield
     up_count = low_count = up_cross = low_cross = jnp.int32(0)
     for g in range(count):
-        if g == count // 2:
-            yield
         rel, place, bit = relative[g]
         below = jnp.where(ups[g], up_mask, low_mask) & (bit - 1)
         rank = below & 1
@@ -144,7 +141,6 @@
             tab[at] = jnp.where(j < used, rows[1, j], 0)
             tab[at + 1] = jnp.int32(3)
             tab[at + 2] = jnp.where(j < used, rows[2, j], 2 * NAMED)
-    yield
 
 
 def pack(tab, shift, aff, t, hl, send, base):
@@ -186,10 +182,10 @@
             t0[g] = value
             put_rounded(hl, g, value)
 
-    stages = fill_table(cols, tab, up_rows, low_rows, axis)
     for c in range(chunks):
         copies[c].wait()
-        next(stages, None)
+        if c == 0:
+            fill_table(cols, tab, up_rows, low_rows, axis)
         scores = dot(buf[parts[c], :], tall[...])
         for i, g in enumerate(range(bounds[c], bounds[c + 1])):
             t0[g] = scores[i * rows : (i + 1) * rows]
@@ -288,8 +284,9 @@
 
 
 def last_kernel(tab, aff, *refs, parity, axis):
-    halo_part, recv_a, recv_b = refs[-10:-7]
-    hl3, t3, t4, hl4, send_b, send_a, halo = refs[-7:]
+    outs = 5 if parity == 0 else 6
+    halo_part, recv_a, recv_b = refs[-outs - 4 : -outs - 1]
+    hl3, t3, t4, hl4, send_a, *send_b, halo = refs[-outs - 1 :]
     width = t3.shape[2]
     _, lists, _, _ = offsets(t3.shape[0])
     active = lax.rem(lax.axis_index(axis), 2) == parity
@@ -298,12 +295,15 @@
     def _():
         two_steps(tab, aff, hl3, t3, halo_part, recv_a, recv_b, t4, hl4, halo, 2)
         for j in range(NAMED):
-            send_b[j] = hl4[tab[lists + NAMED + j], :, :width]
             send_a[j] = hl4[tab[lists + j], :, :width]
-
-    @pl.when(jnp.logical_not(active))
-    def _():
-        send_b[...] = jnp.zeros(send_b.shape, BF)
+            for ref in send_b:
+                ref[j] = hl4[tab[lists + NAMED + j], :, :width]
+
+    if send_b:
+
+        @pl.when(jnp.logical_not(active))
+        def _():
+            send_b[0][...] = jnp.zeros(send_b[0].shape, BF)
 
 
 def gram_kernel(tab, aff, t2, t3, t4, hl, early, out):
@@ -327,26 +327,23 @@
         weight[h] = sums[h]
 
 
-def cross_kernel(weight, recv_a, recv_even, recv_odd, gram, other, out, recv_b, *, axis):
+def cross_kernel(weight, recv_a, recv_b, gram, out, *, axis):
     _, rows, width = weight.shape
     even = lax.rem(lax.axis_index(axis), 2) == 0
+    out[...] = gram[...]
 
     @pl.when(even)
     def _():
-        recv_b[...] = recv_even[...]
-
-    @pl.when(jnp.logical_not(even))
-    def _():
-        recv_b[...] = recv_odd[...]
-
-    total = jnp.zeros((8, width), F32)
-    for h in range(NAMED):
-        part = weight[h] * recv_a[h].astype(F32) + weight[NAMED + h] * recv_b[h].astype(F32)
-        total = total + part.reshape(rows // 8, 8, width).sum(0)
-    value = gram[...] + other[...]
-    extra = jnp.sum(total, axis=0, keepdims=True)
-    index = lax.broadcasted_iota(jnp.int32, value.shape, 0)
-    value = value + jnp.where(index == ROWS - 1, extra, 0.0)
+        total = jnp.zeros((8, width), F32)
+        for h in range(NAMED):
+            part = weight[h] * recv_a[h].astype(F32) + weight[NAMED + h] * recv_b[h].astype(F32)
+            total = total + part.reshape(rows // 8, 8, width).sum(0)
+        last = pl.ds(ROWS - 1, 1)
+        out[last, :] = out[last, :] + jnp.sum(total, axis=0, keepdims=True)
+
+
+def spread_kernel(own, other, out):
+    value = own[...] + other[...]
     for d in range(out.shape[0]):
         out[d] = value
 
@@ -444,7 +441,7 @@
     edge_sum = jax.ShapeDtypeStruct((2 * NAMED, rows, width), F32)
     sums_h = pltpu.VMEM((2 * NAMED + 1, rows, width), F32)
     work = [pltpu.VMEM((2 * NAMED + 1, rows, width), BF)]
-    bounds = (0, count // 6, count // 2, count - count // 6, count)
+    bounds = (0, count)
     flops = 2 * count * rows * 4 * rows * 2 * width
 
     def call(kernel, out_shape, products, scratch=(), aliases=None, limit=24):
@@ -528,29 +525,27 @@
     recv_a = to_chip_partner(send_a, axis)
     gram = call(early_kernel, early, 0.1)(t0, t1, t2)
     last1 = by_parity(last_kernel, 1, rounded, (half, half), first_half)
-    hl3, t3, t4, hl4, send, send_a = last1(
+    hl3, t3, t4, hl4, send_a, send = last1(
         tab, aff, hl3, part, halo_part, recv_a, got_odd
     )
-    recv_even = shift(send, 1, axis)
-    last0 = by_parity(last_kernel, 0, rounded, (half, half), {**second_half, 6: 5})
-    _, t3, t4, hl4, send, send_a = last0(
+    recv_b = shift(send, 1, axis)
+    last0 = by_parity(last_kernel, 0, rounded, (half,), {**second_half, 6: 4})
+    _, t3, t4, hl4, send_a = last0(
         tab, aff, hl3, t3, t4, hl4, send_a, halo_part, recv_a, got_even
     )
-    recv_odd = shift(send, -1, axis)
     recv_a = to_chip_partner(send_a, axis)
     gram = call(
         gram_kernel, jax.ShapeDtypeStruct((ROWS, width), F32), 1
     )(tab, aff, t2, t3, t4, hl4, gram)
+    weight = call(weight_kernel, edge_sum, 0.2, [sums_h])(tab, aff, hl4)
+    entries = jax.ShapeDtypeStruct((ROWS, width), F32)
+    gram = call(functools.partial(cross_kernel, axis=axis), entries, 0.1, limit=8)(
+        weight, recv_a, recv_b, gram
+    )
     other = to_chip_partner(gram, axis)
-    weight = call(weight_kernel, edge_sum, 0.2, [sums_h])(tab, aff, hl4)
-    parts = call(
-        functools.partial(cross_kernel, axis=axis),
-        jax.ShapeDtypeStruct((devices // 2, ROWS, width), F32),
-        0.1,
-        [pltpu.VMEM((NAMED, rows, width), BF)],
-        limit=8,
-    )(weight, recv_a, recv_even, recv_odd, gram, other)
-    groups = [list(range(core, devices, 2)) for core in range(2)]
+    copies = jax.ShapeDtypeStruct((devices // 2, ROWS, width), F32)
+    parts = call(spread_kernel, copies, 0.1, limit=8)(gram, other)
+    groups = [[2 * k + (k + core) % 2 for k in range(devices // 2)] for core in range(2)]
     parts = lax.all_to_all(parts, axis, 0, 0, axis_index_groups=groups)
     return pl.pallas_call(
         final_kernel,

time: 47.8 us -> 46.9 us (0.981)
  the two profiles are of different devices: /device:TPU:1 before, /device:TPU:0 now
where the time goes in v10:
time: 46.9 us; the launch traced here: 46.7 us
  waiting for transfers between devices  17 us (36%)
  starting transfers between devices  11.3 us (24%)
  Pallas kernels  9.54 us (20%)
  blocking collectives  8.79 us (19%)
    ppermute x5, waiting for transfers between devices, shift(): return lax.ppermute(block, axis, [(i, (i + by) % n) for i in range(n)])  15.8 us
    ppermute x5, starting transfers between devices, shift(): return lax.ppermute(block, axis, [(i, (i + by) % n) for i in range(n)])  9.79 us
    all_to_all x1, blocking collectives, shards(): parts = lax.all_to_all(parts, axis, 0, 0, axis_index_groups=groups)  8.79 us
    pallas_call x11, Pallas kernels, run(): pl.pallas_call(kernel, out_shape=out_shape, in_specs=specs, out_specs=(VM...  5.41 us
    pallas_call x1, Pallas kernels, shards(): pl.pallas_call(functools.partial(first_kernel, bounds=bounds, axis=axis),...  3.06 us
    ppermute x4, starting transfers between devices, to_chip_partner(): lax.ppermute(block, axis, [(i, i ^ 1) for i in range(lax.axis_size(axis))])  1.46 us
    ppermute x4, waiting for transfers between devices, to_chip_partner(): lax.ppermute(block, axis, [(i, i ^ 1) for i in range(lax.axis_size(axis))])  1.17 us
    pallas_call x1, Pallas kernels, shards(): pl.pallas_call(final_kernel, out_shape=jax.ShapeDtypeStruct((count * rows...  1.07 us
  transfers between devices with their start and end apart: 9, of which 5 were waited for; matrix products, arithmetic and copies ran while one was open for 0% of the time, Pallas kernels for 6%

profile of v10, /device:TPU:0, one launch (start us, length us, event | category | flops | bytes accessed | tf_op | source)
XLA Modules:
  0.0 46.7 jit_solution(17526119146755136899)
XLA Ops:
  0.0 3.1 %first.1 = (f32[12,128,128]{2,1,0:T(8,128)S(1)}, bf16[19,128,128]{2,1,0:T(8,128)(2,1)S(1)}, bf16[6,128,128]{2,1,0:T(8,128)(2,1)S(1)}, bf16[12,4,128,128]{3,2,1,0:T(8,128)(2,1)S(1)}, s32[128]{0:T(128)S(4)}) custom-call(bf16[1536,768]{1,0:T(8,128)(2,1)} %desc.1, bf16[128,768]{1,0:T(8,128)(2,1)} %queries.1, bf16[12,4,128,128]{3,2,1,0:T(8,128)(2,1)} %affinity.1, ...), custom_call_target="tpu_custom_call" | custom-call | flops 402653184 | bytes 4194304 | tf_op jit(solution)/shard_map/first/pallas_call | solution.py:472
  3.1 0.8 %shard_map.46 = (f32[12,128,128]{2,1,0:T(8,128)S(1)}, bf16[19,128,256]{2,1,0:T(8,128)(2,1)S(1)}, f32[6,128,128]{2,1,0:T(8,128)S(1)}, bf16[6,128,128]{2,1,0:T(8,128)(2,1)S(1)}) custom-call(s32[128]{0:T(128)S(4)} %get-tuple-element.37.tab, bf16[12,4,128,128]{3,2,1,0:T(8,128)(2,1)S(1)} %get-tuple-element.38.aff, f32[12,128,128]{2,1,0:T(8,128)S(1)} %get-tuple-element.39.t.t0, ...), custom_call_target="tpu_custom_call" | custom-call | flops 402653184 | bytes 4194304 | tf_op jit(solution)/shard_map/pallas_call | solution.py:456
  3.9 0.6 %collective-permute-start = (bf16[6,128,128]{2,1,0:T(8,128)(2,1)S(1)}, bf16[6,128,128]{2,1,0:T(8,128)(2,1)S(1)}, u32[]{:S(2)}, u32[]{:S(2)}) collective-permute-start(bf16[6,128,128]{2,1,0:T(8,128)(2,1)S(1)} %get-tuple-element.44), channel_id=1, source_target_pairs={{0,1},{1,0},{2,3},{3,2},{4,5},{5,4},{6,7},{7,6},{8,9},{9,8},{10,11... | collective-permute-start | bytes 589832 | tf_op jit(solution)/shard_map/ppermute | solution.py:419
  4.4 0.1 collective-permute-start.1
  4.5 5.6 %collective-permute-start.2 = (bf16[6,128,128]{2,1,0:T(8,128)(2,1)S(1)}, bf16[6,128,128]{2,1,0:T(8,128)(2,1)S(1)}, u32[]{:S(2)}, u32[]{:S(2)}) collective-permute-start(bf16[6,128,128]{2,1,0:T(8,128)(2,1)S(1)} %get-tuple-element.45), channel_id=1, source_target_pairs={{0,15},{1,0},{2,1},{3,2},{4,3},{5,4},{6,5},{7,6},{8,7},{9,8},{10,9... | collective-permute-start | bytes 589832 | tf_op jit(solution)/shard_map/ppermute | solution.py:424
  10.1 3.4 %collective-permute-done.1.refs_4_ = bf16[6,128,128]{2,1,0:T(8,128)(2,1)S(1)} collective-permute-done((bf16[6,128,128]{2,1,0:T(8,128)(2,1)S(1)}, bf16[6,128,128]{2,1,0:T(8,128)(2,1)S(1)}, u32[]{:S(2)}, u32[]{:S(2)}) %collective-permute-start.1) | collective-permute-done | bytes 196640 | tf_op jit(solution)/shard_map/ppermute | solution.py:424
  13.5 1.2 %shard_map.47 = (bf16[19,128,256]{2,1,0:T(8,128)(2,1)S(1)}, f32[12,128,128]{2,1,0:T(8,128)S(1)}, f32[12,128,128]{2,1,0:T(8,128)S(1)}, bf16[19,128,128]{2,1,0:T(8,128)(2,1)S(1)}, bf16[6,128,128]{2,1,0:T(8,128)(2,1)S(1)}) custom-call(s32[128]{0:T(128)S(4)} %get-tuple-element.37.tab, ...), custom_call_target="tpu_custom_call", output_to_operand_aliasing={{0}: (2, {}), {1}: (3, {})} | custom-call | flops 805306368 | bytes 4194304 | tf_op jit(solution)/shard_map/pallas_call | solution.py:456
  14.8 0.8 %shard_map.49 = (f32[12,128,128]{2,1,0:T(8,128)S(1)}, bf16[19,128,128]{2,1,0:T(8,128)(2,1)S(1)}, f32[6,128,128]{2,1,0:T(8,128)S(1)}, bf16[6,128,128]{2,1,0:T(8,128)(2,1)S(1)}) custom-call(s32[128]{0:T(128)S(4)} %get-tuple-element.37.tab, bf16[12,4,128,128]{3,2,1,0:T(8,128)(2,1)S(1)} %get-tuple-element.38.aff, f32[12,128,128]{2,1,0:T(8,128)S(1)} %get-tuple-element.50.t.t2, ...), custom_call_target="tpu_custom_call" | custom-call | flops 402653184 | bytes 4194304 | tf_op jit(solution)/shard_map/pallas_call | solution.py:456
  15.6 0.8 %collective-permute-start.3 = (bf16[6,128,128]{2,1,0:T(8,128)(2,1)S(1)}, bf16[6,128,128]{2,1,0:T(8,128)(2,1)S(1)}, u32[]{:S(2)}, u32[]{:S(2)}) collective-permute-start(bf16[6,128,128]{2,1,0:T(8,128)(2,1)S(1)} %get-tuple-element.55), channel_id=1, source_target_pairs={{0,1},{1,0},{2,3},{3,2},{4,5},{5,4},{6,7},{7,6},{8,9},{9,8},{10,11... | collective-permute-start | bytes 589832 | tf_op jit(solution)/shard_map/ppermute | solution.py:419
  16.4 3.6 %collective-permute-start.4 = (bf16[6,128,128]{2,1,0:T(8,128)(2,1)S(1)}, bf16[6,128,128]{2,1,0:T(8,128)(2,1)S(1)}, u32[]{:S(2)}, u32[]{:S(2)}) collective-permute-start(bf16[6,128,128]{2,1,0:T(8,128)(2,1)S(1)} %get-tuple-element.56), channel_id=1, source_target_pairs={{0,15},{1,0},{2,1},{3,2},{4,3},{5,4},{6,5},{7,6},{8,7},{9,8},{10,9... | collective-permute-start | bytes 589832 | tf_op jit(solution)/shard_map/ppermute | solution.py:424
  20.0 3.2 %collective-permute-done.4.refs_4_ = bf16[6,128,128]{2,1,0:T(8,128)(2,1)S(1)} collective-permute-done((bf16[6,128,128]{2,1,0:T(8,128)(2,1)S(1)}, bf16[6,128,128]{2,1,0:T(8,128)(2,1)S(1)}, u32[]{:S(2)}, u32[]{:S(2)}) %collective-permute-start.4) | collective-permute-done | bytes 196640 | tf_op jit(solution)/shard_map/ppermute | solution.py:424
  23.2 4.6 %collective-permute-done.5.refs_7_ = bf16[6,128,128]{2,1,0:T(8,128)(2,1)S(1)} collective-permute-done((bf16[6,128,128]{2,1,0:T(8,128)(2,1)S(1)}, bf16[6,128,128]{2,1,0:T(8,128)(2,1)S(1)}, u32[]{:S(2)}, u32[]{:S(2)}) %collective-permute-start.5) | collective-permute-done | bytes 196640 | tf_op jit(solution)/shard_map/ppermute | solution.py:424
  27.8 0.8 %shard_map.51 = (bf16[19,128,128]{2,1,0:T(8,128)(2,1)S(1)}, f32[12,128,128]{2,1,0:T(8,128)S(1)}, f32[12,128,128]{2,1,0:T(8,128)S(1)}, bf16[19,128,128]{2,1,0:T(8,128)(2,1)S(1)}, bf16[3,128,128]{2,1,0:T(8,128)(2,1)S(1)}) custom-call(s32[128]{0:T(128)S(4)} %get-tuple-element.37.tab, ...), custom_call_target="tpu_custom_call", output_to_operand_aliasing={{0}: (2, {}), {1}: (3, {}), {2}: (4, {}), {3}: (5, {}), {4}... | custom-call | flops 805306368 | bytes 4194304 | tf_op jit(solution)/shard_map/pallas_call | solution.py:456
  28.7 0.1 collective-permute-start.6
  28.7 0.5 %collective-permute-start.7 = (bf16[3,128,128]{2,1,0:T(8,128)(2,1)S(1)}, bf16[3,128,128]{2,1,0:T(8,128)(2,1)S(1)}, u32[]{:S(2)}, u32[]{:S(2)}) collective-permute-start(bf16[3,128,128]{2,1,0:T(8,128)(2,1)S(1)} %get-tuple-element.65), channel_id=1, source_target_pairs={{0,1},{1,2},{2,3},{3,4},{4,5},{5,6},{6,7},{7,8},{8,9},{9,10},{10,1... | collective-permute-start | bytes 294920 | tf_op jit(solution)/shard_map/ppermute | solution.py:424
  29.2 0.8 %shard_map.53.early = f32[6,128]{1,0:T(8,128)S(1)} custom-call(f32[12,128,128]{2,1,0:T(8,128)S(1)} %get-tuple-element.39.t.t0, f32[12,128,128]{2,1,0:T(8,128)S(1)} %get-tuple-element.68.t1, f32[12,128,128]{2,1,0:T(8,128)S(1)} %get-tuple-element.50.t.t2), custom_call_target="tpu_custom_call" | custom-call | flops 40265320 | bytes 4194304 | tf_op jit(solution)/shard_map/pallas_call | solution.py:456
  30.0 0.3 shard_map.52.weight
  30.3 0.6 %shard_map.54.gram = f32[11,128]{1,0:T(8,128)S(1)} custom-call(s32[128]{0:T(128)S(4)} %get-tuple-element.37.tab, bf16[12,4,128,128]{3,2,1,0:T(8,128)(2,1)S(1)} %get-tuple-element.38.aff, f32[12,128,128]{2,1,0:T(8,128)S(1)} %get-tuple-element.50.t.t2, f32[12,128,128]{2,1,0:T(8,128)S(1)} %get-tuple-element.66.t3, f32[12,128,128]{2,1,0:T(8,128)S(1)} %get-tuple-element.67.t4, ...), custom_call_target="tpu_custom_call" | custom-call | flops 402653184 | bytes 4194304 | tf_op jit(solution)/shard_map/pallas_call | solution.py:456
  30.9 4.6 %collective-permute-done.7.recv_b = bf16[3,128,128]{2,1,0:T(8,128)(2,1)S(1)} collective-permute-done((bf16[3,128,128]{2,1,0:T(8,128)(2,1)S(1)}, bf16[3,128,128]{2,1,0:T(8,128)(2,1)S(1)}, u32[]{:S(2)}, u32[]{:S(2)}) %collective-permute-start.7) | collective-permute-done | bytes 98336 | tf_op jit(solution)/shard_map/ppermute | solution.py:424
  35.5 0.1 shard_map.55.own
  35.6 0.1 collective-permute-start.8
  35.7 1.2 %collective-permute-done.8.other = f32[11,128]{1,0:T(8,128)S(1)} collective-permute-done((f32[11,128]{1,0:T(8,128)S(1)}, f32[11,128]{1,0:T(8,128)S(1)}, u32[]{:S(2)}, u32[]{:S(2)}) %collective-permute-start.8) | collective-permute-done | bytes 5664 | tf_op jit(solution)/shard_map/ppermute | solution.py:419
  36.8 8.8 %all_to_all.5.parts = f32[8,11,128]{2,1,0:T(8,128)S(1)} all-to-all(f32[8,11,128]{2,1,0:T(8,128)S(1)} %shard_map.56), channel_id=1, replica_groups={{0,3,4,7,8,11,12,15},{1,2,5,6,9,10,13,14},{16,19,20,23,24,27,28,31},{17..., dimensions={0} | all-to-all | bytes 90112 | tf_op jit(solution)/shard_map/all_to_all | solution.py:549
  45.6 1.1 %final.1 = f32[1536,128]{1,0:T(8,128)} custom-call(f32[8,11,128]{2,1,0:T(8,128)S(1)} %all_to_all.5.parts, f32[12,128,128]{2,1,0:T(8,128)S(1)} %get-tuple-element.39.t.t0, f32[12,128,128]{2,1,0:T(8,128)S(1)} %get-tuple-element.68.t1, f32[12,128,128]{2,1,0:T(8,128)S(1)} %get-tuple-element.50.t.t2, f32[12,128,128]{2,1,0:T(8,128)S(1)} %get-tuple-element.66.t3, ...), custom_call_target="tpu_custom_call" | custom-call | tf_op jit(solution)/shard_map/final/pallas_call | solution.py:550
  (8 shorter events, 0.1 us)
Async XLA Ops:
  3.9 6.2 %collective-permute-start = (bf16[6,128,128]{2,1,0:T(8,128)(2,1)S(1)}, bf16[6,128,128]{2,1,0:T(8,128)(2,1)S(1)}, u32[]{:S(2)}, u32[]{:S(2)}) collective-permute-start(bf16[6,128,128]{2,1,0:T(8,128)(2,1)S(1)} %get-tuple-element.44), channel_id=1, source_target_pairs={{0,1},{1,0},{2,3},{3,2},{4,5},{5,4},{6,7},{7,6},{8,9},{9,8},{10,11... | collective-permute-start | bytes 589832 | tf_op jit(solution)/shard_map/ppermute | solution.py:419
  4.4 9.1 %collective-permute-start.1 = (bf16[6,128,128]{2,1,0:T(8,128)(2,1)S(1)}, bf16[6,128,128]{2,1,0:T(8,128)(2,1)S(1)}, u32[]{:S(2)}, u32[]{:S(2)}) collective-permute-start(bf16[6,128,128]{2,1,0:T(8,128)(2,1)S(1)} %get-tuple-element.45), channel_id=1, source_target_pairs={{0,1},{1,2},{2,3},{3,4},{4,5},{5,6},{6,7},{7,8},{8,9},{9,10},{10,1... | collective-permute-start | bytes 589832 | tf_op jit(solution)/shard_map/ppermute | solution.py:424
  4.5 10.3 %collective-permute-start.2 = (bf16[6,128,128]{2,1,0:T(8,128)(2,1)S(1)}, bf16[6,128,128]{2,1,0:T(8,128)(2,1)S(1)}, u32[]{:S(2)}, u32[]{:S(2)}) collective-permute-start(bf16[6,128,128]{2,1,0:T(8,128)(2,1)S(1)} %get-tuple-element.45), channel_id=1, source_target_pairs={{0,15},{1,0},{2,1},{3,2},{4,3},{5,4},{6,5},{7,6},{8,7},{9,8},{10,9... | collective-permute-start | bytes 589832 | tf_op jit(solution)/shard_map/ppermute | solution.py:424
  15.6 4.4 %collective-permute-start.3 = (bf16[6,128,128]{2,1,0:T(8,128)(2,1)S(1)}, bf16[6,128,128]{2,1,0:T(8,128)(2,1)S(1)}, u32[]{:S(2)}, u32[]{:S(2)}) collective-permute-start(bf16[6,128,128]{2,1,0:T(8,128)(2,1)S(1)} %get-tuple-element.55), channel_id=1, source_target_pairs={{0,1},{1,0},{2,3},{3,2},{4,5},{5,4},{6,7},{7,6},{8,9},{9,8},{10,11... | collective-permute-start | bytes 589832 | tf_op jit(solution)/shard_map/ppermute | solution.py:419
  16.4 6.8 %collective-permute-start.4 = (bf16[6,128,128]{2,1,0:T(8,128)(2,1)S(1)}, bf16[6,128,128]{2,1,0:T(8,128)(2,1)S(1)}, u32[]{:S(2)}, u32[]{:S(2)}) collective-permute-start(bf16[6,128,128]{2,1,0:T(8,128)(2,1)S(1)} %get-tuple-element.56), channel_id=1, source_target_pairs={{0,15},{1,0},{2,1},{3,2},{4,3},{5,4},{6,5},{7,6},{8,7},{9,8},{10,9... | collective-permute-start | bytes 589832 | tf_op jit(solution)/shard_map/ppermute | solution.py:424
  20.0 7.8 %collective-permute-start.5 = (bf16[6,128,128]{2,1,0:T(8,128)(2,1)S(1)}, bf16[6,128,128]{2,1,0:T(8,128)(2,1)S(1)}, u32[]{:S(2)}, u32[]{:S(2)}) collective-permute-start(bf16[6,128,128]{2,1,0:T(8,128)(2,1)S(1)} %get-tuple-element.62), channel_id=1, source_target_pairs={{0,1},{1,2},{2,3},{3,4},{4,5},{5,6},{6,7},{7,8},{8,9},{9,10},{10,1... | collective-permute-start | bytes 589832 | tf_op jit(solution)/shard_map/ppermute | solution.py:424
  28.7 2.3 %collective-permute-start.6 = (bf16[3,128,128]{2,1,0:T(8,128)(2,1)S(1)}, bf16[3,128,128]{2,1,0:T(8,128)(2,1)S(1)}, u32[]{:S(2)}, u32[]{:S(2)}) collective-permute-start(bf16[3,128,128]{2,1,0:T(8,128)(2,1)S(1)} %get-tuple-element.64), channel_id=1, source_target_pairs={{0,1},{1,0},{2,3},{3,2},{4,5},{5,4},{6,7},{7,6},{8,9},{9,8},{10,11... | collective-permute-start | bytes 294920 | tf_op jit(solution)/shard_map/ppermute | solution.py:419
  28.7 6.8 %collective-permute-start.7 = (bf16[3,128,128]{2,1,0:T(8,128)(2,1)S(1)}, bf16[3,128,128]{2,1,0:T(8,128)(2,1)S(1)}, u32[]{:S(2)}, u32[]{:S(2)}) collective-permute-start(bf16[3,128,128]{2,1,0:T(8,128)(2,1)S(1)} %get-tuple-element.65), channel_id=1, source_target_pairs={{0,1},{1,2},{2,3},{3,4},{4,5},{5,6},{6,7},{7,8},{8,9},{9,10},{10,1... | collective-permute-start | bytes 294920 | tf_op jit(solution)/shard_map/ppermute | solution.py:424
  35.6 1.2 %collective-permute-start.8 = (f32[11,128]{1,0:T(8,128)S(1)}, f32[11,128]{1,0:T(8,128)S(1)}, u32[]{:S(2)}, u32[]{:S(2)}) collective-permute-start(f32[11,128]{1,0:T(8,128)S(1)} %shard_map.55.own), channel_id=1, source_target_pairs={{0,1},{1,0},{2,3},{3,2},{4,5},{5,4},{6,7},{7,6},{8,9},{9,8},{10,11... | collective-permute-start | bytes 16904 | tf_op jit(solution)/shard_map/ppermute | solution.py:419

commit v11 on v10

--- a/solution.py
+++ b/solution.py
@@ -243,11 +243,10 @@
         out[pl.ds(n, 1), :] = jnp.sum(total, axis=0, keepdims=True)
 
 
-def two_steps(tab, aff, hl1, t1, halo_part, recv_a, recv_b, t2, hl2, halo, step):
-    count, _, _ = t2.shape
-    full, lists, cross, _ = offsets(count)
+def complete(tab, aff, hl1, t1, halo_part, recv_a, recv_b, halo):
+    count = t1.shape[0]
+    _, lists, cross, _ = offsets(count)
     hl1[count + 2 * NAMED] = jnp.zeros(hl1.shape[1:], BF)
-    hl2[count + 2 * NAMED] = jnp.zeros(hl2.shape[1:], BF)
     halo[2 * NAMED] = jnp.zeros(halo.shape[1:], BF)
     for h in range(NAMED):
         halo[h] = recv_a[h]
@@ -261,8 +260,14 @@
     for j in range(2 * NAMED):
         g = tab[lists + j]
         put_rounded(hl1, g, t1[g])
+
+
+def advance(tab, aff, hl1, t1, t2, hl2, step):
+    count = t1.shape[0]
+    full = offsets(count)[0]
+    hl2[count + 2 * NAMED] = jnp.zeros(hl2.shape[1:], BF)
     for g in range(count):
-        value = shifted(row_product(aff, tab, full, g, hl1), SHIFTS[step + 1], t1[g])
+        value = shifted(row_product(aff, tab, full, g, hl1), SHIFTS[step], t1[g])
         t2[g] = value
         put_rounded(hl2, g, value)
 
@@ -275,7 +280,8 @@
 
     @pl.when(active)
     def _():
-        two_steps(tab, aff, hl1, t1, halo_part, recv_a, recv_b, t2, hl2, halo, 0)
+        complete(tab, aff, hl1, t1, halo_part, recv_a, recv_b, halo)
+        advance(tab, aff, hl1, t1, t2, hl2, 1)
         pack(tab, SHIFTS[2], aff, t2, hl2, send_b, lists + NAMED)
 
     @pl.when(jnp.logical_not(active))
@@ -283,27 +289,36 @@
         send_b[...] = jnp.zeros(send_b.shape, BF)
 
 
-def last_kernel(tab, aff, *refs, parity, axis):
-    outs = 5 if parity == 0 else 6
-    halo_part, recv_a, recv_b = refs[-outs - 4 : -outs - 1]
-    hl3, t3, t4, hl4, send_a, *send_b, halo = refs[-outs - 1 :]
-    width = t3.shape[2]
-    _, lists, _, _ = offsets(t3.shape[0])
-    active = lax.rem(lax.axis_index(axis), 2) == parity
-
-    @pl.when(active)
+def edge_kernel(tab, aff, _, __, halo_part, recv_a, recv_b, hl3, t3, send_b, halo, *, axis):
+    full, lists, _, _ = offsets(t3.shape[0])
+    odd = lax.rem(lax.axis_index(axis), 2) == 1
+
+    @pl.when(odd)
     def _():
-        two_steps(tab, aff, hl3, t3, halo_part, recv_a, recv_b, t4, hl4, halo, 2)
+        complete(tab, aff, hl3, t3, halo_part, recv_a, recv_b, halo)
         for j in range(NAMED):
-            send_a[j] = hl4[tab[lists + j], :, :width]
-            for ref in send_b:
-                ref[j] = hl4[tab[lists + NAMED + j], :, :width]
-
-    if send_b:
-
-        @pl.when(jnp.logical_not(active))
-        def _():
-            send_b[0][...] = jnp.zeros(send_b[0].shape, BF)
+            g = tab[lists + NAMED + j]
+            product = row_product(aff, tab, full, g, hl3)
+            send_b[j] = shifted(product, SHIFTS[3], t3[g]).astype(BF)
+
+    @pl.when(jnp.logical_not(odd))
+    def _():
+        send_b[...] = jnp.zeros(send_b.shape, BF)
+
+
+def last_kernel(
+    tab, aff, _, __, halo_part, recv_a, recv_b, hl3, t3, t4, hl4, send_a, halo, *, axis
+):
+    count, _, width = t3.shape
+    _, lists, _, _ = offsets(count)
+
+    @pl.when(lax.rem(lax.axis_index(axis), 2) == 0)
+    def _():
+        complete(tab, aff, hl3, t3, halo_part, recv_a, recv_b, halo)
+
+    advance(tab, aff, hl3, t3, t4, hl4, 3)
+    for j in range(NAMED):
+        send_a[j] = hl4[tab[lists + j], :, :width]
 
 
 def gram_kernel(tab, aff, t2, t3, t4, hl, early, out):
@@ -524,15 +539,17 @@
     )(tab, aff, t2, hl2)
     recv_a = to_chip_partner(send_a, axis)
     gram = call(early_kernel, early, 0.1)(t0, t1, t2)
-    last1 = by_parity(last_kernel, 1, rounded, (half, half), first_half)
-    hl3, t3, t4, hl4, send_a, send = last1(
-        tab, aff, hl3, part, halo_part, recv_a, got_odd
-    )
+    hl3, t3, send = call(
+        functools.partial(edge_kernel, axis=axis), (rounded, field, half), 0.5, work, first_half
+    )(tab, aff, hl3, part, halo_part, recv_a, got_odd)
     recv_b = shift(send, 1, axis)
-    last0 = by_parity(last_kernel, 0, rounded, (half,), {**second_half, 6: 4})
-    _, t3, t4, hl4, send_a = last0(
-        tab, aff, hl3, t3, t4, hl4, send_a, halo_part, recv_a, got_even
-    )
+    _, t3, t4, hl4, send_a = call(
+        functools.partial(last_kernel, axis=axis),
+        (rounded, field, field, rounded, half),
+        1,
+        work,
+        first_half,
+    )(tab, aff, hl3, t3, halo_part, recv_a, got_even)
     recv_a = to_chip_partner(send_a, axis)
     gram = call(
         gram_kernel, jax.ShapeDtypeStruct((ROWS, width), F32), 1

time: 46.9 us -> 38.2 us (0.81)
  waiting for transfers between devices: 17 us -> 9.5 us
  starting transfers between devices: 11.3 us -> 9.69 us
    ppermute x5, waiting for transfers between devices: 15.8 us -> 8.15 us  [shift(): return lax.ppermute(block, axis, [(i, (i + by) % n) for i in range(n)])]
    ppermute x5, starting transfers between devices: 9.79 us -> 4.68 us  [shift(): return lax.ppermute(block, axis, [(i, (i + by) % n) for i in range(n)])]
    ppermute x4, starting transfers between devices: 1.46 us -> 5.01 us  [to_chip_partner(): lax.ppermute(block, axis, [(i, i ^ 1) for i in range(lax.axis_size(axis))])]
  transfers between devices with their start and end apart: 9 -> 9, of which waited for: 5 -> 5; matrix products, arithmetic and copies ran while one was open for 0% -> 0% of each run, Pallas kernels for 6% -> 14%
where the time goes in v11:
time: 38.2 us; the launch traced here: 38 us
  starting transfers between devices  9.69 us (25%)
  Pallas kernels  9.57 us (25%)
  waiting for transfers between devices  9.5 us (25%)
  blocking collectives  9.18 us (24%)
    all_to_all x1, blocking collectives, shards(): parts = lax.all_to_all(parts, axis, 0, 0, axis_index_groups=groups)  9.18 us
    ppermute x5, waiting for transfers between devices, shift(): return lax.ppermute(block, axis, [(i, (i + by) % n) for i in range(n)])  8.15 us
    pallas_call x11, Pallas kernels, run(): pl.pallas_call(kernel, out_shape=out_shape, in_specs=specs, out_specs=(VM...  5.44 us
    ppermute x4, starting transfers between devices, to_chip_partner(): lax.ppermute(block, axis, [(i, i ^ 1) for i in range(lax.axis_size(axis))])  5.01 us
    ppermute x5, starting transfers between devices, shift(): return lax.ppermute(block, axis, [(i, (i + by) % n) for i in range(n)])  4.68 us
    pallas_call x1, Pallas kernels, shards(): pl.pallas_call(functools.partial(first_kernel, bounds=bounds, axis=axis),...  3.06 us
    ppermute x4, waiting for transfers between devices, to_chip_partner(): lax.ppermute(block, axis, [(i, i ^ 1) for i in range(lax.axis_size(axis))])  1.34 us
    pallas_call x1, Pallas kernels, shards(): pl.pallas_call(final_kernel, out_shape=jax.ShapeDtypeStruct((count * rows...  1.07 us
  transfers between devices with their start and end apart: 9, of which 5 were waited for; matrix products, arithmetic and copies ran while one was open for 0% of the time, Pallas kernels for 14%

profile of v11, /device:TPU:0, one launch (start us, length us, event | category | flops | bytes accessed | tf_op | source)
XLA Modules:
  0.0 38.0 jit_solution(2803646330972214011)
XLA Ops:
  0.0 3.1 %first.1 = (f32[12,128,128]{2,1,0:T(8,128)S(1)}, bf16[19,128,128]{2,1,0:T(8,128)(2,1)S(1)}, bf16[6,128,128]{2,1,0:T(8,128)(2,1)S(1)}, bf16[12,4,128,128]{3,2,1,0:T(8,128)(2,1)S(1)}, s32[128]{0:T(128)S(4)}) custom-call(bf16[1536,768]{1,0:T(8,128)(2,1)} %desc.1, bf16[128,768]{1,0:T(8,128)(2,1)} %queries.1, bf16[12,4,128,128]{3,2,1,0:T(8,128)(2,1)} %affinity.1, ...), custom_call_target="tpu_custom_call" | custom-call | flops 402653184 | bytes 4194304 | tf_op jit(solution)/shard_map/first/pallas_call | solution.py:487
  3.1 0.5 %collective-permute-start.1 = (bf16[6,128,128]{2,1,0:T(8,128)(2,1)S(1)}, bf16[6,128,128]{2,1,0:T(8,128)(2,1)S(1)}, u32[]{:S(2)}, u32[]{:S(2)}) collective-permute-start(bf16[6,128,128]{2,1,0:T(8,128)(2,1)S(1)} %get-tuple-element.42), channel_id=1, source_target_pairs={{0,1},{1,2},{2,3},{3,4},{4,5},{5,6},{6,7},{7,8},{8,9},{9,10},{10,1... | collective-permute-start | bytes 589832 | tf_op jit(solution)/shard_map/ppermute | solution.py:439
  3.6 0.8 %shard_map.46 = (f32[12,128,128]{2,1,0:T(8,128)S(1)}, bf16[19,128,256]{2,1,0:T(8,128)(2,1)S(1)}, f32[6,128,128]{2,1,0:T(8,128)S(1)}, bf16[6,128,128]{2,1,0:T(8,128)(2,1)S(1)}) custom-call(s32[128]{0:T(128)S(4)} %get-tuple-element.34.tab, bf16[12,4,128,128]{3,2,1,0:T(8,128)(2,1)S(1)} %get-tuple-element.35.aff, f32[12,128,128]{2,1,0:T(8,128)S(1)} %get-tuple-element.36.t.t0, ...), custom_call_target="tpu_custom_call" | custom-call | flops 402653184 | bytes 4194304 | tf_op jit(solution)/shard_map/pallas_call | solution.py:471
  4.4 2.7 %collective-permute-start = (bf16[6,128,128]{2,1,0:T(8,128)(2,1)S(1)}, bf16[6,128,128]{2,1,0:T(8,128)(2,1)S(1)}, u32[]{:S(2)}, u32[]{:S(2)}) collective-permute-start(bf16[6,128,128]{2,1,0:T(8,128)(2,1)S(1)} %get-tuple-element.41), channel_id=1, source_target_pairs={{0,1},{1,0},{2,3},{3,2},{4,5},{5,4},{6,7},{7,6},{8,9},{9,8},{10,11... | collective-permute-start | bytes 589832 | tf_op jit(solution)/shard_map/ppermute | solution.py:434
  7.1 3.1 %collective-permute-start.2 = (bf16[6,128,128]{2,1,0:T(8,128)(2,1)S(1)}, bf16[6,128,128]{2,1,0:T(8,128)(2,1)S(1)}, u32[]{:S(2)}, u32[]{:S(2)}) collective-permute-start(bf16[6,128,128]{2,1,0:T(8,128)(2,1)S(1)} %get-tuple-element.42), channel_id=1, source_target_pairs={{0,15},{1,0},{2,1},{3,2},{4,3},{5,4},{6,5},{7,6},{8,7},{9,8},{10,9... | collective-permute-start | bytes 589832 | tf_op jit(solution)/shard_map/ppermute | solution.py:439
  10.1 1.9 %collective-permute-done.1.refs_4_ = bf16[6,128,128]{2,1,0:T(8,128)(2,1)S(1)} collective-permute-done((bf16[6,128,128]{2,1,0:T(8,128)(2,1)S(1)}, bf16[6,128,128]{2,1,0:T(8,128)(2,1)S(1)}, u32[]{:S(2)}, u32[]{:S(2)}) %collective-permute-start.1) | collective-permute-done | bytes 196640 | tf_op jit(solution)/shard_map/ppermute | solution.py:439
  12.0 1.2 %shard_map.47 = (bf16[19,128,256]{2,1,0:T(8,128)(2,1)S(1)}, f32[12,128,128]{2,1,0:T(8,128)S(1)}, f32[12,128,128]{2,1,0:T(8,128)S(1)}, bf16[19,128,128]{2,1,0:T(8,128)(2,1)S(1)}, bf16[6,128,128]{2,1,0:T(8,128)(2,1)S(1)}) custom-call(s32[128]{0:T(128)S(4)} %get-tuple-element.34.tab, ...), custom_call_target="tpu_custom_call", output_to_operand_aliasing={{0}: (2, {}), {1}: (3, {})} | custom-call | flops 805306368 | bytes 4194304 | tf_op jit(solution)/shard_map/pallas_call | solution.py:471
  13.4 0.8 %shard_map.49 = (f32[12,128,128]{2,1,0:T(8,128)S(1)}, bf16[19,128,128]{2,1,0:T(8,128)(2,1)S(1)}, f32[6,128,128]{2,1,0:T(8,128)S(1)}, bf16[6,128,128]{2,1,0:T(8,128)(2,1)S(1)}) custom-call(s32[128]{0:T(128)S(4)} %get-tuple-element.34.tab, bf16[12,4,128,128]{3,2,1,0:T(8,128)(2,1)S(1)} %get-tuple-element.35.aff, f32[12,128,128]{2,1,0:T(8,128)S(1)} %get-tuple-element.47.t.t2, ...), custom_call_target="tpu_custom_call" | custom-call | flops 402653184 | bytes 4194304 | tf_op jit(solution)/shard_map/pallas_call | solution.py:471
  14.2 1.8 %collective-permute-start.3 = (bf16[6,128,128]{2,1,0:T(8,128)(2,1)S(1)}, bf16[6,128,128]{2,1,0:T(8,128)(2,1)S(1)}, u32[]{:S(2)}, u32[]{:S(2)}) collective-permute-start(bf16[6,128,128]{2,1,0:T(8,128)(2,1)S(1)} %get-tuple-element.52), channel_id=1, source_target_pairs={{0,1},{1,0},{2,3},{3,2},{4,5},{5,4},{6,7},{7,6},{8,9},{9,8},{10,11... | collective-permute-start | bytes 589832 | tf_op jit(solution)/shard_map/ppermute | solution.py:434
  15.9 0.1 collective-permute-start.5
  16.0 0.5 %collective-permute-done.4.recv_b = bf16[6,128,128]{2,1,0:T(8,128)(2,1)S(1)} collective-permute-done((bf16[6,128,128]{2,1,0:T(8,128)(2,1)S(1)}, bf16[6,128,128]{2,1,0:T(8,128)(2,1)S(1)}, u32[]{:S(2)}, u32[]{:S(2)}) %collective-permute-start.4) | collective-permute-done | bytes 196640 | tf_op jit(solution)/shard_map/ppermute | solution.py:439
  16.5 0.5 %collective-permute-done.3.recv_a = bf16[6,128,128]{2,1,0:T(8,128)(2,1)S(1)} collective-permute-done((bf16[6,128,128]{2,1,0:T(8,128)(2,1)S(1)}, bf16[6,128,128]{2,1,0:T(8,128)(2,1)S(1)}, u32[]{:S(2)}, u32[]{:S(2)}) %collective-permute-start.3) | collective-permute-done | bytes 196640 | tf_op jit(solution)/shard_map/ppermute | solution.py:434
  17.0 1.0 %collective-permute-start.7 = (bf16[3,128,128]{2,1,0:T(8,128)(2,1)S(1)}, bf16[3,128,128]{2,1,0:T(8,128)(2,1)S(1)}, u32[]{:S(2)}, u32[]{:S(2)}) collective-permute-start(bf16[3,128,128]{2,1,0:T(8,128)(2,1)S(1)} %get-tuple-element.59), channel_id=1, source_target_pairs={{0,1},{1,2},{2,3},{3,4},{4,5},{5,6},{6,7},{7,8},{8,9},{9,10},{10,1... | collective-permute-start | bytes 294920 | tf_op jit(solution)/shard_map/ppermute | solution.py:439
  18.0 5.7 %collective-permute-done.5.recv_b = bf16[6,128,128]{2,1,0:T(8,128)(2,1)S(1)} collective-permute-done((bf16[6,128,128]{2,1,0:T(8,128)(2,1)S(1)}, bf16[6,128,128]{2,1,0:T(8,128)(2,1)S(1)}, u32[]{:S(2)}, u32[]{:S(2)}) %collective-permute-start.5) | collective-permute-done | bytes 196640 | tf_op jit(solution)/shard_map/ppermute | solution.py:439
  23.7 0.9 %shard_map.51 = (bf16[19,128,128]{2,1,0:T(8,128)(2,1)S(1)}, f32[12,128,128]{2,1,0:T(8,128)S(1)}, f32[12,128,128]{2,1,0:T(8,128)S(1)}, bf16[19,128,128]{2,1,0:T(8,128)(2,1)S(1)}, bf16[3,128,128]{2,1,0:T(8,128)(2,1)S(1)}) custom-call(s32[128]{0:T(128)S(4)} %get-tuple-element.34.tab, ...), custom_call_target="tpu_custom_call", output_to_operand_aliasing={{0}: (2, {}), {1}: (3, {})} | custom-call | flops 402653184 | bytes 4194304 | tf_op jit(solution)/shard_map/pallas_call | solution.py:471
  24.6 0.1 collective-permute-start.6
  24.7 0.8 %shard_map.53.early = f32[6,128]{1,0:T(8,128)S(1)} custom-call(f32[12,128,128]{2,1,0:T(8,128)S(1)} %get-tuple-element.36.t.t0, f32[12,128,128]{2,1,0:T(8,128)S(1)} %get-tuple-element.62.t1, f32[12,128,128]{2,1,0:T(8,128)S(1)} %get-tuple-element.47.t.t2), custom_call_target="tpu_custom_call" | custom-call | flops 40265320 | bytes 4194304 | tf_op jit(solution)/shard_map/pallas_call | solution.py:471
  25.5 0.3 shard_map.52.weight
  25.8 0.6 %shard_map.54.gram = f32[11,128]{1,0:T(8,128)S(1)} custom-call(s32[128]{0:T(128)S(4)} %get-tuple-element.34.tab, bf16[12,4,128,128]{3,2,1,0:T(8,128)(2,1)S(1)} %get-tuple-element.35.aff, f32[12,128,128]{2,1,0:T(8,128)S(1)} %get-tuple-element.47.t.t2, f32[12,128,128]{2,1,0:T(8,128)S(1)} %get-tuple-element.60.t3, f32[12,128,128]{2,1,0:T(8,128)S(1)} %get-tuple-element.61.t4, ...), custom_call_target="tpu_custom_call" | custom-call | flops 402653184 | bytes 4194304 | tf_op jit(solution)/shard_map/pallas_call | solution.py:471
  26.4 0.1 shard_map.55.own
  26.5 0.5 %collective-permute-start.8 = (f32[11,128]{1,0:T(8,128)S(1)}, f32[11,128]{1,0:T(8,128)S(1)}, u32[]{:S(2)}, u32[]{:S(2)}) collective-permute-start(f32[11,128]{1,0:T(8,128)S(1)} %shard_map.55.own), channel_id=1, source_target_pairs={{0,1},{1,0},{2,3},{3,2},{4,5},{5,4},{6,7},{7,6},{8,9},{9,8},{10,11... | collective-permute-start | bytes 16904 | tf_op jit(solution)/shard_map/ppermute | solution.py:434
  27.0 0.8 %collective-permute-done.8.other = f32[11,128]{1,0:T(8,128)S(1)} collective-permute-done((f32[11,128]{1,0:T(8,128)S(1)}, f32[11,128]{1,0:T(8,128)S(1)}, u32[]{:S(2)}, u32[]{:S(2)}) %collective-permute-start.8) | collective-permute-done | bytes 5664 | tf_op jit(solution)/shard_map/ppermute | solution.py:434
  27.8 9.2 %all_to_all.5.parts = f32[8,11,128]{2,1,0:T(8,128)S(1)} all-to-all(f32[8,11,128]{2,1,0:T(8,128)S(1)} %shard_map.56), channel_id=1, replica_groups={{0,3,4,7,8,11,12,15},{1,2,5,6,9,10,13,14},{16,19,20,23,24,27,28,31},{17..., dimensions={0} | all-to-all | bytes 90112 | tf_op jit(solution)/shard_map/all_to_all | solution.py:566
  37.0 1.1 %final.1 = f32[1536,128]{1,0:T(8,128)} custom-call(f32[8,11,128]{2,1,0:T(8,128)S(1)} %all_to_all.5.parts, f32[12,128,128]{2,1,0:T(8,128)S(1)} %get-tuple-element.36.t.t0, f32[12,128,128]{2,1,0:T(8,128)S(1)} %get-tuple-element.62.t1, f32[12,128,128]{2,1,0:T(8,128)S(1)} %get-tuple-element.47.t.t2, f32[12,128,128]{2,1,0:T(8,128)S(1)} %get-tuple-element.60.t3, ...), custom_call_target="tpu_custom_call" | custom-call | tf_op jit(solution)/shard_map/final/pallas_call | solution.py:567
  (8 shorter events, 0.1 us)
Async XLA Ops:
  3.1 9.0 %collective-permute-start.1 = (bf16[6,128,128]{2,1,0:T(8,128)(2,1)S(1)}, bf16[6,128,128]{2,1,0:T(8,128)(2,1)S(1)}, u32[]{:S(2)}, u32[]{:S(2)}) collective-permute-start(bf16[6,128,128]{2,1,0:T(8,128)(2,1)S(1)} %get-tuple-element.42), channel_id=1, source_target_pairs={{0,1},{1,2},{2,3},{3,4},{4,5},{5,6},{6,7},{7,8},{8,9},{9,10},{10,1... | collective-permute-start | bytes 589832 | tf_op jit(solution)/shard_map/ppermute | solution.py:439
  4.4 7.6 %collective-permute-start = (bf16[6,128,128]{2,1,0:T(8,128)(2,1)S(1)}, bf16[6,128,128]{2,1,0:T(8,128)(2,1)S(1)}, u32[]{:S(2)}, u32[]{:S(2)}) collective-permute-start(bf16[6,128,128]{2,1,0:T(8,128)(2,1)S(1)} %get-tuple-element.41), channel_id=1, source_target_pairs={{0,1},{1,0},{2,3},{3,2},{4,5},{5,4},{6,7},{7,6},{8,9},{9,8},{10,11... | collective-permute-start | bytes 589832 | tf_op jit(solution)/shard_map/ppermute | solution.py:434
  7.1 6.2 %collective-permute-start.2 = (bf16[6,128,128]{2,1,0:T(8,128)(2,1)S(1)}, bf16[6,128,128]{2,1,0:T(8,128)(2,1)S(1)}, u32[]{:S(2)}, u32[]{:S(2)}) collective-permute-start(bf16[6,128,128]{2,1,0:T(8,128)(2,1)S(1)} %get-tuple-element.42), channel_id=1, source_target_pairs={{0,15},{1,0},{2,1},{3,2},{4,3},{5,4},{6,5},{7,6},{8,7},{9,8},{10,9... | collective-permute-start | bytes 589832 | tf_op jit(solution)/shard_map/ppermute | solution.py:439
  13.3 3.2 %collective-permute-start.4 = (bf16[6,128,128]{2,1,0:T(8,128)(2,1)S(1)}, bf16[6,128,128]{2,1,0:T(8,128)(2,1)S(1)}, u32[]{:S(2)}, u32[]{:S(2)}) collective-permute-start(bf16[6,128,128]{2,1,0:T(8,128)(2,1)S(1)} %get-tuple-element.53), channel_id=1, source_target_pairs={{0,15},{1,0},{2,1},{3,2},{4,3},{5,4},{6,5},{7,6},{8,7},{9,8},{10,9... | collective-permute-start | bytes 589832 | tf_op jit(solution)/shard_map/ppermute | solution.py:439
  14.2 2.8 %collective-permute-start.3 = (bf16[6,128,128]{2,1,0:T(8,128)(2,1)S(1)}, bf16[6,128,128]{2,1,0:T(8,128)(2,1)S(1)}, u32[]{:S(2)}, u32[]{:S(2)}) collective-permute-start(bf16[6,128,128]{2,1,0:T(8,128)(2,1)S(1)} %get-tuple-element.52), channel_id=1, source_target_pairs={{0,1},{1,0},{2,3},{3,2},{4,5},{5,4},{6,7},{7,6},{8,9},{9,8},{10,11... | collective-permute-start | bytes 589832 | tf_op jit(solution)/shard_map/ppermute | solution.py:434
  15.9 7.8 %collective-permute-start.5 = (bf16[6,128,128]{2,1,0:T(8,128)(2,1)S(1)}, bf16[6,128,128]{2,1,0:T(8,128)(2,1)S(1)}, u32[]{:S(2)}, u32[]{:S(2)}) collective-permute-start(bf16[6,128,128]{2,1,0:T(8,128)(2,1)S(1)} %get-tuple-element.56), channel_id=1, source_target_pairs={{0,1},{1,2},{2,3},{3,4},{4,5},{5,6},{6,7},{7,8},{8,9},{9,10},{10,1... | collective-permute-start | bytes 589832 | tf_op jit(solution)/shard_map/ppermute | solution.py:439
  17.0 9.3 %collective-permute-start.7 = (bf16[3,128,128]{2,1,0:T(8,128)(2,1)S(1)}, bf16[3,128,128]{2,1,0:T(8,128)(2,1)S(1)}, u32[]{:S(2)}, u32[]{:S(2)}) collective-permute-start(bf16[3,128,128]{2,1,0:T(8,128)(2,1)S(1)} %get-tuple-element.59), channel_id=1, source_target_pairs={{0,1},{1,2},{2,3},{3,4},{4,5},{5,6},{6,7},{7,8},{8,9},{9,10},{10,1... | collective-permute-start | bytes 294920 | tf_op jit(solution)/shard_map/ppermute | solution.py:439
  24.6 1.8 %collective-permute-start.6 = (bf16[3,128,128]{2,1,0:T(8,128)(2,1)S(1)}, bf16[3,128,128]{2,1,0:T(8,128)(2,1)S(1)}, u32[]{:S(2)}, u32[]{:S(2)}) collective-permute-start(bf16[3,128,128]{2,1,0:T(8,128)(2,1)S(1)} %get-tuple-element.58), channel_id=1, source_target_pairs={{0,1},{1,0},{2,3},{3,2},{4,5},{5,4},{6,7},{7,6},{8,9},{9,8},{10,11... | collective-permute-start | bytes 294920 | tf_op jit(solution)/shard_map/ppermute | solution.py:434
  26.5 1.3 %collective-permute-start.8 = (f32[11,128]{1,0:T(8,128)S(1)}, f32[11,128]{1,0:T(8,128)S(1)}, u32[]{:S(2)}, u32[]{:S(2)}) collective-permute-start(f32[11,128]{1,0:T(8,128)S(1)} %shard_map.55.own), channel_id=1, source_target_pairs={{0,1},{1,0},{2,3},{3,2},{4,5},{5,4},{6,7},{7,6},{8,9},{9,8},{10,11... | collective-permute-start | bytes 16904 | tf_op jit(solution)/shard_map/ppermute | solution.py:434

commit v12 on v11

--- a/solution.py
+++ b/solution.py
@@ -262,30 +262,50 @@
         put_rounded(hl1, g, t1[g])
 
 
-def advance(tab, aff, hl1, t1, t2, hl2, step):
+def advance(tab, aff, hl1, t1, t2, hl2, step, blocks=None):
     count = t1.shape[0]
     full = offsets(count)[0]
     hl2[count + 2 * NAMED] = jnp.zeros(hl2.shape[1:], BF)
-    for g in range(count):
+    for g in range(count) if blocks is None else blocks:
         value = shifted(row_product(aff, tab, full, g, hl1), SHIFTS[step], t1[g])
         t2[g] = value
         put_rounded(hl2, g, value)
 
 
-def middle_kernel(tab, aff, *refs, parity, axis):
-    halo_part, recv_a, recv_b = refs[-9:-6]
-    hl1, t1, t2, hl2, send_b, halo = refs[-6:]
+def near_kernel(
+    tab, aff, _, __, halo_part, recv_a, recv_b, hl1, t1, send_b, halo, t2, hl2, *, axis
+):
+    count = t1.shape[0]
+    _, lists, _, _ = offsets(count)
+    even = lax.rem(lax.axis_index(axis), 2) == 0
+
+    @pl.when(even)
+    def _():
+        complete(tab, aff, hl1, t1, halo_part, recv_a, recv_b, halo)
+        partner = jnp.where(tab[0] < count, tab[0], 0)
+        advance(tab, aff, hl1, t1, t2, hl2, 1, [*range(HALO_W + 1), partner])
+        pack(tab, SHIFTS[2], aff, t2, hl2, send_b, lists + NAMED)
+
+    @pl.when(jnp.logical_not(even))
+    def _():
+        send_b[...] = jnp.zeros(send_b.shape, BF)
+
+
+def middle_kernel(
+    tab, aff, _, __, halo_part, recv_a, recv_b, hl1, t1, t2, hl2, send_b, halo, *, axis
+):
     _, lists, _, _ = offsets(t1.shape[0])
-    active = lax.rem(lax.axis_index(axis), 2) == parity
-
-    @pl.when(active)
+    odd = lax.rem(lax.axis_index(axis), 2) == 1
+
+    @pl.when(odd)
     def _():
         complete(tab, aff, hl1, t1, halo_part, recv_a, recv_b, halo)
         advance(tab, aff, hl1, t1, t2, hl2, 1)
         pack(tab, SHIFTS[2], aff, t2, hl2, send_b, lists + NAMED)
 
-    @pl.when(jnp.logical_not(active))
-    def _():
+    @pl.when(jnp.logical_not(odd))
+    def _():
+        advance(tab, aff, hl1, t1, t2, hl2, 1)
         send_b[...] = jnp.zeros(send_b.shape, BF)
 
 
@@ -514,25 +534,23 @@
         functools.partial(rest_kernel, step=0), (field, split, edge_sum, edge), 1, [sums_h]
     )(tab, aff, t0, hl0)
     recv_a = to_chip_partner(send_a, axis)
-
-    def by_parity(kernel, parity, before, edges, aliases):
-        return call(
-            functools.partial(kernel, parity=parity, axis=axis),
-            (before, field, field, rounded, *edges),
-            2,
-            work,
-            dict(aliases),
-        )
-
     first_half = {2: 0, 3: 1}
-    second_half = {2: 0, 3: 1, 4: 2, 5: 3}
-    hl1, t1, t2, hl2, send = by_parity(middle_kernel, 0, split, (edge,), first_half)(
-        tab, aff, hl1, part, halo_part, recv_a, recv_even
-    )
+    hl1, t1, send = call(
+        functools.partial(near_kernel, axis=axis),
+        (split, field, edge),
+        1,
+        work
+        + [pltpu.VMEM((count, rows, width), F32), pltpu.VMEM((blocks, rows, width), BF)],
+        first_half,
+    )(tab, aff, hl1, part, halo_part, recv_a, recv_even)
     got_odd = shift(send, -1, axis)
-    hl1, t1, t2, hl2, send = by_parity(middle_kernel, 1, split, (edge,), second_half)(
-        tab, aff, hl1, t1, t2, hl2, halo_part, recv_a, recv_odd
-    )
+    _, t1, t2, hl2, send = call(
+        functools.partial(middle_kernel, axis=axis),
+        (split, field, field, rounded, edge),
+        2,
+        work,
+        first_half,
+    )(tab, aff, hl1, t1, halo_part, recv_a, recv_odd)
     got_even = shift(send, 1, axis)
     part, hl3, halo_part, send_a = call(
         functools.partial(rest_kernel, step=2), (field, rounded, edge_sum, edge), 1, [sums_h]

time: 38.2 us -> 46.9 us (1.23)
  waiting for transfers between devices: 9.5 us -> 17 us
  starting transfers between devices: 9.69 us -> 10.8 us
    ppermute x5, waiting for transfers between devices: 8.15 us -> 15.8 us  [shift(): return lax.ppermute(block, axis, [(i, (i + by) % n) for i in range(n)])]
    ppermute x5, starting transfers between devices: 4.68 us -> 9.79 us  [shift(): return lax.ppermute(block, axis, [(i, (i + by) % n) for i in range(n)])]
    ppermute x4, starting transfers between devices: 5.01 us -> 1.02 us  [to_chip_partner(): lax.ppermute(block, axis, [(i, i ^ 1) for i in range(lax.axis_size(axis))])]
  transfers between devices with their start and end apart: 9 -> 9, of which waited for: 5 -> 5; matrix products, arithmetic and copies ran while one was open for 0% -> 0% of each run, Pallas kernels for 14% -> 6%
where the time goes in v12:
time: 46.9 us; the launch traced here: 46.7 us
  waiting for transfers between devices  17 us (36%)
  starting transfers between devices  10.8 us (23%)
  Pallas kernels  10 us (21%)
  blocking collectives  8.79 us (19%)
    ppermute x5, waiting for transfers between devices, shift(): return lax.ppermute(block, axis, [(i, (i + by) % n) for i in range(n)])  15.8 us
    ppermute x5, starting transfers between devices, shift(): return lax.ppermute(block, axis, [(i, (i + by) % n) for i in range(n)])  9.79 us
    all_to_all x1, blocking collectives, shards(): parts = lax.all_to_all(parts, axis, 0, 0, axis_index_groups=groups)  8.79 us
    pallas_call x11, Pallas kernels, run(): pl.pallas_call(kernel, out_shape=out_shape, in_specs=specs, out_specs=(VM...  5.87 us
    pallas_call x1, Pallas kernels, shards(): pl.pallas_call(functools.partial(first_kernel, bounds=bounds, axis=axis),...  3.06 us
    ppermute x4, waiting for transfers between devices, to_chip_partner(): lax.ppermute(block, axis, [(i, i ^ 1) for i in range(lax.axis_size(axis))])  1.17 us
    pallas_call x1, Pallas kernels, shards(): pl.pallas_call(final_kernel, out_shape=jax.ShapeDtypeStruct((count * rows...  1.07 us
    ppermute x4, starting transfers between devices, to_chip_partner(): lax.ppermute(block, axis, [(i, i ^ 1) for i in range(lax.axis_size(axis))])  1.02 us
  transfers between devices with their start and end apart: 9, of which 5 were waited for; matrix products, arithmetic and copies ran while one was open for 0% of the time, Pallas kernels for 6%

profile of v12, /device:TPU:0, one launch (start us, length us, event | category | flops | bytes accessed | tf_op | source)
XLA Modules:
  0.0 46.7 jit_solution(12827182895143071657)
XLA Ops:
  0.0 3.1 %first.1 = (f32[12,128,128]{2,1,0:T(8,128)S(1)}, bf16[19,128,128]{2,1,0:T(8,128)(2,1)S(1)}, bf16[6,128,128]{2,1,0:T(8,128)(2,1)S(1)}, bf16[12,4,128,128]{3,2,1,0:T(8,128)(2,1)S(1)}, s32[128]{0:T(128)S(4)}) custom-call(bf16[1536,768]{1,0:T(8,128)(2,1)} %desc.1, bf16[128,768]{1,0:T(8,128)(2,1)} %queries.1, bf16[12,4,128,128]{3,2,1,0:T(8,128)(2,1)} %affinity.1, ...), custom_call_target="tpu_custom_call" | custom-call | flops 402653184 | bytes 4194304 | tf_op jit(solution)/shard_map/first/pallas_call | solution.py:507
  3.1 0.8 %shard_map.46 = (f32[12,128,128]{2,1,0:T(8,128)S(1)}, bf16[19,128,256]{2,1,0:T(8,128)(2,1)S(1)}, f32[6,128,128]{2,1,0:T(8,128)S(1)}, bf16[6,128,128]{2,1,0:T(8,128)(2,1)S(1)}) custom-call(s32[128]{0:T(128)S(4)} %get-tuple-element.32.tab, bf16[12,4,128,128]{3,2,1,0:T(8,128)(2,1)S(1)} %get-tuple-element.33.aff, f32[12,128,128]{2,1,0:T(8,128)S(1)} %get-tuple-element.34.t.t0, ...), custom_call_target="tpu_custom_call" | custom-call | flops 402653184 | bytes 4194304 | tf_op jit(solution)/shard_map/pallas_call | solution.py:491
  3.9 0.6 %collective-permute-start = (bf16[6,128,128]{2,1,0:T(8,128)(2,1)S(1)}, bf16[6,128,128]{2,1,0:T(8,128)(2,1)S(1)}, u32[]{:S(2)}, u32[]{:S(2)}) collective-permute-start(bf16[6,128,128]{2,1,0:T(8,128)(2,1)S(1)} %get-tuple-element.39), channel_id=1, source_target_pairs={{0,1},{1,0},{2,3},{3,2},{4,5},{5,4},{6,7},{7,6},{8,9},{9,8},{10,11... | collective-permute-start | bytes 589832 | tf_op jit(solution)/shard_map/ppermute | solution.py:454
  4.4 0.1 collective-permute-start.1
  4.5 5.6 %collective-permute-start.2 = (bf16[6,128,128]{2,1,0:T(8,128)(2,1)S(1)}, bf16[6,128,128]{2,1,0:T(8,128)(2,1)S(1)}, u32[]{:S(2)}, u32[]{:S(2)}) collective-permute-start(bf16[6,128,128]{2,1,0:T(8,128)(2,1)S(1)} %get-tuple-element.40), channel_id=1, source_target_pairs={{0,15},{1,0},{2,1},{3,2},{4,3},{5,4},{6,5},{7,6},{8,7},{9,8},{10,9... | collective-permute-start | bytes 589832 | tf_op jit(solution)/shard_map/ppermute | solution.py:459
  10.1 3.4 %collective-permute-done.1.recv_b = bf16[6,128,128]{2,1,0:T(8,128)(2,1)S(1)} collective-permute-done((bf16[6,128,128]{2,1,0:T(8,128)(2,1)S(1)}, bf16[6,128,128]{2,1,0:T(8,128)(2,1)S(1)}, u32[]{:S(2)}, u32[]{:S(2)}) %collective-permute-start.1) | collective-permute-done | bytes 196640 | tf_op jit(solution)/shard_map/ppermute | solution.py:459
  13.5 1.1 %shard_map.47 = (bf16[19,128,256]{2,1,0:T(8,128)(2,1)S(1)}, f32[12,128,128]{2,1,0:T(8,128)S(1)}, bf16[6,128,128]{2,1,0:T(8,128)(2,1)S(1)}) custom-call(s32[128]{0:T(128)S(4)} %get-tuple-element.32.tab, bf16[12,4,128,128]{3,2,1,0:T(8,128)(2,1)S(1)} %get-tuple-element.33.aff, ...), custom_call_target="tpu_custom_call", output_to_operand_aliasing={{0}: (2, {}), {1}: (3, {})} | custom-call | flops 402653184 | bytes 4194304 | tf_op jit(solution)/shard_map/pallas_call | solution.py:491
  14.6 0.6 %shard_map.48 = (bf16[19,128,256]{2,1,0:T(8,128)(2,1)S(1)}, f32[12,128,128]{2,1,0:T(8,128)S(1)}, f32[12,128,128]{2,1,0:T(8,128)S(1)}, bf16[19,128,128]{2,1,0:T(8,128)(2,1)S(1)}, bf16[6,128,128]{2,1,0:T(8,128)(2,1)S(1)}) custom-call(s32[128]{0:T(128)S(4)} %get-tuple-element.32.tab, ...), custom_call_target="tpu_custom_call", output_to_operand_aliasing={{0}: (2, {}), {1}: (3, {})} | custom-call | flops 805306368 | bytes 4194304 | tf_op jit(solution)/shard_map/pallas_call | solution.py:491
  15.3 0.8 %shard_map.49 = (f32[12,128,128]{2,1,0:T(8,128)S(1)}, bf16[19,128,128]{2,1,0:T(8,128)(2,1)S(1)}, f32[6,128,128]{2,1,0:T(8,128)S(1)}, bf16[6,128,128]{2,1,0:T(8,128)(2,1)S(1)}) custom-call(s32[128]{0:T(128)S(4)} %get-tuple-element.32.tab, bf16[12,4,128,128]{3,2,1,0:T(8,128)(2,1)S(1)} %get-tuple-element.33.aff, f32[12,128,128]{2,1,0:T(8,128)S(1)} %get-tuple-element.43.t.t2, ...), custom_call_target="tpu_custom_call" | custom-call | flops 402653184 | bytes 4194304 | tf_op jit(solution)/shard_map/pallas_call | solution.py:491
  16.1 0.3 collective-permute-start.3
  16.4 3.6 %collective-permute-start.4 = (bf16[6,128,128]{2,1,0:T(8,128)(2,1)S(1)}, bf16[6,128,128]{2,1,0:T(8,128)(2,1)S(1)}, u32[]{:S(2)}, u32[]{:S(2)}) collective-permute-start(bf16[6,128,128]{2,1,0:T(8,128)(2,1)S(1)} %get-tuple-element.49), channel_id=1, source_target_pairs={{0,15},{1,0},{2,1},{3,2},{4,3},{5,4},{6,5},{7,6},{8,7},{9,8},{10,9... | collective-permute-start | bytes 589832 | tf_op jit(solution)/shard_map/ppermute | solution.py:459
  20.0 3.2 %collective-permute-done.4.recv_b = bf16[6,128,128]{2,1,0:T(8,128)(2,1)S(1)} collective-permute-done((bf16[6,128,128]{2,1,0:T(8,128)(2,1)S(1)}, bf16[6,128,128]{2,1,0:T(8,128)(2,1)S(1)}, u32[]{:S(2)}, u32[]{:S(2)}) %collective-permute-start.4) | collective-permute-done | bytes 196640 | tf_op jit(solution)/shard_map/ppermute | solution.py:459
  23.2 4.6 %collective-permute-done.5.recv_b = bf16[6,128,128]{2,1,0:T(8,128)(2,1)S(1)} collective-permute-done((bf16[6,128,128]{2,1,0:T(8,128)(2,1)S(1)}, bf16[6,128,128]{2,1,0:T(8,128)(2,1)S(1)}, u32[]{:S(2)}, u32[]{:S(2)}) %collective-permute-start.5) | collective-permute-done | bytes 196640 | tf_op jit(solution)/shard_map/ppermute | solution.py:459
  27.8 0.9 %shard_map.51 = (bf16[19,128,128]{2,1,0:T(8,128)(2,1)S(1)}, f32[12,128,128]{2,1,0:T(8,128)S(1)}, f32[12,128,128]{2,1,0:T(8,128)S(1)}, bf16[19,128,128]{2,1,0:T(8,128)(2,1)S(1)}, bf16[3,128,128]{2,1,0:T(8,128)(2,1)S(1)}) custom-call(s32[128]{0:T(128)S(4)} %get-tuple-element.32.tab, ...), custom_call_target="tpu_custom_call", output_to_operand_aliasing={{0}: (2, {}), {1}: (3, {})} | custom-call | flops 402653184 | bytes 4194304 | tf_op jit(solution)/shard_map/pallas_call | solution.py:491
  28.7 0.1 collective-permute-start.6
  28.7 0.5 %collective-permute-start.7 = (bf16[3,128,128]{2,1,0:T(8,128)(2,1)S(1)}, bf16[3,128,128]{2,1,0:T(8,128)(2,1)S(1)}, u32[]{:S(2)}, u32[]{:S(2)}) collective-permute-start(bf16[3,128,128]{2,1,0:T(8,128)(2,1)S(1)} %get-tuple-element.55), channel_id=1, source_target_pairs={{0,1},{1,2},{2,3},{3,4},{4,5},{5,6},{6,7},{7,8},{8,9},{9,10},{10,1... | collective-permute-start | bytes 294920 | tf_op jit(solution)/shard_map/ppermute | solution.py:459
  29.2 0.8 %shard_map.53.early = f32[6,128]{1,0:T(8,128)S(1)} custom-call(f32[12,128,128]{2,1,0:T(8,128)S(1)} %get-tuple-element.34.t.t0, f32[12,128,128]{2,1,0:T(8,128)S(1)} %get-tuple-element.58.t1, f32[12,128,128]{2,1,0:T(8,128)S(1)} %get-tuple-element.43.t.t2), custom_call_target="tpu_custom_call" | custom-call | flops 40265320 | bytes 4194304 | tf_op jit(solution)/shard_map/pallas_call | solution.py:491
  30.0 0.3 shard_map.52.weight
  30.3 0.6 %shard_map.54.gram = f32[11,128]{1,0:T(8,128)S(1)} custom-call(s32[128]{0:T(128)S(4)} %get-tuple-element.32.tab, bf16[12,4,128,128]{3,2,1,0:T(8,128)(2,1)S(1)} %get-tuple-element.33.aff, f32[12,128,128]{2,1,0:T(8,128)S(1)} %get-tuple-element.43.t.t2, f32[12,128,128]{2,1,0:T(8,128)S(1)} %get-tuple-element.56.t3, f32[12,128,128]{2,1,0:T(8,128)S(1)} %get-tuple-element.57.t4, ...), custom_call_target="tpu_custom_call" | custom-call | flops 402653184 | bytes 4194304 | tf_op jit(solution)/shard_map/pallas_call | solution.py:491
  30.9 4.6 %collective-permute-done.7.recv_b = bf16[3,128,128]{2,1,0:T(8,128)(2,1)S(1)} collective-permute-done((bf16[3,128,128]{2,1,0:T(8,128)(2,1)S(1)}, bf16[3,128,128]{2,1,0:T(8,128)(2,1)S(1)}, u32[]{:S(2)}, u32[]{:S(2)}) %collective-permute-start.7) | collective-permute-done | bytes 98336 | tf_op jit(solution)/shard_map/ppermute | solution.py:459
  35.6 0.1 collective-permute-start.8
  35.7 1.2 %collective-permute-done.8.other = f32[11,128]{1,0:T(8,128)S(1)} collective-permute-done((f32[11,128]{1,0:T(8,128)S(1)}, f32[11,128]{1,0:T(8,128)S(1)}, u32[]{:S(2)}, u32[]{:S(2)}) %collective-permute-start.8) | collective-permute-done | bytes 5664 | tf_op jit(solution)/shard_map/ppermute | solution.py:454
  36.8 8.8 %all_to_all.5.parts = f32[8,11,128]{2,1,0:T(8,128)S(1)} all-to-all(f32[8,11,128]{2,1,0:T(8,128)S(1)} %shard_map.56), channel_id=1, replica_groups={{0,3,4,7,8,11,12,15},{1,2,5,6,9,10,13,14},{16,19,20,23,24,27,28,31},{17..., dimensions={0} | all-to-all | bytes 90112 | tf_op jit(solution)/shard_map/all_to_all | solution.py:584
  45.6 1.1 %final.1 = f32[1536,128]{1,0:T(8,128)} custom-call(f32[8,11,128]{2,1,0:T(8,128)S(1)} %all_to_all.5.parts, f32[12,128,128]{2,1,0:T(8,128)S(1)} %get-tuple-element.34.t.t0, f32[12,128,128]{2,1,0:T(8,128)S(1)} %get-tuple-element.58.t1, f32[12,128,128]{2,1,0:T(8,128)S(1)} %get-tuple-element.43.t.t2, f32[12,128,128]{2,1,0:T(8,128)S(1)} %get-tuple-element.56.t3, ...), custom_call_target="tpu_custom_call" | custom-call | tf_op jit(solution)/shard_map/final/pallas_call | solution.py:585
  (8 shorter events, 0.1 us)
Async XLA Ops:
  3.9 6.2 %collective-permute-start = (bf16[6,128,128]{2,1,0:T(8,128)(2,1)S(1)}, bf16[6,128,128]{2,1,0:T(8,128)(2,1)S(1)}, u32[]{:S(2)}, u32[]{:S(2)}) collective-permute-start(bf16[6,128,128]{2,1,0:T(8,128)(2,1)S(1)} %get-tuple-element.39), channel_id=1, source_target_pairs={{0,1},{1,0},{2,3},{3,2},{4,5},{5,4},{6,7},{7,6},{8,9},{9,8},{10,11... | collective-permute-start | bytes 589832 | tf_op jit(solution)/shard_map/ppermute | solution.py:454
  4.4 9.1 %collective-permute-start.1 = (bf16[6,128,128]{2,1,0:T(8,128)(2,1)S(1)}, bf16[6,128,128]{2,1,0:T(8,128)(2,1)S(1)}, u32[]{:S(2)}, u32[]{:S(2)}) collective-permute-start(bf16[6,128,128]{2,1,0:T(8,128)(2,1)S(1)} %get-tuple-element.40), channel_id=1, source_target_pairs={{0,1},{1,2},{2,3},{3,4},{4,5},{5,6},{6,7},{7,8},{8,9},{9,10},{10,1... | collective-permute-start | bytes 589832 | tf_op jit(solution)/shard_map/ppermute | solution.py:459
  4.5 10.1 %collective-permute-start.2 = (bf16[6,128,128]{2,1,0:T(8,128)(2,1)S(1)}, bf16[6,128,128]{2,1,0:T(8,128)(2,1)S(1)}, u32[]{:S(2)}, u32[]{:S(2)}) collective-permute-start(bf16[6,128,128]{2,1,0:T(8,128)(2,1)S(1)} %get-tuple-element.40), channel_id=1, source_target_pairs={{0,15},{1,0},{2,1},{3,2},{4,3},{5,4},{6,5},{7,6},{8,7},{9,8},{10,9... | collective-permute-start | bytes 589832 | tf_op jit(solution)/shard_map/ppermute | solution.py:459
  16.1 4.0 %collective-permute-start.3 = (bf16[6,128,128]{2,1,0:T(8,128)(2,1)S(1)}, bf16[6,128,128]{2,1,0:T(8,128)(2,1)S(1)}, u32[]{:S(2)}, u32[]{:S(2)}) collective-permute-start(bf16[6,128,128]{2,1,0:T(8,128)(2,1)S(1)} %get-tuple-element.48), channel_id=1, source_target_pairs={{0,1},{1,0},{2,3},{3,2},{4,5},{5,4},{6,7},{7,6},{8,9},{9,8},{10,11... | collective-permute-start | bytes 589832 | tf_op jit(solution)/shard_map/ppermute | solution.py:454
  16.4 6.8 %collective-permute-start.4 = (bf16[6,128,128]{2,1,0:T(8,128)(2,1)S(1)}, bf16[6,128,128]{2,1,0:T(8,128)(2,1)S(1)}, u32[]{:S(2)}, u32[]{:S(2)}) collective-permute-start(bf16[6,128,128]{2,1,0:T(8,128)(2,1)S(1)} %get-tuple-element.49), channel_id=1, source_target_pairs={{0,15},{1,0},{2,1},{3,2},{4,3},{5,4},{6,5},{7,6},{8,7},{9,8},{10,9... | collective-permute-start | bytes 589832 | tf_op jit(solution)/shard_map/ppermute | solution.py:459
  20.0 7.8 %collective-permute-start.5 = (bf16[6,128,128]{2,1,0:T(8,128)(2,1)S(1)}, bf16[6,128,128]{2,1,0:T(8,128)(2,1)S(1)}, u32[]{:S(2)}, u32[]{:S(2)}) collective-permute-start(bf16[6,128,128]{2,1,0:T(8,128)(2,1)S(1)} %get-tuple-element.52), channel_id=1, source_target_pairs={{0,1},{1,2},{2,3},{3,4},{4,5},{5,6},{6,7},{7,8},{8,9},{9,10},{10,1... | collective-permute-start | bytes 589832 | tf_op jit(solution)/shard_map/ppermute | solution.py:459
  28.7 2.3 %collective-permute-start.6 = (bf16[3,128,128]{2,1,0:T(8,128)(2,1)S(1)}, bf16[3,128,128]{2,1,0:T(8,128)(2,1)S(1)}, u32[]{:S(2)}, u32[]{:S(2)}) collective-permute-start(bf16[3,128,128]{2,1,0:T(8,128)(2,1)S(1)} %get-tuple-element.54), channel_id=1, source_target_pairs={{0,1},{1,0},{2,3},{3,2},{4,5},{5,4},{6,7},{7,6},{8,9},{9,8},{10,11... | collective-permute-start | bytes 294920 | tf_op jit(solution)/shard_map/ppermute | solution.py:454
  28.7 6.8 %collective-permute-start.7 = (bf16[3,128,128]{2,1,0:T(8,128)(2,1)S(1)}, bf16[3,128,128]{2,1,0:T(8,128)(2,1)S(1)}, u32[]{:S(2)}, u32[]{:S(2)}) collective-permute-start(bf16[3,128,128]{2,1,0:T(8,128)(2,1)S(1)} %get-tuple-element.55), channel_id=1, source_target_pairs={{0,1},{1,2},{2,3},{3,4},{4,5},{5,6},{6,7},{7,8},{8,9},{9,10},{10,1... | collective-permute-start | bytes 294920 | tf_op jit(solution)/shard_map/ppermute | solution.py:459
  35.6 1.2 %collective-permute-start.8 = (f32[11,128]{1,0:T(8,128)S(1)}, f32[11,128]{1,0:T(8,128)S(1)}, u32[]{:S(2)}, u32[]{:S(2)}) collective-permute-start(f32[11,128]{1,0:T(8,128)S(1)} %shard_map.55.own), channel_id=1, source_target_pairs={{0,1},{1,0},{2,3},{3,2},{4,5},{5,4},{6,7},{7,6},{8,9},{9,8},{10,11... | collective-permute-start | bytes 16904 | tf_op jit(solution)/shard_map/ppermute | solution.py:454
